TPU v7x, 32 devices: a whole 2x2x4 slice. The times are simulated.
32 devices in a mesh: wide: 16 (over z, y, x), narrow: 2 (over core).
Axes of the slice: x: 2, y: 2, z: 4, core: 2. Of those that a mesh axis runs over, the one named last changes fastest.
Arguments:
- tokens: bfloat16 [16384, 1024], P(('wide', 'narrow')), may hold values from -6 to 6
- window_span: int32 [32], P('wide'), may hold values from 1 to 2, as said below
- valid_len: int32 [32], P('wide'), may hold values from 384 to 512, as said below
- norm1_gain: float32 [1024], replicated, may hold values from 0.5 to 1.5
- norm1_shift: float32 [1024], replicated, may hold values from -1.8 to 1.8
- w_query: bfloat16 [1024, 1024], P(None, 'narrow'), may hold values from -0.25 to 0.25
- w_key: bfloat16 [1024, 1024], P(None, 'narrow'), may hold values from -0.25 to 0.25
- w_value: bfloat16 [1024, 1024], P(None, 'narrow'), may hold values from -0.1875 to 0.1875
- w_out: bfloat16 [1024, 1024], P('narrow'), may hold values from -1.5 to 1.5
- norm2_gain: float32 [1024], replicated, may hold values from 0.5 to 1.5
- norm2_shift: float32 [1024], replicated, may hold values from -1.8 to 1.8
- w_gate: bfloat16 [1024, 4096], P(None, 'narrow'), may hold values from -0.1875 to 0.1875
- w_up: bfloat16 [1024, 4096], P(None, 'narrow'), may hold values from -0.1875 to 0.1875
- w_down: bfloat16 [4096, 1024], P('narrow'), may hold values from -0.09375 to 0.09375
- cotangent: bfloat16 [16384, 1024], P(('wide', 'narrow')), may hold values from -6 to 6
Outputs:
- out: float32 [16384, 1024], P(('wide', 'narrow'))
- token_grad: float32 [16384, 1024], P(('wide', 'narrow'))
- norm1_gain_grad: float32 [1024], replicated
- norm1_shift_grad: float32 [1024], replicated
- w_query_grad: float32 [1024, 1024], P(None, 'narrow')
- w_key_grad: float32 [1024, 1024], P(None, 'narrow')
- w_value_grad: float32 [1024, 1024], P(None, 'narrow')
- w_out_grad: float32 [1024, 1024], P('narrow')
- norm2_gain_grad: float32 [1024], replicated
- norm2_shift_grad: float32 [1024], replicated
- w_gate_grad: float32 [1024, 4096], P(None, 'narrow')
- w_up_grad: float32 [1024, 4096], P(None, 'narrow')
- w_down_grad: float32 [4096, 1024], P('narrow')
Inputs may be any that keep to these rules, and one draw needn't show every extreme that they name: `window_span`: within each group, blocks 2k and 2k+1 hold the same value: 2 where one window fills both blocks, 1 where each block holds a window of its own. `valid_len`: blocks whose window_span is 2 hold 512.
All inputs are finite; a program needn't handle non-finite values.
Results may differ from a plain program's by a relative error of at most 0.019.
Values may be sent and summed in bfloat16 or wider, within the bound.
A program may use at most 256 MiB of HBM per device.

v0:
```python
import jax
import jax.numpy as jnp
from jax import lax
from jax.sharding import PartitionSpec as P

HD = 64


EPSILON = 1e-05
MASKED = -1e30
ROPE_BASE = 10000.0


def times_transpose(left, right):
    return lax.dot_general(
        left, right, (((1,), (1,)), ((), ())), preferred_element_type=jnp.float32
    )


def transpose_times(left, right):
    return lax.dot_general(
        left, right, (((0,), (0,)), ((), ())), preferred_element_type=jnp.float32
    )


def norm_forward(values, norm_gain, norm_shift):
    average = jnp.mean(values, axis=-1, keepdims=True)
    centred = values - average
    inverse = lax.rsqrt(jnp.mean(centred * centred, axis=-1, keepdims=True) + EPSILON)
    scaled = centred * inverse
    return (scaled * norm_gain + norm_shift, scaled, inverse)


def norm_backward(grad_out, scaled, inverse, norm_gain):
    grad_scaled = grad_out * norm_gain
    first_term = jnp.mean(grad_scaled, axis=-1, keepdims=True)
    second_term = jnp.mean(grad_scaled * scaled, axis=-1, keepdims=True)
    grad_in = inverse * (grad_scaled - first_term - scaled * second_term)
    return (grad_in, jnp.sum(grad_out * scaled, axis=0), jnp.sum(grad_out, axis=0))


def rotary_tables(span_table, block_rows, width):
    row_count = span_table.shape[0] * block_rows
    row_ids = jnp.arange(row_count)
    block_ids = row_ids // block_rows
    span_rows = jnp.repeat(span_table, block_rows)
    position = (row_ids % block_rows + block_rows * (block_ids % 2) * (span_rows == 2)).astype(
        jnp.float32
    )
    columns = jnp.arange(width) % HD
    half_dim = HD // 2
    freq_index = (columns % half_dim).astype(jnp.float32)
    frequency = ROPE_BASE ** (-2.0 * freq_index / HD)
    angles = position[:, None] * frequency[None, :]
    signs = jnp.where(columns < half_dim, -1.0, 1.0).astype(jnp.float32)
    return (jnp.cos(angles), jnp.sin(angles) * signs)


def swap_halves(values):
    row_count = values.shape[0]
    width = values.shape[1]
    parts = values.reshape(row_count, width // HD, 2, HD // 2)
    return jnp.flip(parts, axis=2).reshape(row_count, width)


def rotate(values, cosine, sine_signed):
    return values * cosine + swap_halves(values) * sine_signed


def rotate_back(grads_in, cosine, sine_signed):
    return grads_in * cosine + swap_halves(grads_in * sine_signed)


def pair_mask(block_index, span_table, valid_table, block_rows):
    pair_first = block_index // 2 * 2
    offsets = jnp.arange(2 * block_rows)
    key_block = pair_first + offsets // block_rows
    within = offsets % block_rows
    first_len = lax.dynamic_index_in_dim(valid_table, pair_first, keepdims=False)
    second_len = lax.dynamic_index_in_dim(valid_table, pair_first + 1, keepdims=False)
    own_span = lax.dynamic_index_in_dim(span_table, block_index, keepdims=False)
    length_bound = jnp.where(offsets < block_rows, first_len, second_len)
    return (within < length_bound) & ((own_span == 2) | (key_block == block_index))


def on_device(
    tokens,
    window_span,
    valid_len,
    norm1_gain,
    norm1_shift,
    w_query,
    w_key,
    w_value,
    w_out,
    norm2_gain,
    norm2_shift,
    w_gate,
    w_up,
    w_down,
    cotangent,
):
    local_rows = tokens.shape[0]
    group_rows = local_rows * lax.axis_size("narrow")
    block_count = window_span.shape[0]
    block_rows = group_rows // block_count
    local_width = w_query.shape[1]
    local_heads = local_width // HD
    local_hidden = w_gate.shape[1]
    softmax_scale = HD ** (-0.5)
    token_values = tokens.astype(jnp.float32)
    normed_one, scaled_one, inverse_one = norm_forward(token_values, norm1_gain, norm1_shift)
    normed_one = normed_one.astype(jnp.bfloat16)
    gathered_one = lax.all_gather(normed_one, "narrow", axis=0, tiled=True)
    joined_qkv = jnp.concatenate([w_query, w_key, w_value], axis=1)
    projected = jnp.dot(gathered_one, joined_qkv, preferred_element_type=jnp.float32)
    cosine, sine_signed = rotary_tables(window_span, block_rows, local_width)
    query_rows = (rotate(projected[:, :local_width], cosine, sine_signed) * softmax_scale).astype(
        jnp.bfloat16
    )
    key_rows = rotate(projected[:, local_width : 2 * local_width], cosine, sine_signed).astype(
        jnp.bfloat16
    )
    value_rows = projected[:, 2 * local_width :].astype(jnp.bfloat16)

    def block_slices(block_index):
        query_block = lax.dynamic_slice_in_dim(query_rows, block_index * block_rows, block_rows, 0)
        pair_start = block_index // 2 * 2 * block_rows
        return (
            query_block.reshape(block_rows, local_heads, HD),
            key_rows.reshape(2 * block_rows, local_heads, HD),
            value_rows.reshape(2 * block_rows, local_heads, HD),
            pair_start,
        )

    def masked_scores(block_index, query_block, key_pair):
        scores = jnp.einsum(
            "qhd,khd->hqk", query_block, key_pair, preferred_element_type=jnp.float32
        )
        key_mask = pair_mask(block_index, window_span, valid_len, block_rows)
        return jnp.where(key_mask[None, None, :], scores, MASKED)

    def attend_forward(block_index):
        query_block, key_pair, value_pair, pair_start = block_slices(block_index)
        scores = masked_scores(block_index, query_block, key_pair)
        highest = jnp.max(scores, axis=-1, keepdims=True)
        weights = jnp.exp(scores - highest)
        weight_total = jnp.sum(weights, axis=-1, keepdims=True)
        attention_probs = (weights / weight_total).astype(jnp.bfloat16)
        mixed_block = jnp.einsum(
            "hqk,khd->qhd", attention_probs, value_pair, preferred_element_type=jnp.float32
        )
        return (
            mixed_block.reshape(block_rows, local_width).astype(jnp.bfloat16),
            (highest + jnp.log(weight_total))[:, :, 0],
        )

    mixed_blocks, log_totals = lax.map(attend_forward, jnp.arange(block_count))
    mixed_rows = mixed_blocks.reshape(group_rows, local_width)
    resid_values = token_values + lax.psum_scatter(
        jnp.dot(mixed_rows, w_out, preferred_element_type=jnp.float32),
        "narrow",
        scatter_dimension=0,
        tiled=True,
    )
    normed_two, scaled_two, inverse_two = norm_forward(resid_values, norm2_gain, norm2_shift)
    normed_two = normed_two.astype(jnp.bfloat16)
    gathered_two = lax.all_gather(normed_two, "narrow", axis=0, tiled=True)
    joined_gate_up = jnp.concatenate([w_gate, w_up], axis=1)
    gate_up = jnp.dot(gathered_two, joined_gate_up, preferred_element_type=jnp.float32)
    gate_values = gate_up[:, :local_hidden]
    up_values = gate_up[:, local_hidden:]
    sigmoid_gate = jax.nn.sigmoid(gate_values)
    hidden_rows = (gate_values * sigmoid_gate * up_values).astype(jnp.bfloat16)
    out_values = resid_values + lax.psum_scatter(
        jnp.dot(hidden_rows, w_down, preferred_element_type=jnp.float32).astype(jnp.bfloat16),
        "narrow",
        scatter_dimension=0,
        tiled=True,
    ).astype(jnp.float32)
    shard_rows = lax.all_gather(cotangent, "narrow", axis=0, tiled=True)
    grad_hidden = times_transpose(shard_rows, w_down)
    grad_down_w, grad_hidden = (transpose_times(hidden_rows, shard_rows), grad_hidden)
    silu_grad = sigmoid_gate * (1.0 + gate_values * (1.0 - sigmoid_gate))
    grad_gate_up = jnp.concatenate(
        [grad_hidden * up_values * silu_grad, grad_hidden * gate_values * sigmoid_gate], axis=1
    ).astype(jnp.bfloat16)
    grad_normed_two = lax.psum_scatter(
        times_transpose(grad_gate_up, joined_gate_up), "narrow", scatter_dimension=0, tiled=True
    )
    grad_gate_up_w = transpose_times(gathered_two, grad_gate_up)
    grad_in_two, gain_two_grad, shift_two_grad = norm_backward(
        grad_normed_two, scaled_two, inverse_two, norm2_gain
    )
    grad_resid = cotangent.astype(jnp.float32) + grad_in_two
    shard_rows = lax.all_gather(grad_resid.astype(jnp.bfloat16), "narrow", axis=0, tiled=True)
    grad_mixed_sum = times_transpose(shard_rows, w_out)
    grad_out_w, grad_mixed_sum = (transpose_times(mixed_rows, shard_rows), grad_mixed_sum)
    grad_mixed = grad_mixed_sum.astype(jnp.bfloat16)

    def attend_backward(block_index, running):
        grad_query, grad_key, grad_value = running
        query_block, key_pair, value_pair, pair_start = block_slices(block_index)
        grad_rows = lax.dynamic_slice_in_dim(
            grad_mixed, block_index * block_rows, block_rows, 0
        ).reshape(block_rows, local_heads, HD)
        scores = masked_scores(block_index, query_block, key_pair)
        log_total = lax.dynamic_index_in_dim(log_totals, block_index, keepdims=False)
        attention_probs = jnp.exp(scores - log_total[:, :, None])
        grad_probs = jnp.einsum(
            "qhd,khd->hqk", grad_rows, value_pair, preferred_element_type=jnp.float32
        )
        centre = jnp.sum(attention_probs * grad_probs, axis=-1, keepdims=True)
        grad_scores = (attention_probs * (grad_probs - centre)).astype(jnp.bfloat16)
        block_query = jnp.einsum(
            "hqk,khd->qhd", grad_scores, key_pair, preferred_element_type=jnp.float32
        ).reshape(block_rows, local_width)
        pair_key = jnp.einsum(
            "hqk,qhd->khd", grad_scores, query_block, preferred_element_type=jnp.float32
        ).reshape(2 * block_rows, local_width)
        pair_value = jnp.einsum(
            "hqk,qhd->khd",
            attention_probs.astype(jnp.bfloat16),
            grad_rows,
            preferred_element_type=jnp.float32,
        ).reshape(2 * block_rows, local_width)
        grad_query = lax.dynamic_update_slice_in_dim(
            grad_query, block_query, block_index * block_rows, 0
        )
        grad_key = grad_key + pair_key
        grad_value = grad_value + pair_value
        return (grad_query, grad_key, grad_value)

    zero_rows = jnp.zeros((group_rows, local_width), jnp.float32)
    grad_query, grad_key, grad_value = lax.fori_loop(
        0, block_count, attend_backward, (zero_rows, zero_rows, zero_rows)
    )
    grad_query_raw = rotate_back(grad_query * softmax_scale, cosine, sine_signed)
    grad_key_raw = rotate_back(grad_key, cosine, sine_signed)
    grad_qkv = jnp.concatenate([grad_query_raw, grad_key_raw, grad_value], axis=1).astype(
        jnp.bfloat16
    )
    grad_normed_one = lax.psum_scatter(
        times_transpose(grad_qkv, joined_qkv).astype(jnp.bfloat16),
        "narrow",
        scatter_dimension=0,
        tiled=True,
    ).astype(jnp.float32)
    grad_qkv_w = transpose_times(gathered_one, grad_qkv)
    grad_in_one, gain_one_grad, shift_one_grad = norm_backward(
        grad_normed_one, scaled_one, inverse_one, norm1_gain
    )
    token_grad = grad_resid + grad_in_one
    qkv_summed, out_summed, gate_up_summed, down_summed = (
        lax.psum(grad_qkv_w.astype(jnp.bfloat16), "wide").astype(jnp.float32),
        lax.psum(grad_out_w.astype(jnp.bfloat16), "wide").astype(jnp.float32),
        lax.psum(grad_gate_up_w.astype(jnp.bfloat16), "wide").astype(jnp.float32),
        lax.psum(grad_down_w.astype(jnp.bfloat16), "wide").astype(jnp.float32),
    )
    norm_summed = lax.psum(
        (gain_one_grad, shift_one_grad, gain_two_grad, shift_two_grad), ("wide", "narrow")
    )
    return (
        out_values,
        token_grad,
        norm_summed[0],
        norm_summed[1],
        qkv_summed[:, :local_width],
        qkv_summed[:, local_width : 2 * local_width],
        qkv_summed[:, 2 * local_width :],
        out_summed,
        norm_summed[2],
        norm_summed[3],
        gate_up_summed[:, :local_hidden],
        gate_up_summed[:, local_hidden:],
        down_summed,
    )


def solution(mesh):
    in_specs = (
        P(("wide", "narrow"), None),
        P("wide"),
        P("wide"),
        P(),
        P(),
        P(None, "narrow"),
        P(None, "narrow"),
        P(None, "narrow"),
        P("narrow", None),
        P(),
        P(),
        P(None, "narrow"),
        P(None, "narrow"),
        P("narrow", None),
        P(("wide", "narrow"), None),
    )
    out_specs = (
        P(("wide", "narrow"), None),
        P(("wide", "narrow"), None),
        P(),
        P(),
        P(None, "narrow"),
        P(None, "narrow"),
        P(None, "narrow"),
        P("narrow", None),
        P(),
        P(),
        P(None, "narrow"),
        P(None, "narrow"),
        P("narrow", None),
    )
    return jax.shard_map(
        on_device, mesh=mesh, in_specs=in_specs, out_specs=out_specs, check_vma=False
    )
```

profile of v0, /device:TPU:0, one launch (start us, length us, event | category | flops | bytes accessed | tf_op | source)
XLA Modules:
  0.0 900.9 jit_solution(3977947067159316405)
XLA Ops:
  15.9 10.1 %all-gather.5.cloned.1.call-done = bf16[1024,1024]{1,0:T(8,128)(2,1)} async-done(((bf16[512,1024]{1,0:T(8,128)(2,1)}), bf16[1024,1024]{1,0:T(8,128)(2,1)}) %all-gather.5.cloned.1.call-update) | async-done | bytes 2097168 | tf_op jit(solution)/shard_map/all_gather | solution.py:114
  26.1 5.9 fusion.98
  41.6 3.2 rev.14
  50.5 3.2 rev.13
  56.6 11.1 %fusion.54 = (bf16[1024,512]{1,0:T(8,128)(2,1)}, bf16[1024,512]{1,0:T(8,128)(2,1)S(1)}) fusion(f32[1024,512]{1,0:T(8,128)} %copy.42, f32[512]{0:T(512)S(1)} %get-tuple-element.644, f32[512]{0:T(512)S(1)} %get-tuple-element.643, f32[1024]{0:T(1024)S(1)} %fusion.66, f32[1024,1536]{1,0:T(8,128)} %copy-done.15, f32[1024,512]{1,0:T(8,128)} %copy.40), kind=kLoop, calls=%fused_computation.97 | loop fusion | flops 5767168 | bytes 10493952 | tf_op jit(solution)/shard_map/convert_element_type | solution.py:121
  70.5 44.1 %while.36 = (s32[]{:T(128)}, bf16[2,512,512]{2,1,0:T(8,128)(2,1)}, f32[2,8,512]{2,1,0:T(8,128)S(1)}, s32[2]{0:T(128)S(1)}, s32[2]{0:T(128)S(1)}, /*index=5*/s32[...) while((s32[]{:T(128)}, bf16[2,512,512]{2,1,0:T(8,128)(2,1)}, ...), condition=%wide.region_5.6_spmd, body=%wide.region_2.5_spmd.sunk | while | flops 1111768064 | bytes 56758836 | solution.py:158
  83.0 3.5 fusion.161
  86.5 4.9 fusion.162
  105.0 3.5 fusion.161
  108.5 4.9 fusion.162
  114.5 4.5 fusion.99
  119.1 13.3 %reduce-scatter.5.cloned.1.call-done = f32[512,1024]{1,0:T(8,128)} async-done(((f32[1024,1024]{1,0:T(8,128)}), f32[512,1024]{1,0:T(8,128)}) %reduce-scatter.5.cloned.1.call-update) | async-done | bytes 2097168 | tf_op jit(solution)/shard_map/reduce_scatter | solution.py:160
  137.7 4.9 constant_dynamic-update-slice_fusion.6
  144.9 4.1 all-gather.7.cloned.1.call-done
  149.0 16.4 %fusion.100 = f32[1024,4096]{1,0:T(8,128)} fusion(bf16[1024,1024]{1,0:T(8,128)(2,1)} %all-gather.7.cloned.1.call-done, bf16[1024,4096]{1,0:T(8,128)(2,1)} %constant_dynamic-update-slice_fusion.5), kind=kOutput, calls=%fused_computation.183 | convolution fusion | flops 8589934592 | bytes 27262976 | tf_op jit(solution)/shard_map/dot_general | solution.py:170
  165.5 15.5 %multiply_convert_fusion.2 = (bf16[1024,2048]{1,0:T(8,128)(2,1)S(1)}, bf16[1024,2048]{1,0:T(8,128)(2,1)}, bf16[1024,2048]{1,0:T(8,128)(2,1)}) fusion(f32[1024,4096]{1,0:T(8,128)} %fusion.100, bf16[1024,1024]{1,0:T(8,128)(2,1)} %all-gather.9.cloned.1.call-done, bf16[2048,1024]{1,0:T(8,128)(2,1)} %param.32), kind=kOutput, calls=%fused_computation.59 | convolution fusion | flops 4328521728 | bytes 35651584 | tf_op jit(solution)/shard_map/dot_general | solution.py:15
  182.9 13.9 %fusion.31 = f32[1024,1024]{1,0:T(8,128)} fusion(bf16[1024,4096]{1,0:T(8,128)(2,1)} %constant_dynamic-update-slice_fusion.5, bf16[1024,2048]{1,0:T(8,128)(2,1)} %get-tuple-element.627, bf16[1024,2048]{1,0:T(8,128)(2,1)S(1)} %get-tuple-element.626), kind=kOutput, calls=%fused_computation.63 | convolution fusion | flops 8606711808 | bytes 20971520 | tf_op jit(solution)/shard_map/dot_general | solution.py:15
  196.9 9.3 %convolution_convert_fusion.4 = bf16[1024,1024]{1,0:T(8,128)(2,1)} fusion(bf16[1024,2048]{1,0:T(8,128)(2,1)} %get-tuple-element.628, bf16[2048,1024]{1,0:T(8,128)(2,1)} %param.32), kind=kOutput, calls=%fused_computation.117 | convolution fusion | flops 4296015872 | bytes 10485760 | tf_op jit(solution)/shard_map/dot_general | solution.py:176
  206.3 4.0 reduce-scatter.9.cloned.1.call-done
  210.3 3.7 multiply_reduce_fusion.1
  214.0 10.1 %reduce-scatter.7.cloned.1.call-done = bf16[512,1024]{1,0:T(8,128)(2,1)} async-done(((bf16[1024,1024]{1,0:T(8,128)(2,1)}), bf16[512,1024]{1,0:T(8,128)(2,1)}) %reduce-scatter.7.cloned.1.call-update) | async-done | bytes 1048592 | tf_op jit(solution)/shard_map/reduce_scatter | solution.py:175
  224.0 5.8 fusion.88
  229.9 11.9 %all-gather.11.cloned.1.call-done = bf16[1024,1024]{1,0:T(8,128)(2,1)} async-done(((bf16[512,1024]{1,0:T(8,128)(2,1)}), bf16[1024,1024]{1,0:T(8,128)(2,1)}) %all-gather.11.cloned.1.call-update) | async-done | bytes 2097168 | tf_op jit(solution)/shard_map/all_gather | solution.py:196
  241.8 3.8 convolution_convert_fusion.6
  247.3 94.5 %while.37 = (s32[]{:T(128)}, f32[1024,512]{1,0:T(8,128)}, f32[1024,512]{0,1:T(8,128)}, f32[1024,512]{0,1:T(8,128)}, s32[2]{0:T(128)S(1)}, /*index=5*/s32[2]{0:T(...) while((s32[]{:T(128)}, f32[1024,512]{1,0:T(8,128)}, ...), condition=%wide.region_15.16_spmd.clone, body=%wide.region_13.15_spmd.clone.sunk | while | flops 2736798720 | bytes 236049072 | solution.py:235
  255.4 4.2 fusion.177
  259.6 9.7 %multiply_reduce_fusion.6 = (f32[8,512]{1,0:T(8,128)S(1)}, f32[8,512,1024]{2,1,0:T(8,128)}) fusion(f32[8,512,1024]{2,1,0:T(8,128)S(1)} %fusion.173, f32[8,512]{1,0:T(8,128)S(1)} %dynamic-slice_bitcast_fusion.2, pred[1024]{0:T(1024)(128)(4,1)S(1)} %fusion.175, bf16[512,8,64]{0,2,1:T(8,128)(2,1)S(1)} %bitcast.141, bf16[1024,8,64]{0,2,1:T(8,128)(2,1)} %bitcast.133), kind=kOutput, calls=%fused_computation.27.clone.1 | convolution fusion | flops 553644032 | bytes 35161088 | tf_op jit(solution)/shard_map/while/body/eval_jaxpr/qhd,khd->hqk/dot_general | solution.py:210
  269.3 10.4 %multiply_convert_fusion.5 = bf16[8,512,1024]{2,1,0:T(8,128)(2,1)} fusion(f32[8,512,1024]{2,1,0:T(8,128)} %get-tuple-element.783, f32[8,512,1024]{2,1,0:T(8,128)S(1)} %fusion.173, f32[8,512]{1,0:T(8,128)S(1)} %get-tuple-element.784, f32[8,512]{1,0:T(8,128)S(1)} %dynamic-slice_bitcast_fusion.2, pred[1024]{0:T(1024)(128)(4,1)S(1)} %fusion.175), kind=kLoop, calls=%fused_computation.26.clone.1 | loop fusion | flops 20971520 | bytes 41976832 | tf_op jit(solution)/shard_map/while/body/eval_jaxpr/convert_element_type | solution.py:214
  279.7 7.2 fusion.176
  302.5 4.2 fusion.177
  306.8 9.7 %multiply_reduce_fusion.6 = (f32[8,512]{1,0:T(8,128)S(1)}, f32[8,512,1024]{2,1,0:T(8,128)}) fusion(f32[8,512,1024]{2,1,0:T(8,128)S(1)} %fusion.173, f32[8,512]{1,0:T(8,128)S(1)} %dynamic-slice_bitcast_fusion.2, pred[1024]{0:T(1024)(128)(4,1)S(1)} %fusion.175, bf16[512,8,64]{0,2,1:T(8,128)(2,1)S(1)} %bitcast.141, bf16[1024,8,64]{0,2,1:T(8,128)(2,1)} %bitcast.133), kind=kOutput, calls=%fused_computation.27.clone.1 | convolution fusion | flops 553644032 | bytes 35161088 | tf_op jit(solution)/shard_map/while/body/eval_jaxpr/qhd,khd->hqk/dot_general | solution.py:210
  316.5 10.4 %multiply_convert_fusion.5 = bf16[8,512,1024]{2,1,0:T(8,128)(2,1)} fusion(f32[8,512,1024]{2,1,0:T(8,128)} %get-tuple-element.783, f32[8,512,1024]{2,1,0:T(8,128)S(1)} %fusion.173, f32[8,512]{1,0:T(8,128)S(1)} %get-tuple-element.784, f32[8,512]{1,0:T(8,128)S(1)} %dynamic-slice_bitcast_fusion.2, pred[1024]{0:T(1024)(128)(4,1)S(1)} %fusion.175), kind=kLoop, calls=%fused_computation.26.clone.1 | loop fusion | flops 20971520 | bytes 41976832 | tf_op jit(solution)/shard_map/while/body/eval_jaxpr/convert_element_type | solution.py:214
  326.9 7.2 fusion.176
  346.0 9.4 %fusion.61 = (f32[1024,512]{1,0:T(8,128)}, f32[1024,512]{1,0:T(8,128)S(1)}) fusion(f32[1024,512]{1,0:T(8,128)} %get-tuple-element.477, f32[512]{0:T(512)S(1)} %copy-done.45, f32[512]{0:T(512)S(1)} %copy-done.43, f32[1024]{0:T(1024)S(1)} %copy-done.34, f32[1024,512]{1,0:T(8,128)} %copy.54), kind=kLoop, calls=%fused_computation.104 | loop fusion | flops 2621440 | bytes 8396800 | tf_op jit(solution)/shard_map/mul | solution.py:71
  358.3 3.2 rev.15
  366.1 3.2 rev.16
  369.3 3.0 copy.57
  372.3 9.1 %fusion.56 = (bf16[1024,512]{1,0:T(8,128)(2,1)S(1)}, bf16[1024,512]{1,0:T(8,128)(2,1)S(1)}) fusion(f32[1024,512]{1,0:T(8,128)} %copy.53, f32[1024,512]{1,0:T(8,128)} %get-tuple-element.477, f32[512]{0:T(512)S(1)} %copy-done.43, f32[1024]{0:T(1024)S(1)} %copy-done.34, f32[1024,512]{1,0:T(8,128)} %copy.57, f32[1024,512]{1,0:T(8,128)S(1)} %copy-done.14), kind=kLoop, calls=%fused_computation.99 | loop fusion | flops 4194304 | bytes 10491904 | tf_op jit(solution)/shard_map/convert
  382.8 4.6 convolution_convert_fusion.3
  389.0 8.7 convolution_convert_fusion.2
  397.7 11.5 %convolution_convert_fusion = bf16[1024,4096]{1,0:T(8,128)(2,1)} fusion(bf16[1024,1024]{1,0:T(8,128)(2,1)S(1)} %copy-done.51, bf16[1024,2048]{1,0:T(8,128)(2,1)S(1)} %copy-done.56, bf16[1024,2048]{1,0:T(8,128)(2,1)S(1)} %copy-done.55), kind=kOutput, calls=%fused_computation.62 | convolution fusion | flops 8610906112 | bytes 18874368 | tf_op jit(solution)/shard_map/dot_general | solution.py:21
  411.6 5.5 convolution_convert_fusion.1
  420.6 44.3 %all-reduce = (f32[1024]{0:T(1024)}, f32[1024]{0:T(1024)}, f32[1024]{0:T(1024)}, f32[1024]{0:T(1024)}) all-reduce(f32[1024]{0:T(1024)S(1)} %get-tuple-element.559, f32[1024]{0:T(1024)S(1)} %get-tuple-element.563, f32[1024]{0:T(1024)S(1)} %copy-done.46, f32[1024]{0:T(1024)S(1)} %copy-done.47), channel_id=1, replica_groups=mesh['wide'=16,'narrow'=2] {'wide','narrow'}, use_global_device_ids=true, to_apply=%region_20.21 | all-reduce | flops 4096 | bytes 32768 | tf_op jit(solution)/shard_map/psum | solution.py:260
  465.0 3.7 fusion.47
  468.7 401.7 %all-reduce.4.cloned.1.call-done = (bf16[1024,1536]{1,0:T(8,128)(2,1)}, bf16[512,1024]{1,0:T(8,128)(2,1)}, bf16[1024,4096]{1,0:T(8,128)(2,1)}, bf16[2048,1024]{1,0:T(8,128)(2,1)}) async-done(((bf16[1024,1536]{1,0:T(8,128)(2,1)}, bf16[512,1024]{1,0:T(8,128)(2,1)}, bf16[1024,4096]{1,0:T(8,128)(2,1)}, bf16[2048,1024]{1,0:T(8,128)(2,1)}), (bf16[1024,1536]{1,0:T(8,128)(2,1)}, bf16[512,1024]{1,0:T(8,128)(2,1)}, ...) | async-done | bytes 16777232 | tf_op jit(solution)/shard_map/psum | solution.py:255
  873.3 3.4 fusion.94
  877.7 4.4 convert_element_type.152
  882.1 11.8 %fusion.92 = (f32[1024,2048]{1,0:T(8,128)}, f32[1024,2048]{1,0:T(8,128)}) fusion(bf16[1024,4096]{1,0:T(8,128)(2,1)} %get-tuple-element.610), kind=kLoop, calls=%fused_computation.175 | loop fusion | bytes 33554432 | tf_op jit(solution)/shard_map/slice | solution.py:275
  (236 shorter events, 111.9 us)
Async XLA Ops:
  7.2 107.4 %copy-start = (bf16[512,1024]{1,0:T(8,128)(2,1)S(1)}, bf16[512,1024]{1,0:T(8,128)(2,1)}, u32[]{:S(2)}) copy-start(bf16[512,1024]{1,0:T(8,128)(2,1)} %param.27) | copy-start | bytes 3145732
  7.2 4.0 copy-start.11
  7.2 4.0 copy-start.38
  7.2 4.0 copy-start.48
  7.2 18.8 %all-gather.5.cloned.1.call-start = ((), (), s32[]{:S(2)}) async-start(), calls=%async_computation.4 | async-start | bytes 3145728 | tf_op jit(solution)/shard_map/all_gather | solution.py:114
  8.9 3.8 copy-start.53
  8.9 4.0 copy-start.22
  12.6 119.8 %reduce-scatter.5.cloned.1.call-start = ((), (), s32[]{:S(2)}) async-start(), calls=%async_computation.5 | async-start | bytes 6291456 | tf_op jit(solution)/shard_map/reduce_scatter | solution.py:160
  12.8 43.7 %copy-start.42 = (f32[512]{0:T(512)}, f32[512]{0:T(512)S(1)}, u32[]{:S(2)}) copy-start(f32[512]{0:T(512)S(1)} %get-tuple-element.643) | copy-start | bytes 6148
  12.8 43.7 %copy-start.44 = (f32[512]{0:T(512)}, f32[512]{0:T(512)S(1)}, u32[]{:S(2)}) copy-start(f32[512]{0:T(512)S(1)} %get-tuple-element.644) | copy-start | bytes 6148
  15.9 40.6 %copy-start.33 = (f32[1024]{0:T(1024)}, f32[1024]{0:T(1024)S(1)}, u32[]{:S(2)}) copy-start(f32[1024]{0:T(1024)S(1)} %fusion.66) | copy-start | bytes 12292
  32.0 2.7 copy-start.15
  67.6 2.8 copy-start.32
  119.0 13.4 %copy-start.12 = (bf16[512,1024]{1,0:T(8,128)(2,1)S(1)}, bf16[512,1024]{1,0:T(8,128)(2,1)}, u32[]{:S(2)}) copy-start(bf16[512,1024]{1,0:T(8,128)(2,1)} %param.19) | copy-start | bytes 3145732
  119.0 30.0 %all-gather.7.cloned.1.call-start = ((), (), s32[]{:S(2)}) async-start(), calls=%async_computation.6 | async-start | bytes 3145728 | tf_op jit(solution)/shard_map/all_gather | solution.py:168
  137.0 28.5 %all-gather.9.cloned.1.call-start = ((), (), s32[]{:S(2)}) async-start(), calls=%async_computation.8 | async-start | bytes 3145728 | tf_op jit(solution)/shard_map/all_gather | solution.py:181
  137.6 72.7 %reduce-scatter.9.cloned.1.call-start = ((), (), s32[]{:S(2)}) async-start(), calls=%async_computation.9 | async-start | bytes 6291456 | tf_op jit(solution)/shard_map/reduce_scatter | solution.py:188
  137.7 5.0 copy-start.19
  196.9 27.1 %reduce-scatter.7.cloned.1.call-start = ((), (), s32[]{:S(2)}) async-start(), calls=%async_computation.7 | async-start | bytes 3145728 | tf_op jit(solution)/shard_map/reduce_scatter | solution.py:175
  206.2 17.8 %copy-start.18 = (bf16[512,1024]{1,0:T(8,128)(2,1)S(1)}, bf16[512,1024]{1,0:T(8,128)(2,1)}, u32[]{:S(2)}) copy-start(bf16[512,1024]{1,0:T(8,128)(2,1)} %param.33) | copy-start | bytes 3145732
  206.2 35.6 %all-gather.11.cloned.1.call-start = ((), (), s32[]{:S(2)}) async-start(), calls=%async_computation.10 | async-start | bytes 3145728 | tf_op jit(solution)/shard_map/all_gather | solution.py:196
  229.8 187.3 %reduce-scatter.11.cloned.1.call-start = ((), (), s32[]{:S(2)}) async-start(), calls=%async_computation.11 | async-start | bytes 3145728 | tf_op jit(solution)/shard_map/reduce_scatter | solution.py:243
  279.7 7.2 copy-start.2
  286.9 2.2 copy-start.5
  286.9 2.9 copy-start.7
  289.7 3.5 copy-start.4
  326.9 7.2 copy-start.2
  334.0 2.2 copy-start.5
  334.0 2.9 copy-start.7
  336.9 3.5 copy-start.4
  341.8 2.2 copy-start.9
  369.3 3.0 copy-start.14
  372.3 10.4 %copy-start.31 = (bf16[1024,1536]{1,0:T(8,128)(2,1)S(1)}, bf16[1024,1536]{1,0:T(8,128)(2,1)}, u32[]{:S(2)}) copy-start(bf16[1024,1536]{1,0:T(8,128)(2,1)} %copy-done.30) | copy-start | bytes 9437188
  387.4 482.9 %all-reduce.4.cloned.1.call-start = ((), (), s32[]{:S(2)}) async-start(), calls=%async_computation.12 | async-start | bytes 33554432 | tf_op jit(solution)/shard_map/psum | solution.py:255
  389.0 8.8 copy-start.51
  389.0 8.8 copy-start.55
  389.0 8.8 copy-start.56
  397.7 11.5 %copy-start.21 = (bf16[1024,1024]{1,0:T(8,128)(2,1)S(1)}, bf16[1024,1024]{1,0:T(8,128)(2,1)}, u32[]{:S(2)}) copy-start(bf16[1024,1024]{1,0:T(8,128)(2,1)} %all-gather.11.cloned.1.call-done) | copy-start | bytes 6291460
  397.7 11.5 %copy-start.25 = (bf16[2,512,512]{2,1,0:T(8,128)(2,1)S(1)}, bf16[2,512,512]{2,1,0:T(8,128)(2,1)}, u32[]{:S(2)}) copy-start(bf16[2,512,512]{2,1,0:T(8,128)(2,1)} %get-tuple-element.475) | copy-start | bytes 3145732
  409.3 2.3 copy-start.27
  409.3 2.3 copy-start.29
  409.3 2.3 copy-start.50
  417.1 3.5 copy-start.46
  417.1 3.5 copy-start.47
  418.3 46.7 %copy-start.20 = (bf16[512,1024]{1,0:T(8,128)(2,1)S(1)}, bf16[512,1024]{1,0:T(8,128)(2,1)}, u32[]{:S(2)}) copy-start(bf16[512,1024]{1,0:T(8,128)(2,1)} %reduce-scatter.11.cloned.1.call-done) | copy-start | bytes 3145732
  870.3 2.9 copy-start.16
  873.3 4.4 copy-start.17
  882.1 11.8 %copy-start.1 = (bf16[512,1024]{1,0:T(8,128)(2,1)S(1)}, bf16[512,1024]{1,0:T(8,128)(2,1)}, u32[]{:S(2)}) copy-start(bf16[512,1024]{1,0:T(8,128)(2,1)} %param.27) | copy-start | bytes 3145732
  (25 other events, 37.1 us)
Sparse Core Ops, SparseCore 0:
  12.7 13.2 all-gather.4
  119.2 13.2 reduce-scatter.4
  137.1 11.8 all-gather.6
  150.4 11.7 all-gather.8
  197.0 13.2 reduce-scatter.8
  212.9 11.0 reduce-scatter.6
  229.9 11.8 all-gather.10
  387.5 10.9 reduce-scatter.10
  417.2 453.0 all-reduce.3
where the time goes:
time: 906 us; the launch traced here: 901 us
  waiting for transfers between devices  456 us (50%)
  matrix products  167 us (18%)
  local copies, waits for them, and re-layouts  108 us (12%)
  other arithmetic  98.1 us (11%)
  blocking collectives  44.3 us (5%)
  between operations  14.8 us (2%)
  loops' own time  12.2 us (1%)
    psum x1, waiting for transfers between devices, on_device(): lax.psum(grad_qkv_w.astype(jnp.bfloat16), 'wide').astype(jnp.float32)  402 us
    psum x1, blocking collectives, on_device(): lax.psum((gain_one_grad, shift_one_grad, gain_two_grad, shift_two_grad),...  44.3 us
    dot_general x4, matrix products, times_transpose(): lax.dot_general(left, right, (((1,), (1,)), ((), ())), preferred_element_...  37.9 us
    dot_general x4, matrix products, transpose_times(): lax.dot_general(left, right, (((0,), (0,)), ((), ())), preferred_element_...  28 us
    convert_element_type x2, other arithmetic, attend_backward(): grad_scores = (attention_probs * (grad_probs - centre)).astype(jnp.bfloat16)  20.8 us
    dot_general x2, matrix products, attend_backward(): jnp.einsum('qhd,khd->hqk', grad_rows, value_pair, preferred_element_type=...  19.4 us
    unnamed x103, local copies, waits for them, and re-layouts  19.3 us
  transfers between devices with their start and end apart: 9, of which 7 were waited for; matrix products, arithmetic and copies ran while one was open for 8% of the time, Pallas kernels for 0%

commit v1 on v0

--- a/solution.py
+++ b/solution.py
@@ -83,7 +83,7 @@
     return (within < length_bound) & ((own_span == 2) | (key_block == block_index))
 
 
-def on_device(
+def on_device_any_mesh(
     tokens,
     window_span,
     valid_len,
@@ -277,7 +277,308 @@
     )
 
 
+PLANES = 4
+
+
+def wide_index(x, y, z):
+    return z * 4 + y * 2 + x
+
+
+def chip_positions():
+    return [(x, y, z) for z in range(PLANES) for y in range(2) for x in range(2)]
+
+
+def flip_pairs(axis):
+    if axis == "x":
+        return [(wide_index(x, y, z), wide_index(1 - x, y, z)) for x, y, z in chip_positions()]
+    return [(wide_index(x, y, z), wide_index(x, 1 - y, z)) for x, y, z in chip_positions()]
+
+
+def middle_flip_pairs(axis):
+    return [
+        pair for pair, (_, _, z) in zip(flip_pairs(axis), chip_positions()) if z in (1, 2)
+    ]
+
+
+def plane_pairs(moves):
+    return [
+        (wide_index(x, y, src), wide_index(x, y, dst))
+        for src, dst in moves
+        for y in range(2)
+        for x in range(2)
+    ]
+
+
+INWARD = ((0, 1), (3, 2))
+ACROSS = ((1, 2), (2, 1))
+OUTWARD = ((1, 0), (2, 3))
+
+
+def send(values, pairs):
+    return lax.ppermute(values, "wide", pairs)
+
+
+def partner(values):
+    return lax.ppermute(values, "narrow", [(0, 1), (1, 0)])
+
+
+def add_low(left, right):
+    return (left.astype(jnp.float32) + right.astype(jnp.float32)).astype(jnp.bfloat16)
+
+
+def ordered(own, other, own_first):
+    first = jnp.where(own_first, own, other)
+    second = jnp.where(own_first, other, own)
+    return jnp.concatenate([first, second], axis=0)
+
+
+def summed_over_wide(product, rows, outer):
+    position = lax.axis_index("wide")
+    inner = "y" if outer == "x" else "x"
+    outer_bit = position % 2 if outer == "x" else position // 2 % 2
+    plane = position // 4
+    half = rows // 2
+    away = product((1 - outer_bit) * half, half).astype(jnp.bfloat16)
+    received = send(away, flip_pairs(outer))
+    pair_sum = (product(outer_bit * half, half) + received.astype(jnp.float32)).astype(jnp.bfloat16)
+    column_sum = add_low(pair_sum, send(pair_sum, plane_pairs(INWARD)))
+    quarter = half // 2
+    upper = plane >= 2
+    first, second = column_sum[:quarter], column_sum[quarter:]
+    kept = jnp.where(upper, second, first)
+    given = jnp.where(upper, first, second)
+    line_sum = add_low(kept, send(given, plane_pairs(ACROSS)))
+    total = add_low(line_sum, send(line_sum, middle_flip_pairs(inner)))
+    full = ordered(total, send(total, plane_pairs(ACROSS)), jnp.logical_not(upper))
+    outward = send(full, plane_pairs(OUTWARD))
+    is_middle = (plane == 1) | (plane == 2)
+    full = jnp.where(is_middle, full, outward)
+    return ordered(full, send(full, flip_pairs(outer)), outer_bit == 0)
+
+
+def gradient_sum(left, right):
+    rows = left.shape[1]
+
+    def half_sum(base, outer):
+        def product(start, size):
+            columns = lax.dynamic_slice_in_dim(left, base + start, size, 1)
+            return transpose_times(columns, right)
+
+        return summed_over_wide(product, rows // 2, outer)
+
+    return jnp.concatenate([half_sum(0, "x"), half_sum(rows // 2, "y")], axis=0).astype(
+        jnp.float32
+    )
+
+
+def vector_sum(values):
+    values = values + partner(values)
+    values = values + send(values, flip_pairs("x"))
+    values = values + send(values, flip_pairs("y"))
+    values = values + send(values, plane_pairs(INWARD))
+    values = values + send(values, plane_pairs(ACROSS))
+    plane = lax.axis_index("wide") // 4
+    outward = send(values, plane_pairs(OUTWARD))
+    return jnp.where((plane == 1) | (plane == 2), values, outward)
+
+
+def rows_of(own, other):
+    return jnp.concatenate([own, other], axis=0)
+
+
+def rotary_own_first(position, width):
+    columns = jnp.arange(width) % HD
+    half_dim = HD // 2
+    freq_index = (columns % half_dim).astype(jnp.float32)
+    frequency = ROPE_BASE ** (-2.0 * freq_index / HD)
+    angles = position[:, None] * frequency[None, :]
+    signs = jnp.where(columns < half_dim, -1.0, 1.0).astype(jnp.float32)
+    return (jnp.cos(angles), jnp.sin(angles) * signs)
+
+
+def on_device(
+    tokens,
+    window_span,
+    valid_len,
+    norm1_gain,
+    norm1_shift,
+    w_query,
+    w_key,
+    w_value,
+    w_out,
+    norm2_gain,
+    norm2_shift,
+    w_gate,
+    w_up,
+    w_down,
+    cotangent,
+):
+    block_rows = tokens.shape[0]
+    local_width = w_query.shape[1]
+    local_heads = local_width // HD
+    local_hidden = w_gate.shape[1]
+    softmax_scale = HD ** (-0.5)
+    own_block = lax.axis_index("narrow")
+    joined = window_span[0] == 2
+    block_ids = jnp.stack([own_block, 1 - own_block])
+    lengths = valid_len[block_ids]
+    position = (
+        jnp.arange(block_rows)[None, :]
+        + block_rows * (block_ids[:, None] * joined.astype(jnp.int32))
+    ).reshape(-1).astype(jnp.float32)
+
+    token_values = tokens.astype(jnp.float32)
+    normed_one, scaled_one, inverse_one = norm_forward(token_values, norm1_gain, norm1_shift)
+    normed_one = normed_one.astype(jnp.bfloat16)
+    gathered_one = rows_of(normed_one, partner(normed_one))
+    cot_rows = rows_of(cotangent, partner(cotangent))
+    joined_qkv = jnp.concatenate([w_query, w_key, w_value], axis=1)
+    projected = jnp.dot(gathered_one, joined_qkv, preferred_element_type=jnp.float32)
+    cosine, sine_signed = rotary_own_first(position, local_width)
+    query_rows = (rotate(projected[:, :local_width], cosine, sine_signed) * softmax_scale).astype(
+        jnp.bfloat16
+    )
+    key_rows = rotate(projected[:, local_width : 2 * local_width], cosine, sine_signed).astype(
+        jnp.bfloat16
+    )
+    value_rows = projected[:, 2 * local_width :].astype(jnp.bfloat16)
+    query_heads = query_rows.reshape(2, block_rows, local_heads, HD)
+    key_heads = key_rows.reshape(2 * block_rows, local_heads, HD)
+    value_heads = value_rows.reshape(2 * block_rows, local_heads, HD)
+    offsets = jnp.arange(2 * block_rows)
+    within = offsets % block_rows < jnp.repeat(lengths, block_rows)
+
+    def masked_scores(index):
+        scores = jnp.einsum(
+            "qhd,khd->hqk", query_heads[index], key_heads, preferred_element_type=jnp.float32
+        )
+        key_mask = within & (joined | (offsets // block_rows == index))
+        return jnp.where(key_mask[None, None, :], scores, MASKED)
+
+    def attend_forward(index):
+        scores = masked_scores(index)
+        highest = jnp.max(scores, axis=-1, keepdims=True)
+        weights = jnp.exp(scores - highest)
+        weight_total = jnp.sum(weights, axis=-1, keepdims=True)
+        attention_probs = (weights / weight_total).astype(jnp.bfloat16)
+        mixed_block = jnp.einsum(
+            "hqk,khd->qhd", attention_probs, value_heads, preferred_element_type=jnp.float32
+        )
+        return (
+            mixed_block.reshape(block_rows, local_width).astype(jnp.bfloat16),
+            (highest + jnp.log(weight_total))[:, :, 0],
+        )
+
+    mixed_own, log_own = attend_forward(0)
+    mixed_other, log_other = attend_forward(1)
+    mixed_rows = rows_of(mixed_own, mixed_other)
+    other_share = jnp.dot(mixed_other, w_out, preferred_element_type=jnp.float32)
+    resid_values = (
+        token_values
+        + jnp.dot(mixed_own, w_out, preferred_element_type=jnp.float32)
+        + partner(other_share)
+    )
+    normed_two, scaled_two, inverse_two = norm_forward(resid_values, norm2_gain, norm2_shift)
+    normed_two = normed_two.astype(jnp.bfloat16)
+    gathered_two = rows_of(normed_two, partner(normed_two))
+    gate_values = jnp.dot(gathered_two, w_gate, preferred_element_type=jnp.float32)
+    up_values = jnp.dot(gathered_two, w_up, preferred_element_type=jnp.float32)
+    sigmoid_gate = jax.nn.sigmoid(gate_values)
+    hidden_rows = (gate_values * sigmoid_gate * up_values).astype(jnp.bfloat16)
+    down_summed = gradient_sum(hidden_rows, cot_rows)
+
+    out_other = jnp.dot(
+        hidden_rows[block_rows:], w_down, preferred_element_type=jnp.float32
+    ).astype(jnp.bfloat16)
+    out_values = (
+        resid_values
+        + jnp.dot(hidden_rows[:block_rows], w_down, preferred_element_type=jnp.float32)
+        + partner(out_other).astype(jnp.float32)
+    )
+    grad_hidden = times_transpose(cot_rows, w_down)
+    silu_grad = sigmoid_gate * (1.0 + gate_values * (1.0 - sigmoid_gate))
+    grad_gate = (grad_hidden * up_values * silu_grad).astype(jnp.bfloat16)
+    grad_up = (grad_hidden * gate_values * sigmoid_gate).astype(jnp.bfloat16)
+    gate_summed = gradient_sum(gathered_two, grad_gate)
+    up_summed = gradient_sum(gathered_two, grad_up)
+
+    def grad_two_share(rows):
+        return times_transpose(grad_gate[rows], w_gate) + times_transpose(grad_up[rows], w_up)
+
+    grad_two_other = grad_two_share(slice(block_rows, None))
+    grad_normed_two = grad_two_share(slice(0, block_rows)) + partner(grad_two_other)
+    grad_in_two, gain_two_grad, shift_two_grad = norm_backward(
+        grad_normed_two, scaled_two, inverse_two, norm2_gain
+    )
+    grad_resid = cotangent.astype(jnp.float32) + grad_in_two
+    grad_attention = grad_resid.astype(jnp.bfloat16)
+    grad_rows = rows_of(grad_attention, partner(grad_attention))
+    grad_mixed = times_transpose(grad_rows, w_out).astype(jnp.bfloat16)
+    out_summed = gradient_sum(mixed_rows, grad_rows)
+    grad_mixed_heads = grad_mixed.reshape(2, block_rows, local_heads, HD)
+
+    def attend_backward(index, log_total):
+        grad_block = grad_mixed_heads[index]
+        scores = masked_scores(index)
+        attention_probs = jnp.exp(scores - log_total[:, :, None])
+        grad_probs = jnp.einsum(
+            "qhd,khd->hqk", grad_block, value_heads, preferred_element_type=jnp.float32
+        )
+        centre = jnp.sum(attention_probs * grad_probs, axis=-1, keepdims=True)
+        grad_scores = (attention_probs * (grad_probs - centre)).astype(jnp.bfloat16)
+        block_query = jnp.einsum(
+            "hqk,khd->qhd", grad_scores, key_heads, preferred_element_type=jnp.float32
+        ).reshape(block_rows, local_width)
+        pair_key = jnp.einsum(
+            "hqk,qhd->khd", grad_scores, query_heads[index], preferred_element_type=jnp.float32
+        ).reshape(2 * block_rows, local_width)
+        pair_value = jnp.einsum(
+            "hqk,qhd->khd",
+            attention_probs.astype(jnp.bfloat16),
+            grad_block,
+            preferred_element_type=jnp.float32,
+        ).reshape(2 * block_rows, local_width)
+        return block_query, pair_key, pair_value
+
+    query_own, key_own, value_own = attend_backward(0, log_own)
+    query_other, key_other, value_other = attend_backward(1, log_other)
+    grad_query = rows_of(query_own, query_other)
+    grad_query_raw = rotate_back(grad_query * softmax_scale, cosine, sine_signed)
+    grad_key_raw = rotate_back(key_own + key_other, cosine, sine_signed)
+    grad_qkv = jnp.concatenate(
+        [grad_query_raw, grad_key_raw, value_own + value_other], axis=1
+    ).astype(jnp.bfloat16)
+    qkv_summed = gradient_sum(gathered_one, grad_qkv)
+    grad_one_other = times_transpose(grad_qkv[block_rows:], joined_qkv).astype(jnp.bfloat16)
+    grad_normed_one = times_transpose(grad_qkv[:block_rows], joined_qkv) + partner(
+        grad_one_other
+    ).astype(jnp.float32)
+    grad_in_one, gain_one_grad, shift_one_grad = norm_backward(
+        grad_normed_one, scaled_one, inverse_one, norm1_gain
+    )
+    token_grad = grad_resid + grad_in_one
+    norm_summed = vector_sum(
+        jnp.stack([gain_one_grad, shift_one_grad, gain_two_grad, shift_two_grad])
+    )
+    return (
+        out_values,
+        token_grad,
+        norm_summed[0],
+        norm_summed[1],
+        qkv_summed[:, :local_width],
+        qkv_summed[:, local_width : 2 * local_width],
+        qkv_summed[:, 2 * local_width :],
+        out_summed,
+        norm_summed[2],
+        norm_summed[3],
+        gate_summed,
+        up_summed,
+        down_summed,
+    )
+
+
 def solution(mesh):
+    fits = mesh.shape["wide"] == PLANES * 4 and mesh.shape["narrow"] == 2
     in_specs = (
         P(("wide", "narrow"), None),
         P("wide"),
@@ -311,5 +612,5 @@
         P("narrow", None),
     )
     return jax.shard_map(
-        on_device, mesh=mesh, in_specs=in_specs, out_specs=out_specs, check_vma=False
-    )
+        on_device if fits else on_device_any_mesh, mesh=mesh, in_specs=in_specs, out_specs=out_specs, check_vma=False
+    )

time: 906 us -> 885 us (0.977)
  starting transfers between devices: 0.37 us -> 205 us
  waiting for transfers between devices: 456 us -> 331 us
  blocking collectives: 44.3 us -> 0 us
  local copies, waits for them, and re-layouts: 108 us -> 67.3 us
  loops' own time: 12.2 us -> 0 us
  between operations: 14.8 us -> 3.49 us
  other arithmetic: 98.1 us -> 108 us
    psum x1 -> x0, waiting for transfers between devices: 402 us -> none  [on_device(): lax.psum(grad_qkv_w.astype(jnp.bfloat16), 'wide').astype(jnp.float32)]
    ppermute x0 -> x84, waiting for transfers between devices: none -> 331 us  [the longest x75 330 us: send(): return lax.ppermute(values, 'wide', pairs)]
    ppermute x0 -> x84, starting transfers between devices: none -> 205 us  [the longest x75 203 us: send(): return lax.ppermute(values, 'wide', pairs)]
    psum x1 -> x0, blocking collectives: 44.3 us -> none  [on_device(): lax.psum((gain_one_grad, shift_one_grad, gain_two_grad, shift_two_grad),...]
    reduce_scatter x4 -> x0, waiting for transfers between devices: 27.4 us -> none  [the longest x1 13.3 us: on_device(): lax.psum_scatter(jnp.dot(mixed_rows, w_out, preferred_element_type=jnp.fl...]
    all_gather x4 -> x0, waiting for transfers between devices: 26.2 us -> none  [the longest x1 11.9 us: on_device(): lax.all_gather(grad_resid.astype(jnp.bfloat16), 'narrow', axis=0, tiled=T...]
    convert_element_type x4 -> x36, other arithmetic: 13.2 us -> 33.5 us  [the longest x30 17.2 us: add_low(): (left.astype(jnp.float32) + right.astype(jnp.float32)).astype(jnp.bfloat16)]
    while x33 -> x0, local copies, waits for them, and re-layouts: 14.9 us -> none
  transfers between devices with their start and end apart: 9 -> 84, of which waited for: 7 -> 28; matrix products, arithmetic and copies ran while one was open for 8% -> 33% of each run, Pallas kernels for 0% -> 0%
where the time goes in v1:
time: 885 us; the launch traced here: 879 us
  waiting for transfers between devices  331 us (37%)
  starting transfers between devices  205 us (23%)
  matrix products  164 us (19%)
  other arithmetic  108 us (12%)
  local copies, waits for them, and re-layouts  67.3 us (8%)
    ppermute x75, waiting for transfers between devices, send(): return lax.ppermute(values, 'wide', pairs)  330 us
    ppermute x75, starting transfers between devices, send(): return lax.ppermute(values, 'wide', pairs)  203 us
    dot_general x8, matrix products, times_transpose(): lax.dot_general(left, right, (((1,), (1,)), ((), ())), preferred_element_...  31.2 us
    dot_general x20, matrix products, transpose_times(): lax.dot_general(left, right, (((0,), (0,)), ((), ())), preferred_element_...  26 us
    dot_general x2, matrix products, attend_backward(): jnp.einsum('qhd,khd->hqk', grad_block, value_heads, preferred_element_typ...  23.5 us
    convert_element_type x2, other arithmetic, attend_backward(): grad_scores = (attention_probs * (grad_probs - centre)).astype(jnp.bfloat16)  22.6 us
  transfers between devices with their start and end apart: 84, of which 28 were waited for; matrix products, arithmetic and copies ran while one was open for 33% of the time, Pallas kernels for 0%

profile of v1, /device:TPU:0, one launch (start us, length us, event | category | flops | bytes accessed | tf_op | source)
XLA Modules:
  0.0 878.8 jit_solution(8958427594670382393)
XLA Ops:
  10.9 6.0 fusion.53
  41.6 11.1 %fusion.44 = (bf16[1024,512]{1,0:T(8,128)(2,1)}, bf16[1024,512]{1,0:T(8,128)(2,1)S(1)}) fusion(f32[1024,512]{1,0:T(8,128)} %copy.52, f32[512]{0:T(512)S(1)} %get-tuple-element.102, f32[512]{0:T(512)S(1)} %get-tuple-element.101, f32[1024]{0:T(1024)S(1)} %bitcast.151, f32[1024,1536]{1,0:T(8,128)} %copy-done.14, f32[1024,512]{1,0:T(8,128)} %copy.49), kind=kLoop, calls=%fused_computation.99 | loop fusion | flops 5767168 | bytes 10493952 | tf_op jit(solution)/shard_map/convert_element_type | solution.py:441
  56.0 3.9 select_reduce_fusion
  65.8 4.3 fusion.91
  84.8 4.9 fusion.92
  96.1 6.8 fusion.191
  102.9 7.6 fusion.89
  110.5 14.3 %multiply_convert_fusion.3 = (bf16[1024,2048]{1,0:T(8,128)(2,1)S(1)}, bf16[1024,2048]{1,0:T(8,128)(2,1)}, bf16[1024,2048]{1,0:T(8,128)(2,1)S(1)}) fusion(f32[1024,2048]{1,0:T(8,128)} %fusion.191, f32[1024,2048]{1,0:T(8,128)} %fusion.89, bf16[1024,2048]{1,0:T(8,128)(2,1)} %param.26, bf16[512,1024]{1,0:T(8,128)(2,1)S(1)} %collective-permute-done.2, ...), kind=kOutput, calls=%fused_computation.22 | convolution fusion | flops 4332716032 | bytes 35651584 | tf_op jit(solution)/shard_map/dot_general | solution.py:484
  124.9 4.7 fusion.54
  136.9 3.8 fusion.80
  153.9 15.2 %collective-permute-done.49 = bf16[256,2048]{1,0:T(8,128)(2,1)S(1)} collective-permute-done((bf16[256,2048]{1,0:T(8,128)(2,1)S(1)}, bf16[256,2048]{1,0:T(8,128)(2,1)S(1)}, u32[]{:S(2)}, u32[]{:S(2)}) %collective-permute-start.49) | collective-permute-done | bytes 1048608 | tf_op jit(solution)/shard_map/ppermute | solution.py:318
  175.2 16.3 %collective-permute-done.77 = bf16[512,1024]{1,0:T(8,128)(2,1)S(1)} collective-permute-done((bf16[512,1024]{1,0:T(8,128)(2,1)S(1)}, bf16[512,1024]{1,0:T(8,128)(2,1)S(1)}, u32[]{:S(2)}, u32[]{:S(2)}) %collective-permute-start.77) | collective-permute-done | bytes 1048608 | tf_op jit(solution)/shard_map/ppermute | solution.py:318
  199.7 13.9 %collective-permute-done.63 = bf16[256,2048]{1,0:T(8,128)(2,1)S(1)} collective-permute-done((bf16[256,2048]{1,0:T(8,128)(2,1)S(1)}, bf16[256,2048]{1,0:T(8,128)(2,1)S(1)}, u32[]{:S(2)}, u32[]{:S(2)}) %collective-permute-start.63) | collective-permute-done | bytes 1048608 | tf_op jit(solution)/shard_map/ppermute | solution.py:318
  223.2 5.0 convert_add_fusion.2
  230.8 6.7 multiply_reduce_fusion.2
  244.8 22.0 %collective-permute-done.64 = bf16[256,2048]{1,0:T(8,128)(2,1)S(1)} collective-permute-done((bf16[256,2048]{1,0:T(8,128)(2,1)S(1)}, bf16[256,2048]{1,0:T(8,128)(2,1)S(1)}, u32[]{:S(2)}, u32[]{:S(2)}) %collective-permute-start.64) | collective-permute-done | bytes 1048608 | tf_op jit(solution)/shard_map/ppermute | solution.py:318
  268.1 43.7 %collective-permute-done.78 = bf16[512,1024]{1,0:T(8,128)(2,1)S(1)} collective-permute-done((bf16[512,1024]{1,0:T(8,128)(2,1)S(1)}, bf16[512,1024]{1,0:T(8,128)(2,1)S(1)}, u32[]{:S(2)}, u32[]{:S(2)}) %collective-permute-start.78) | collective-permute-done | bytes 1048608 | tf_op jit(solution)/shard_map/ppermute | solution.py:318
  314.1 17.8 %collective-permute-done.71 = bf16[512,1024]{1,0:T(8,128)(2,1)S(1)} collective-permute-done((bf16[512,1024]{1,0:T(8,128)(2,1)S(1)}, bf16[512,1024]{1,0:T(8,128)(2,1)S(1)}, u32[]{:S(2)}, u32[]{:S(2)}) %collective-permute-start.71) | collective-permute-done | bytes 1048608 | tf_op jit(solution)/shard_map/ppermute | solution.py:318
  350.9 4.4 fusion.4
  355.3 8.2 multiply_reduce_fusion
  363.6 15.2 %multiply_reduce_fusion.1 = (f32[8,512]{1,0:T(8,128)S(1)}, f32[8,512,1024]{2,1,0:T(8,128)}) fusion(f32[8,512,1024]{2,1,0:T(8,128)} %copy-done.4, f32[8,512]{1,0:T(8,128)S(1)} %log_add_fusion.1, pred[1024]{0:T(1024)(128)(4,1)S(1)} %get-tuple-element.23, bf16[512,8,64]{0,2,1:T(8,128)(2,1)S(1)} %bitcast.136, bf16[1024,8,64]{0,2,1:T(8,128)(2,1)S(1)} %bitcast.121), kind=kOutput, calls=%fused_computation.5 | convolution fusion | flops 553644032 | bytes 35161088 | tf_op jit(solution)/shard_map/qhd,khd->hqk/dot_general | solution.py:524
  378.8 10.5 %multiply_convert_fusion.1 = bf16[8,512,1024]{2,1,0:T(8,128)(2,1)} fusion(f32[8,512,1024]{2,1,0:T(8,128)} %get-tuple-element.97, f32[8,512,1024]{2,1,0:T(8,128)S(1)} %bitcast.111, f32[8,512]{1,0:T(8,128)S(1)} %get-tuple-element.96, f32[8,512]{1,0:T(8,128)S(1)} %log_add_fusion.1, pred[1024]{0:T(1024)(128)(4,1)S(1)} %get-tuple-element.23), kind=kLoop, calls=%fused_computation.4 | loop fusion | flops 20971520 | bytes 41976832 | tf_op jit(solution)/shard_map/convert_element_type | solution.py:528
  389.4 7.1 fusion.192
  396.4 6.5 fusion.194
  402.9 3.8 add_convert_fusion.8
  408.1 12.1 %multiply_convert_fusion = bf16[8,512,1024]{2,1,0:T(8,128)(2,1)S(1)} fusion(f32[8,512,1024]{2,1,0:T(8,128)} %get-tuple-element.95, f32[8,512,1024]{2,1,0:T(8,128)} %copy-done.3, f32[8,512]{1,0:T(8,128)S(1)} %get-tuple-element.94, f32[8,512]{1,0:T(8,128)S(1)} %copy-done.43, pred[1024]{0:T(1024)(128)(4,1)S(1)} %fusion.146), kind=kLoop, calls=%fused_computation.1 | loop fusion | flops 20971520 | bytes 41976832 | tf_op jit(solution)/shard_map/convert_element_type | solution.py:528
  424.5 8.5 fusion.66
  450.7 9.9 %fusion.46 = (bf16[1024,512]{1,0:T(8,128)(2,1)S(1)}, bf16[1024,512]{1,0:T(8,128)(2,1)S(1)}) fusion(f32[1024,512]{1,0:T(8,128)} %copy.57, f32[512,512]{1,0:T(8,128)S(1)} %copy-done.30, f32[512,512]{1,0:T(8,128)} %copy.55, f32[512]{0:T(512)S(1)} %copy-done.51, f32[1024]{0:T(1024)S(1)} %bitcast.153, f32[1024,512]{1,0:T(8,128)} %copy.59, f32[1024,512]{1,0:T(8,128)} %copy.58), kind=kLoop, calls=%fused_computation.101 | loop fusion | flops 4718592 | bytes 10491904 | tf_op jit(solution)/shard_map/convert
  480.7 18.8 %collective-permute-done.35 = bf16[128,1024]{1,0:T(8,128)(2,1)S(1)} collective-permute-done((bf16[128,1024]{1,0:T(8,128)(2,1)S(1)}, bf16[128,1024]{1,0:T(8,128)(2,1)S(1)}, u32[]{:S(2)}, u32[]{:S(2)}) %collective-permute-start.35) | collective-permute-done | bytes 262176 | tf_op jit(solution)/shard_map/ppermute | solution.py:318
  500.5 37.1 %collective-permute-start.36 = (bf16[128,1024]{1,0:T(8,128)(2,1)S(1)}, bf16[128,1024]{1,0:T(8,128)(2,1)S(1)}, u32[]{:S(2)}, u32[]{:S(2)}) collective-permute-start(bf16[128,1024]{1,0:T(8,128)(2,1)S(1)} %fusion.94), channel_id=1, source_target_pairs={{0,8},{2,10},{4,12},{6,14},{24,16},{26,18},{28,20},{30,22},{1,9},{... | collective-permute-start | bytes 786440 | tf_op jit(solution)/shard_map/ppermute | solution.py:318
  541.5 5.6 collective-permute-start.29
  547.2 3.8 collective-permute-done.29
  565.5 65.9 %collective-permute-start.22 = (bf16[256,1536]{1,0:T(8,128)(2,1)S(1)}, bf16[256,1536]{1,0:T(8,128)(2,1)S(1)}, u32[]{:S(2)}, u32[]{:S(2)}) collective-permute-start(bf16[256,1536]{1,0:T(8,128)(2,1)S(1)} %fusion.21), channel_id=1, source_target_pairs={{0,8},{2,10},{4,12},{6,14},{24,16},{26,18},{28,20},{30,22},{1,9},{... | collective-permute-start | bytes 2359304 | tf_op jit(solution)/shard_map/ppermute | solution.py:318
  645.6 10.7 %collective-permute-start.11 = (f32[4,1024]{1,0:T(4,128)S(1)}, f32[4,1024]{1,0:T(4,128)S(1)}, u32[]{:S(2)}, u32[]{:S(2)}) collective-permute-start(f32[4,1024]{1,0:T(4,128)S(1)} %add.477), channel_id=1, source_target_pairs={{0,8},{2,10},{4,12},{6,14},{24,16},{26,18},{28,20},{30,22},{1,9},{... | collective-permute-start | bytes 49160 | tf_op jit(solution)/shard_map/ppermute | solution.py:318
  661.7 7.1 collective-permute-done.13
  671.3 6.0 collective-permute-done.33
  688.9 6.3 collective-permute-done.15
  698.7 31.5 %collective-permute-done.82 = bf16[512,1024]{1,0:T(8,128)(2,1)S(1)} collective-permute-done((bf16[512,1024]{1,0:T(8,128)(2,1)S(1)}, bf16[512,1024]{1,0:T(8,128)(2,1)S(1)}, u32[]{:S(2)}, u32[]{:S(2)}) %collective-permute-start.82) | collective-permute-done | bytes 1048608 | tf_op jit(solution)/shard_map/ppermute | solution.py:318
  731.3 21.4 %collective-permute-done.75 = bf16[512,1024]{1,0:T(8,128)(2,1)S(1)} collective-permute-done((bf16[512,1024]{1,0:T(8,128)(2,1)S(1)}, bf16[512,1024]{1,0:T(8,128)(2,1)S(1)}, u32[]{:S(2)}, u32[]{:S(2)}) %collective-permute-start.75) | collective-permute-done | bytes 1048608 | tf_op jit(solution)/shard_map/ppermute | solution.py:318
  755.9 11.0 %collective-permute-done.61 = bf16[256,2048]{1,0:T(8,128)(2,1)S(1)} collective-permute-done((bf16[256,2048]{1,0:T(8,128)(2,1)S(1)}, bf16[256,2048]{1,0:T(8,128)(2,1)S(1)}, u32[]{:S(2)}, u32[]{:S(2)}) %collective-permute-start.61) | collective-permute-done | bytes 1048608 | tf_op jit(solution)/shard_map/ppermute | solution.py:318
  777.9 20.4 %collective-permute-done.69 = bf16[256,2048]{1,0:T(8,128)(2,1)S(1)} collective-permute-done((bf16[256,2048]{1,0:T(8,128)(2,1)S(1)}, bf16[256,2048]{1,0:T(8,128)(2,1)S(1)}, u32[]{:S(2)}, u32[]{:S(2)}) %collective-permute-start.69) | collective-permute-done | bytes 1048608 | tf_op jit(solution)/shard_map/ppermute | solution.py:318
  799.2 3.9 maximum_convert_fusion
  803.3 10.3 %collective-permute-done.83 = bf16[512,1024]{1,0:T(8,128)(2,1)S(1)} collective-permute-done((bf16[512,1024]{1,0:T(8,128)(2,1)S(1)}, bf16[512,1024]{1,0:T(8,128)(2,1)S(1)}, u32[]{:S(2)}, u32[]{:S(2)}) %collective-permute-start.83) | collective-permute-done | bytes 1048608 | tf_op jit(solution)/shard_map/ppermute | solution.py:318
  813.7 3.9 maximum_convert_fusion.1
  820.7 32.2 %collective-permute-done.26 = bf16[256,1536]{1,0:T(8,128)(2,1)S(1)} collective-permute-done((bf16[256,1536]{1,0:T(8,128)(2,1)S(1)}, bf16[256,1536]{1,0:T(8,128)(2,1)S(1)}, u32[]{:S(2)}, u32[]{:S(2)}) %collective-permute-start.26) | collective-permute-done | bytes 786464 | tf_op jit(solution)/shard_map/ppermute | solution.py:318
  854.1 7.2 collective-permute-done.19
  864.8 3.9 maximum_convert_fusion.2
  868.8 6.0 collective-permute-done.20
  (481 shorter events, 268.4 us)
Async XLA Ops:
  0.7 93.2 %collective-permute-start.4 = (bf16[512,1024]{1,0:T(8,128)(2,1)}, bf16[512,1024]{1,0:T(8,128)(2,1)}, u32[]{:S(2)}, u32[]{:S(2)}) collective-permute-start(bf16[512,1024]{1,0:T(8,128)(2,1)} %param.29), channel_id=1, source_target_pairs={{0,1},{1,0},{2,3},{3,2},{4,5},{5,4},{6,7},{7,6},{8,9},{9,8},{10,11... | collective-permute-start | bytes 3145736 | tf_op jit(solution)/shard_map/ppermute | solution.py:322
  136.7 85.0 %collective-permute-start.3 = (bf16[512,1024]{1,0:T(8,128)(2,1)}, bf16[512,1024]{1,0:T(8,128)(2,1)}, u32[]{:S(2)}, u32[]{:S(2)}) collective-permute-start(bf16[512,1024]{1,0:T(8,128)(2,1)} %fusion.86), channel_id=1, source_target_pairs={{0,1},{1,0},{2,3},{3,2},{4,5},{5,4},{6,7},{7,6},{8,9},{9,8},{10,11... | collective-permute-start | bytes 3145736 | tf_op jit(solution)/shard_map/ppermute | solution.py:322
  140.6 87.5 %collective-permute-start.5 = (f32[512,1024]{1,0:T(8,128)}, f32[512,1024]{1,0:T(8,128)S(1)}, u32[]{:S(2)}, u32[]{:S(2)}) collective-permute-start(f32[512,1024]{1,0:T(8,128)} %fusion.80), channel_id=1, source_target_pairs={{0,1},{1,0},{2,3},{3,2},{4,5},{5,4},{6,7},{7,6},{8,9},{9,8},{10,11... | collective-permute-start | bytes 6291464 | tf_op jit(solution)/shard_map/ppermute | solution.py:322
  142.3 26.7 %collective-permute-start.49 = (bf16[256,2048]{1,0:T(8,128)(2,1)S(1)}, bf16[256,2048]{1,0:T(8,128)(2,1)S(1)}, u32[]{:S(2)}, u32[]{:S(2)}) collective-permute-start(bf16[256,2048]{1,0:T(8,128)(2,1)S(1)} %convolution_convert_fusion.2), channel_id=1, source_target_pairs={{0,4},{2,6},{4,0},{6,2},{8,12},{10,14},{12,8},{14,10},{16,20},{18,... | collective-permute-start | bytes 3145736 | tf_op jit(solution)/shard_map/ppermute | solution.py:318
  146.3 26.0 %collective-permute-start.42 = (bf16[256,2048]{1,0:T(8,128)(2,1)S(1)}, bf16[256,2048]{1,0:T(8,128)(2,1)S(1)}, u32[]{:S(2)}, u32[]{:S(2)}) collective-permute-start(bf16[256,2048]{1,0:T(8,128)(2,1)S(1)} %convolution_convert_fusion.3), channel_id=1, source_target_pairs={{0,2},{2,0},{4,6},{6,4},{8,10},{10,8},{12,14},{14,12},{16,18},{18,... | collective-permute-start | bytes 3145736 | tf_op jit(solution)/shard_map/ppermute | solution.py:318
  149.2 42.4 %collective-permute-start.77 = (bf16[512,1024]{1,0:T(8,128)(2,1)S(1)}, bf16[512,1024]{1,0:T(8,128)(2,1)S(1)}, u32[]{:S(2)}, u32[]{:S(2)}) collective-permute-start(bf16[512,1024]{1,0:T(8,128)(2,1)S(1)} %convolution_convert_fusion.6), channel_id=1, source_target_pairs={{0,4},{2,6},{4,0},{6,2},{8,12},{10,14},{12,8},{14,10},{16,20},{18,... | collective-permute-start | bytes 3145736 | tf_op jit(solution)/shard_map/ppermute | solution.py:318
  169.1 25.8 %collective-permute-start.70 = (bf16[512,1024]{1,0:T(8,128)(2,1)S(1)}, bf16[512,1024]{1,0:T(8,128)(2,1)S(1)}, u32[]{:S(2)}, u32[]{:S(2)}) collective-permute-start(bf16[512,1024]{1,0:T(8,128)(2,1)S(1)} %convolution_convert_fusion.7), channel_id=1, source_target_pairs={{0,2},{2,0},{4,6},{6,4},{8,10},{10,8},{12,14},{14,12},{16,18},{18,... | collective-permute-start | bytes 3145736 | tf_op jit(solution)/shard_map/ppermute | solution.py:318
  172.3 41.3 %collective-permute-start.63 = (bf16[256,2048]{1,0:T(8,128)(2,1)S(1)}, bf16[256,2048]{1,0:T(8,128)(2,1)S(1)}, u32[]{:S(2)}, u32[]{:S(2)}) collective-permute-start(bf16[256,2048]{1,0:T(8,128)(2,1)S(1)} %convolution_convert_fusion), channel_id=1, source_target_pairs={{0,4},{2,6},{4,0},{6,2},{8,12},{10,14},{12,8},{14,10},{16,20},{18,... | collective-permute-start | bytes 3145736 | tf_op jit(solution)/shard_map/ppermute | solution.py:318
  191.5 27.3 %collective-permute-start.56 = (bf16[256,2048]{1,0:T(8,128)(2,1)S(1)}, bf16[256,2048]{1,0:T(8,128)(2,1)S(1)}, u32[]{:S(2)}, u32[]{:S(2)}) collective-permute-start(bf16[256,2048]{1,0:T(8,128)(2,1)S(1)} %convolution_convert_fusion.1), channel_id=1, source_target_pairs={{0,2},{2,0},{4,6},{6,4},{8,10},{10,8},{12,14},{14,12},{16,18},{18,... | collective-permute-start | bytes 3145736 | tf_op jit(solution)/shard_map/ppermute | solution.py:318
  194.8 44.8 %collective-permute-start.50 = (bf16[256,2048]{1,0:T(8,128)(2,1)S(1)}, bf16[256,2048]{1,0:T(8,128)(2,1)S(1)}, u32[]{:S(2)}, u32[]{:S(2)}) collective-permute-start(bf16[256,2048]{1,0:T(8,128)(2,1)S(1)} %fusion.23), channel_id=1, source_target_pairs={{0,8},{2,10},{4,12},{6,14},{24,16},{26,18},{28,20},{30,22},{1,9},{... | collective-permute-start | bytes 3145736 | tf_op jit(solution)/shard_map/ppermute | solution.py:318
  213.7 30.7 %collective-permute-start.43 = (bf16[256,2048]{1,0:T(8,128)(2,1)S(1)}, bf16[256,2048]{1,0:T(8,128)(2,1)S(1)}, u32[]{:S(2)}, u32[]{:S(2)}) collective-permute-start(bf16[256,2048]{1,0:T(8,128)(2,1)S(1)} %fusion.22), channel_id=1, source_target_pairs={{0,8},{2,10},{4,12},{6,14},{24,16},{26,18},{28,20},{30,22},{1,9},{... | collective-permute-start | bytes 3145736 | tf_op jit(solution)/shard_map/ppermute | solution.py:318
  218.8 48.0 %collective-permute-start.64 = (bf16[256,2048]{1,0:T(8,128)(2,1)S(1)}, bf16[256,2048]{1,0:T(8,128)(2,1)S(1)}, u32[]{:S(2)}, u32[]{:S(2)}) collective-permute-start(bf16[256,2048]{1,0:T(8,128)(2,1)S(1)} %fusion.25), channel_id=1, source_target_pairs={{0,8},{2,10},{4,12},{6,14},{24,16},{26,18},{28,20},{30,22},{1,9},{... | collective-permute-start | bytes 3145736 | tf_op jit(solution)/shard_map/ppermute | solution.py:318
  221.8 91.1 %collective-permute-start.57 = (bf16[256,2048]{1,0:T(8,128)(2,1)S(1)}, bf16[256,2048]{1,0:T(8,128)(2,1)S(1)}, u32[]{:S(2)}, u32[]{:S(2)}) collective-permute-start(bf16[256,2048]{1,0:T(8,128)(2,1)S(1)} %fusion.24), channel_id=1, source_target_pairs={{0,8},{2,10},{4,12},{6,14},{24,16},{26,18},{28,20},{30,22},{1,9},{... | collective-permute-start | bytes 3145736 | tf_op jit(solution)/shard_map/ppermute | solution.py:318
  229.5 82.3 %collective-permute-start.78 = (bf16[512,1024]{1,0:T(8,128)(2,1)S(1)}, bf16[512,1024]{1,0:T(8,128)(2,1)S(1)}, u32[]{:S(2)}, u32[]{:S(2)}) collective-permute-start(bf16[512,1024]{1,0:T(8,128)(2,1)S(1)} %add_convert_fusion.1), channel_id=1, source_target_pairs={{0,8},{2,10},{4,12},{6,14},{24,16},{26,18},{28,20},{30,22},{1,9},{... | collective-permute-start | bytes 3145736 | tf_op jit(solution)/shard_map/ppermute | solution.py:318
  239.6 92.2 %collective-permute-start.71 = (bf16[512,1024]{1,0:T(8,128)(2,1)S(1)}, bf16[512,1024]{1,0:T(8,128)(2,1)S(1)}, u32[]{:S(2)}, u32[]{:S(2)}) collective-permute-start(bf16[512,1024]{1,0:T(8,128)(2,1)S(1)} %add_convert_fusion.3), channel_id=1, source_target_pairs={{0,8},{2,10},{4,12},{6,14},{24,16},{26,18},{28,20},{30,22},{1,9},{... | collective-permute-start | bytes 3145736 | tf_op jit(solution)/shard_map/ppermute | solution.py:318
  244.3 103.0 %collective-permute-start.6 = (bf16[512,1024]{1,0:T(8,128)(2,1)S(1)}, bf16[512,1024]{1,0:T(8,128)(2,1)S(1)}, u32[]{:S(2)}, u32[]{:S(2)}) collective-permute-start(bf16[512,1024]{1,0:T(8,128)(2,1)S(1)} %get-tuple-element.21), channel_id=1, source_target_pairs={{0,1},{1,0},{2,3},{3,2},{4,5},{5,4},{6,7},{7,6},{8,9},{9,8},{10,11... | collective-permute-start | bytes 3145736 | tf_op jit(solution)/shard_map/ppermute | solution.py:322
  266.8 66.3 %collective-permute-start.51 = (bf16[128,2048]{1,0:T(8,128)(2,1)S(1)}, bf16[128,2048]{1,0:T(8,128)(2,1)S(1)}, u32[]{:S(2)}, u32[]{:S(2)}) collective-permute-start(bf16[128,2048]{1,0:T(8,128)(2,1)S(1)} %broadcast_select_fusion.32), channel_id=1, source_target_pairs={{8,16},{10,18},{12,20},{14,22},{16,8},{18,10},{20,12},{22,14},{9,1... | collective-permute-start | bytes 1572872 | tf_op jit(solution)/shard_map/ppermute | solution.py:318
  311.8 23.4 %collective-permute-start.44 = (bf16[128,2048]{1,0:T(8,128)(2,1)S(1)}, bf16[128,2048]{1,0:T(8,128)(2,1)S(1)}, u32[]{:S(2)}, u32[]{:S(2)}) collective-permute-start(bf16[128,2048]{1,0:T(8,128)(2,1)S(1)} %broadcast_select_fusion.33), channel_id=1, source_target_pairs={{8,16},{10,18},{12,20},{14,22},{16,8},{18,10},{20,12},{22,14},{9,1... | collective-permute-start | bytes 1572872 | tf_op jit(solution)/shard_map/ppermute | solution.py:318
  312.9 24.1 %collective-permute-start.65 = (bf16[128,2048]{1,0:T(8,128)(2,1)S(1)}, bf16[128,2048]{1,0:T(8,128)(2,1)S(1)}, u32[]{:S(2)}, u32[]{:S(2)}) collective-permute-start(bf16[128,2048]{1,0:T(8,128)(2,1)S(1)} %broadcast_select_fusion.30), channel_id=1, source_target_pairs={{8,16},{10,18},{12,20},{14,22},{16,8},{18,10},{20,12},{22,14},{9,1... | collective-permute-start | bytes 1572872 | tf_op jit(solution)/shard_map/ppermute | solution.py:318
  337.0 132.4 %collective-permute-start.52 = (bf16[128,2048]{1,0:T(8,128)(2,1)}, bf16[128,2048]{1,0:T(8,128)(2,1)}, u32[]{:S(2)}, u32[]{:S(2)}) collective-permute-start(bf16[128,2048]{1,0:T(8,128)(2,1)} %add_convert_fusion.21), channel_id=1, source_target_pairs={{8,10},{10,8},{12,14},{14,12},{16,18},{18,16},{20,22},{22,20},{9,1... | collective-permute-start | bytes 1572872 | tf_op jit(solution)/shard_map/ppermute | solution.py:318
  339.6 132.8 %collective-permute-start.45 = (bf16[128,2048]{1,0:T(8,128)(2,1)}, bf16[128,2048]{1,0:T(8,128)(2,1)}, u32[]{:S(2)}, u32[]{:S(2)}) collective-permute-start(bf16[128,2048]{1,0:T(8,128)(2,1)} %add_convert_fusion.23), channel_id=1, source_target_pairs={{8,12},{10,14},{12,8},{14,10},{16,20},{18,22},{20,16},{22,18},{9,1... | collective-permute-start | bytes 1572872 | tf_op jit(solution)/shard_map/ppermute | solution.py:318
  342.1 131.7 %collective-permute-start.66 = (bf16[128,2048]{1,0:T(8,128)(2,1)}, bf16[128,2048]{1,0:T(8,128)(2,1)}, u32[]{:S(2)}, u32[]{:S(2)}) collective-permute-start(bf16[128,2048]{1,0:T(8,128)(2,1)} %add_convert_fusion.17), channel_id=1, source_target_pairs={{8,10},{10,8},{12,14},{14,12},{16,18},{18,16},{20,22},{22,20},{9,1... | collective-permute-start | bytes 1572872 | tf_op jit(solution)/shard_map/ppermute | solution.py:318
  344.6 132.1 %collective-permute-start.59 = (bf16[128,2048]{1,0:T(8,128)(2,1)}, bf16[128,2048]{1,0:T(8,128)(2,1)}, u32[]{:S(2)}, u32[]{:S(2)}) collective-permute-start(bf16[128,2048]{1,0:T(8,128)(2,1)} %add_convert_fusion.19), channel_id=1, source_target_pairs={{8,12},{10,14},{12,8},{14,10},{16,20},{18,22},{20,16},{22,18},{9,1... | collective-permute-start | bytes 1572872 | tf_op jit(solution)/shard_map/ppermute | solution.py:318
  347.3 131.4 %collective-permute-start.80 = (bf16[256,1024]{1,0:T(8,128)(2,1)}, bf16[256,1024]{1,0:T(8,128)(2,1)}, u32[]{:S(2)}, u32[]{:S(2)}) collective-permute-start(bf16[256,1024]{1,0:T(8,128)(2,1)} %add_convert_fusion.13), channel_id=1, source_target_pairs={{8,10},{10,8},{12,14},{14,12},{16,18},{18,16},{20,22},{22,20},{9,1... | collective-permute-start | bytes 1572872 | tf_op jit(solution)/shard_map/ppermute | solution.py:318
  470.0 30.5 %collective-permute-start.73 = (bf16[256,1024]{1,0:T(8,128)(2,1)S(1)}, bf16[256,1024]{1,0:T(8,128)(2,1)S(1)}, u32[]{:S(2)}, u32[]{:S(2)}) collective-permute-start(bf16[256,1024]{1,0:T(8,128)(2,1)S(1)} %copy-done.31), channel_id=1, source_target_pairs={{8,12},{10,14},{12,8},{14,10},{16,20},{18,22},{20,16},{22,18},{9,1... | collective-permute-start | bytes 1572872 | tf_op jit(solution)/shard_map/ppermute | solution.py:318
  472.4 160.5 %collective-permute-start.7 = (bf16[512,1024]{1,0:T(8,128)(2,1)S(1)}, bf16[512,1024]{1,0:T(8,128)(2,1)S(1)}, u32[]{:S(2)}, u32[]{:S(2)}) collective-permute-start(bf16[512,1024]{1,0:T(8,128)(2,1)S(1)} %fusion.83), channel_id=1, source_target_pairs={{0,1},{1,0},{2,3},{3,2},{4,5},{5,4},{6,7},{7,6},{8,9},{9,8},{10,11... | collective-permute-start | bytes 3145736 | tf_op jit(solution)/shard_map/ppermute | solution.py:322
  473.8 86.0 %collective-permute-start.21 = (bf16[256,1536]{1,0:T(8,128)(2,1)S(1)}, bf16[256,1536]{1,0:T(8,128)(2,1)S(1)}, u32[]{:S(2)}, u32[]{:S(2)}) collective-permute-start(bf16[256,1536]{1,0:T(8,128)(2,1)S(1)} %convolution_convert_fusion.4), channel_id=1, source_target_pairs={{0,4},{2,6},{4,0},{6,2},{8,12},{10,14},{12,8},{14,10},{16,20},{18,... | collective-permute-start | bytes 2359304 | tf_op jit(solution)/shard_map/ppermute | solution.py:318
  476.7 85.9 %collective-permute-start.14 = (bf16[256,1536]{1,0:T(8,128)(2,1)S(1)}, bf16[256,1536]{1,0:T(8,128)(2,1)S(1)}, u32[]{:S(2)}, u32[]{:S(2)}) collective-permute-start(bf16[256,1536]{1,0:T(8,128)(2,1)S(1)} %convolution_convert_fusion.5), channel_id=1, source_target_pairs={{0,2},{2,0},{4,6},{6,4},{8,10},{10,8},{12,14},{14,12},{16,18},{18,... | collective-permute-start | bytes 2359304 | tf_op jit(solution)/shard_map/ppermute | solution.py:318
  499.5 38.4 %collective-permute-start.28 = (bf16[128,1024]{1,0:T(8,128)(2,1)S(1)}, bf16[128,1024]{1,0:T(8,128)(2,1)S(1)}, u32[]{:S(2)}, u32[]{:S(2)}) collective-permute-start(bf16[128,1024]{1,0:T(8,128)(2,1)S(1)} %convolution_convert_fusion.10), channel_id=1, source_target_pairs={{0,2},{2,0},{4,6},{6,4},{8,10},{10,8},{12,14},{14,12},{16,18},{18,... | collective-permute-start | bytes 786440 | tf_op jit(solution)/shard_map/ppermute | solution.py:318
  500.5 41.0 %collective-permute-start.36 = (bf16[128,1024]{1,0:T(8,128)(2,1)S(1)}, bf16[128,1024]{1,0:T(8,128)(2,1)S(1)}, u32[]{:S(2)}, u32[]{:S(2)}) collective-permute-start(bf16[128,1024]{1,0:T(8,128)(2,1)S(1)} %fusion.94), channel_id=1, source_target_pairs={{0,8},{2,10},{4,12},{6,14},{24,16},{26,18},{28,20},{30,22},{1,9},{... | collective-permute-start | bytes 786440 | tf_op jit(solution)/shard_map/ppermute | solution.py:318
  557.1 139.8 %collective-permute-start.54 = (bf16[256,2048]{1,0:T(8,128)(2,1)S(1)}, bf16[256,2048]{1,0:T(8,128)(2,1)S(1)}, u32[]{:S(2)}, u32[]{:S(2)}) collective-permute-start(bf16[256,2048]{1,0:T(8,128)(2,1)S(1)} %pad_maximum_fusion.8), channel_id=1, source_target_pairs={{8,0},{10,2},{12,4},{14,6},{16,24},{18,26},{20,28},{22,30},{9,1},{... | collective-permute-start | bytes 3145736 | tf_op jit(solution)/shard_map/ppermute | solution.py:318
  558.5 195.3 %collective-permute-start.47 = (bf16[256,2048]{1,0:T(8,128)(2,1)S(1)}, bf16[256,2048]{1,0:T(8,128)(2,1)S(1)}, u32[]{:S(2)}, u32[]{:S(2)}) collective-permute-start(bf16[256,2048]{1,0:T(8,128)(2,1)S(1)} %pad_maximum_fusion.7), channel_id=1, source_target_pairs={{8,0},{10,2},{12,4},{14,6},{16,24},{18,26},{20,28},{22,30},{9,1},{... | collective-permute-start | bytes 3145736 | tf_op jit(solution)/shard_map/ppermute | solution.py:318
  562.6 68.8 %collective-permute-start.31 = (bf16[64,1024]{1,0:T(8,128)(2,1)S(1)}, bf16[64,1024]{1,0:T(8,128)(2,1)S(1)}, u32[]{:S(2)}, u32[]{:S(2)}) collective-permute-start(bf16[64,1024]{1,0:T(8,128)(2,1)S(1)} %add_convert_fusion.33), channel_id=1, source_target_pairs={{8,12},{10,14},{12,8},{14,10},{16,20},{18,22},{20,16},{22,18},{9,1... | collective-permute-start | bytes 393224 | tf_op jit(solution)/shard_map/ppermute | solution.py:318
  565.5 122.0 %collective-permute-start.22 = (bf16[256,1536]{1,0:T(8,128)(2,1)S(1)}, bf16[256,1536]{1,0:T(8,128)(2,1)S(1)}, u32[]{:S(2)}, u32[]{:S(2)}) collective-permute-start(bf16[256,1536]{1,0:T(8,128)(2,1)S(1)} %fusion.21), channel_id=1, source_target_pairs={{0,8},{2,10},{4,12},{6,14},{24,16},{26,18},{28,20},{30,22},{1,9},{... | collective-permute-start | bytes 2359304 | tf_op jit(solution)/shard_map/ppermute | solution.py:318
  636.6 33.5 %collective-permute-start.40 = (bf16[128,1024]{1,0:T(8,128)(2,1)S(1)}, bf16[128,1024]{1,0:T(8,128)(2,1)S(1)}, u32[]{:S(2)}, u32[]{:S(2)}) collective-permute-start(bf16[128,1024]{1,0:T(8,128)(2,1)S(1)} %pad_maximum_fusion.16), channel_id=1, source_target_pairs={{8,0},{10,2},{12,4},{14,6},{16,24},{18,26},{20,28},{22,30},{9,1},{... | collective-permute-start | bytes 786440 | tf_op jit(solution)/shard_map/ppermute | solution.py:318
  679.8 75.5 %collective-permute-start.68 = (bf16[256,2048]{1,0:T(8,128)(2,1)S(1)}, bf16[256,2048]{1,0:T(8,128)(2,1)S(1)}, u32[]{:S(2)}, u32[]{:S(2)}) collective-permute-start(bf16[256,2048]{1,0:T(8,128)(2,1)S(1)} %pad_maximum_fusion.10), channel_id=1, source_target_pairs={{8,0},{10,2},{12,4},{14,6},{16,24},{18,26},{20,28},{22,30},{9,1},{... | collective-permute-start | bytes 3145736 | tf_op jit(solution)/shard_map/ppermute | solution.py:318
  687.4 42.8 %collective-permute-start.82 = (bf16[512,1024]{1,0:T(8,128)(2,1)S(1)}, bf16[512,1024]{1,0:T(8,128)(2,1)S(1)}, u32[]{:S(2)}, u32[]{:S(2)}) collective-permute-start(bf16[512,1024]{1,0:T(8,128)(2,1)S(1)} %pad_maximum_fusion.12), channel_id=1, source_target_pairs={{8,0},{10,2},{12,4},{14,6},{16,24},{18,26},{20,28},{22,30},{9,1},{... | collective-permute-start | bytes 3145736 | tf_op jit(solution)/shard_map/ppermute | solution.py:318
  695.3 57.4 %collective-permute-start.75 = (bf16[512,1024]{1,0:T(8,128)(2,1)S(1)}, bf16[512,1024]{1,0:T(8,128)(2,1)S(1)}, u32[]{:S(2)}, u32[]{:S(2)}) collective-permute-start(bf16[512,1024]{1,0:T(8,128)(2,1)S(1)} %pad_maximum_fusion.11), channel_id=1, source_target_pairs={{8,0},{10,2},{12,4},{14,6},{16,24},{18,26},{20,28},{22,30},{9,1},{... | collective-permute-start | bytes 3145736 | tf_op jit(solution)/shard_map/ppermute | solution.py:318
  696.9 70.1 %collective-permute-start.61 = (bf16[256,2048]{1,0:T(8,128)(2,1)S(1)}, bf16[256,2048]{1,0:T(8,128)(2,1)S(1)}, u32[]{:S(2)}, u32[]{:S(2)}) collective-permute-start(bf16[256,2048]{1,0:T(8,128)(2,1)S(1)} %pad_maximum_fusion.9), channel_id=1, source_target_pairs={{8,0},{10,2},{12,4},{14,6},{16,24},{18,26},{20,28},{22,30},{9,1},{... | collective-permute-start | bytes 3145736 | tf_op jit(solution)/shard_map/ppermute | solution.py:318
  730.2 38.1 %collective-permute-start.23 = (bf16[128,1536]{1,0:T(8,128)(2,1)S(1)}, bf16[128,1536]{1,0:T(8,128)(2,1)S(1)}, u32[]{:S(2)}, u32[]{:S(2)}) collective-permute-start(bf16[128,1536]{1,0:T(8,128)(2,1)S(1)} %broadcast_select_fusion.42), channel_id=1, source_target_pairs={{8,16},{10,18},{12,20},{14,22},{16,8},{18,10},{20,12},{22,14},{9,1... | collective-permute-start | bytes 1179656 | tf_op jit(solution)/shard_map/ppermute | solution.py:318
  753.8 22.1 %collective-permute-start.55 = (bf16[256,2048]{1,0:T(8,128)(2,1)S(1)}, bf16[256,2048]{1,0:T(8,128)(2,1)S(1)}, u32[]{:S(2)}, u32[]{:S(2)}) collective-permute-start(bf16[256,2048]{1,0:T(8,128)(2,1)S(1)} %broadcast_select_fusion.12), channel_id=1, source_target_pairs={{0,4},{2,6},{4,0},{6,2},{8,12},{10,14},{12,8},{14,10},{16,20},{18,... | collective-permute-start | bytes 3145736 | tf_op jit(solution)/shard_map/ppermute | solution.py:318
  766.9 31.4 %collective-permute-start.69 = (bf16[256,2048]{1,0:T(8,128)(2,1)S(1)}, bf16[256,2048]{1,0:T(8,128)(2,1)S(1)}, u32[]{:S(2)}, u32[]{:S(2)}) collective-permute-start(bf16[256,2048]{1,0:T(8,128)(2,1)S(1)} %broadcast_select_fusion.10), channel_id=1, source_target_pairs={{0,4},{2,6},{4,0},{6,2},{8,12},{10,14},{12,8},{14,10},{16,20},{18,... | collective-permute-start | bytes 3145736 | tf_op jit(solution)/shard_map/ppermute | solution.py:318
  768.3 34.8 %collective-permute-start.62 = (bf16[256,2048]{1,0:T(8,128)(2,1)S(1)}, bf16[256,2048]{1,0:T(8,128)(2,1)S(1)}, u32[]{:S(2)}, u32[]{:S(2)}) collective-permute-start(bf16[256,2048]{1,0:T(8,128)(2,1)S(1)} %broadcast_select_fusion.11), channel_id=1, source_target_pairs={{0,2},{2,0},{4,6},{6,4},{8,10},{10,8},{12,14},{14,12},{16,18},{18,... | collective-permute-start | bytes 3145736 | tf_op jit(solution)/shard_map/ppermute | solution.py:318
  771.5 42.0 %collective-permute-start.83 = (bf16[512,1024]{1,0:T(8,128)(2,1)S(1)}, bf16[512,1024]{1,0:T(8,128)(2,1)S(1)}, u32[]{:S(2)}, u32[]{:S(2)}) collective-permute-start(bf16[512,1024]{1,0:T(8,128)(2,1)S(1)} %broadcast_select_fusion.2), channel_id=1, source_target_pairs={{0,4},{2,6},{4,0},{6,2},{8,12},{10,14},{12,8},{14,10},{16,20},{18,... | collective-permute-start | bytes 3145736 | tf_op jit(solution)/shard_map/ppermute | solution.py:318
  775.9 44.6 %collective-permute-start.76 = (bf16[512,1024]{1,0:T(8,128)(2,1)S(1)}, bf16[512,1024]{1,0:T(8,128)(2,1)S(1)}, u32[]{:S(2)}, u32[]{:S(2)}) collective-permute-start(bf16[512,1024]{1,0:T(8,128)(2,1)S(1)} %broadcast_select_fusion.3), channel_id=1, source_target_pairs={{0,2},{2,0},{4,6},{6,4},{8,10},{10,8},{12,14},{14,12},{16,18},{18,... | collective-permute-start | bytes 3145736 | tf_op jit(solution)/shard_map/ppermute | solution.py:318
  777.1 40.6 %collective-permute-start.25 = (bf16[128,1536]{1,0:T(8,128)(2,1)S(1)}, bf16[128,1536]{1,0:T(8,128)(2,1)S(1)}, u32[]{:S(2)}, u32[]{:S(2)}) collective-permute-start(bf16[128,1536]{1,0:T(8,128)(2,1)S(1)} %add_convert_fusion.24), channel_id=1, source_target_pairs={{8,16},{10,18},{12,20},{14,22},{16,8},{18,10},{20,12},{22,14},{9,1... | collective-permute-start | bytes 1179656 | tf_op jit(solution)/shard_map/ppermute | solution.py:318
  817.8 35.1 %collective-permute-start.26 = (bf16[256,1536]{1,0:T(8,128)(2,1)S(1)}, bf16[256,1536]{1,0:T(8,128)(2,1)S(1)}, u32[]{:S(2)}, u32[]{:S(2)}) collective-permute-start(bf16[256,1536]{1,0:T(8,128)(2,1)S(1)} %pad_maximum_fusion.14), channel_id=1, source_target_pairs={{8,0},{10,2},{12,4},{14,6},{16,24},{18,26},{20,28},{22,30},{9,1},{... | collective-permute-start | bytes 2359304 | tf_op jit(solution)/shard_map/ppermute | solution.py:318
  819.2 42.1 %collective-permute-start.19 = (bf16[256,1536]{1,0:T(8,128)(2,1)S(1)}, bf16[256,1536]{1,0:T(8,128)(2,1)S(1)}, u32[]{:S(2)}, u32[]{:S(2)}) collective-permute-start(bf16[256,1536]{1,0:T(8,128)(2,1)S(1)} %pad_maximum_fusion.13), channel_id=1, source_target_pairs={{8,0},{10,2},{12,4},{14,6},{16,24},{18,26},{20,28},{22,30},{9,1},{... | collective-permute-start | bytes 2359304 | tf_op jit(solution)/shard_map/ppermute | solution.py:318
  (113 other events, 1187.9 us)

commit v2 on v1

--- a/solution.py
+++ b/solution.py
@@ -1,7 +1,13 @@
+import functools
+
 import jax
 import jax.numpy as jnp
 from jax import lax
+from jax.experimental import pallas as pl
+from jax.experimental.pallas import tpu as pltpu
 from jax.sharding import PartitionSpec as P
+
+MESH = pl.DeviceIdType.MESH
 
 HD = 64
 
@@ -280,6 +286,296 @@
 PLANES = 4
 
 
+class Job:
+    def __init__(self, rows, cols, chunk_rows):
+        self.rows, self.cols, self.chunk_rows = rows, cols, chunk_rows
+        self.count = rows // (2 * chunk_rows)
+
+
+def scratch_for(job):
+    half, quarter = job.chunk_rows // 2, job.chunk_rows // 4
+
+    def slots(rows):
+        return pltpu.VMEM((job.count, 2, rows, job.cols), jnp.bfloat16)
+
+    return [
+        pltpu.VMEM((job.rows, job.cols), jnp.bfloat16),
+        slots(half),
+        slots(half),
+        slots(quarter),
+        slots(quarter),
+        slots(quarter),
+        slots(half),
+        pltpu.SemaphoreType.DMA((job.count, 2, 9)),
+        pltpu.SemaphoreType.DMA((job.count, 2, 9)),
+        pltpu.SemaphoreType.DMA((job.count,)),
+        pltpu.SemaphoreType.DMA((job.count, 2, 3)),
+    ]
+
+
+OUTER, INWARD, ACROSS, CROSS, BACK, OUT_A, OUT_B, GATHER_A, GATHER_B = range(9)
+
+
+class Links:
+    def __init__(self):
+        position = lax.axis_index("wide")
+        self.x = lax.rem(position, 2)
+        self.y = lax.rem(position // 2, 2)
+        self.z = position // 4
+        self.middle = jnp.logical_and(self.z >= 1, self.z <= 2)
+        self.edge = jnp.logical_or(self.z == 0, self.z == PLANES - 1)
+        self.upper = self.z // 2
+        self.across = self.at(self.x, self.y, 3 - self.z)
+        step = 1 - 2 * self.upper
+        self.inward = self.at(self.x, self.y, lax.rem(self.z + step + PLANES, PLANES))
+        self.outward = self.at(self.x, self.y, lax.rem(self.z - step + PLANES, PLANES))
+        self.flips = [self.at(1 - self.x, self.y, self.z), self.at(self.x, 1 - self.y, self.z)]
+        self.bits = [self.x, self.y]
+
+    def at(self, x, y, z):
+        return z * 4 + y * 2 + x
+
+    def greet(self):
+        barrier = pltpu.get_barrier_semaphore()
+
+        def signal(target):
+            pl.semaphore_signal(barrier, inc=1, device_id={"wide": target}, device_id_type=MESH)
+
+        for target in self.flips:
+            signal(target)
+
+        @pl.when(self.edge)
+        def _():
+            signal(self.inward)
+            pl.semaphore_wait(barrier, 3)
+
+        @pl.when(self.middle)
+        def _():
+            signal(self.across)
+            signal(self.outward)
+            pl.semaphore_wait(barrier, 4)
+
+
+def add_rows(held, start, other, rows):
+    held[pl.ds(start, rows), :] = (
+        held[pl.ds(start, rows), :].astype(jnp.float32) + other[...].astype(jnp.float32)
+    ).astype(jnp.bfloat16)
+
+
+class Chunk:
+    STEPS = 8
+
+    def __init__(self, links, job, refs, output, index, colour):
+        self.links, self.colour, self.index, self.output = links, colour, index, output
+        self.held = refs[0]
+        self.pair_in, self.column_in, self.across_in, self.cross_in, self.back_in, self.gather_in = [
+            ref.at[index, colour] for ref in refs[1:7]
+        ]
+        self.sent, self.got, self.loaded, self.stored = refs[7:11]
+        self.half, self.quarter = job.chunk_rows // 2, job.chunk_rows // 4
+        self.base = (2 * index + colour) * job.chunk_rows
+        bit = links.bits[colour]
+        self.keep = pl.multiple_of(self.base + bit * self.half, self.quarter)
+        self.away = pl.multiple_of(self.base + (1 - bit) * self.half, self.quarter)
+        self.near = pl.multiple_of(links.upper * self.quarter, self.quarter)
+        self.far = pl.multiple_of((1 - links.upper) * self.quarter, self.quarter)
+        self.kept = pl.multiple_of(self.keep + self.near, self.quarter)
+        self.given = pl.multiple_of(self.keep + self.far, self.quarter)
+        self.outer_peer = links.flips[colour]
+        self.inner_peer = links.flips[1 - colour]
+
+    def rows(self, start, size):
+        return self.held.at[pl.ds(start, size), :]
+
+    def part(self, ref, start):
+        return ref.at[pl.ds(start, self.quarter), :]
+
+    def copy(self, step, source, target, peer):
+        return pltpu.make_async_remote_copy(
+            src_ref=source,
+            dst_ref=target,
+            send_sem=self.sent.at[self.index, self.colour, step],
+            recv_sem=self.got.at[self.index, self.colour, step],
+            device_id={"wide": peer},
+            device_id_type=MESH,
+        )
+
+    def outer(self):
+        return self.copy(OUTER, self.rows(self.away, self.half), self.pair_in, self.outer_peer)
+
+    def inward(self):
+        return self.copy(INWARD, self.rows(self.keep, self.half), self.column_in, self.links.inward)
+
+    def across(self):
+        return self.copy(ACROSS, self.rows(self.given, self.quarter), self.across_in, self.links.across)
+
+    def cross(self):
+        return self.copy(CROSS, self.rows(self.kept, self.quarter), self.cross_in, self.inner_peer)
+
+    def back(self):
+        return self.copy(BACK, self.rows(self.kept, self.quarter), self.back_in, self.links.across)
+
+    def out_a(self):
+        target = self.part(self.column_in, self.near)
+        return self.copy(OUT_A, self.rows(self.kept, self.quarter), target, self.links.outward)
+
+    def out_b(self):
+        return self.copy(OUT_B, self.back_in, self.part(self.column_in, self.far), self.links.outward)
+
+    def gather_a(self, source):
+        return self.copy(GATHER_A, source, self.part(self.gather_in, self.near), self.outer_peer)
+
+    def gather_b(self, source):
+        return self.copy(GATHER_B, source, self.part(self.gather_in, self.far), self.outer_peer)
+
+    def store(self, place, source, start, size):
+        target = self.output.at[pl.ds(start, size), :]
+        return pltpu.make_async_copy(source, target, self.stored.at[self.index, self.colour, place])
+
+    def totals(self, near, far):
+        return self.store(0, near, self.kept, self.quarter), self.store(1, far, self.given, self.quarter)
+
+    def partner_total(self):
+        return self.store(2, self.gather_in, self.away, self.half)
+
+    def step(self, number):
+        links = self.links
+        near_total = self.rows(self.kept, self.quarter)
+        edge_near, edge_far = self.part(self.column_in, self.near), self.part(self.column_in, self.far)
+        if number == 0:
+            self.outer().start()
+        if number == 1:
+            self.outer().wait_recv()
+            add_rows(self.held, self.keep, self.pair_in, self.half)
+
+            @pl.when(links.edge)
+            def _():
+                self.inward().start()
+
+        if number == 2:
+
+            @pl.when(links.middle)
+            def _():
+                self.inward().wait_recv()
+                add_rows(self.held, self.keep, self.column_in, self.half)
+                self.across().start()
+
+        if number == 3:
+
+            @pl.when(links.middle)
+            def _():
+                self.across().wait_recv()
+                add_rows(self.held, self.kept, self.across_in, self.quarter)
+                self.cross().start()
+
+        if number == 4:
+
+            @pl.when(links.middle)
+            def _():
+                self.cross().wait()
+                add_rows(self.held, self.kept, self.cross_in, self.quarter)
+                self.back().start()
+                self.out_a().start()
+                self.gather_a(near_total).start()
+
+        if number == 5:
+
+            @pl.when(links.middle)
+            def _():
+                self.back().wait_recv()
+                self.out_b().start()
+                self.gather_b(self.back_in).start()
+                for store in self.totals(near_total, self.back_in):
+                    store.start()
+
+            @pl.when(links.edge)
+            def _():
+                self.out_a().wait_recv()
+                self.gather_a(edge_near).start()
+
+        if number == 6:
+
+            @pl.when(links.edge)
+            def _():
+                self.out_b().wait_recv()
+                self.gather_b(edge_far).start()
+                for store in self.totals(edge_near, edge_far):
+                    store.start()
+
+        if number == 7:
+            self.gather_a(near_total).wait_recv()
+            self.gather_b(self.back_in).wait_recv()
+            self.partner_total().start()
+
+    def close(self):
+        near_total = self.rows(self.kept, self.quarter)
+        self.outer().wait_send()
+        self.gather_a(near_total).wait_send()
+        self.gather_b(self.back_in).wait_send()
+
+        @pl.when(self.links.middle)
+        def _():
+            self.across().wait_send()
+            self.back().wait_send()
+            self.out_a().wait_send()
+            self.out_b().wait_send()
+
+        @pl.when(self.links.edge)
+        def _():
+            self.inward().wait_send()
+
+        for store in self.totals(near_total, self.back_in):
+            store.wait()
+        self.partner_total().wait()
+
+
+def sum_kernel(jobs, *refs):
+    count = len(jobs)
+    inputs, outputs, scratch = refs[:count], refs[count : 2 * count], refs[2 * count :]
+    per_job = len(scratch) // count
+    links = Links()
+    items = []
+    for number, job in enumerate(jobs):
+        own = scratch[number * per_job : (number + 1) * per_job]
+        for index in range(job.count):
+            pair = [Chunk(links, job, own, outputs[number], index, colour) for colour in range(2)]
+            span = pl.ds(2 * index * job.chunk_rows, 2 * job.chunk_rows)
+            load = pltpu.make_async_copy(inputs[number].at[span, :], own[0].at[span, :], own[9].at[index])
+            load.start()
+            items.append((pair, load))
+    links.greet()
+    for tick in range(len(items) + Chunk.STEPS - 1):
+        for place, (pair, load) in enumerate(items):
+            step = tick - place
+            if 0 <= step < Chunk.STEPS:
+                if step == 0:
+                    load.wait()
+                for chunk in pair:
+                    chunk.step(step)
+    for pair, _ in items:
+        for chunk in pair:
+            chunk.close()
+
+
+def summed_over_wide(gradients, chunk_rows, collective_id):
+    jobs = [Job(g.shape[0], g.shape[1], r) for g, r in zip(gradients, chunk_rows)]
+    scratch = []
+    for job in jobs:
+        scratch += scratch_for(job)
+    sent = sum(2 * g.size * 5 // 4 for g in gradients)
+    return pl.pallas_call(
+        functools.partial(sum_kernel, jobs),
+        out_shape=[jax.ShapeDtypeStruct(g.shape, jnp.bfloat16) for g in gradients],
+        in_specs=[pl.BlockSpec(memory_space=pl.ANY)] * len(jobs),
+        out_specs=[pl.BlockSpec(memory_space=pl.ANY)] * len(jobs),
+        scratch_shapes=scratch,
+        compiler_params=pltpu.CompilerParams(
+            collective_id=collective_id, has_side_effects=True, vmem_limit_bytes=60 * 1024 * 1024
+        ),
+        cost_estimate=pl.CostEstimate(flops=0, bytes_accessed=2 * sent, transcendentals=0),
+    )(*gradients)
+
+
 def wide_index(x, y, z):
     return z * 4 + y * 2 + x
 
@@ -309,9 +605,9 @@
     ]
 
 
-INWARD = ((0, 1), (3, 2))
-ACROSS = ((1, 2), (2, 1))
-OUTWARD = ((1, 0), (2, 3))
+INWARD_MOVES = ((0, 1), (3, 2))
+ACROSS_MOVES = ((1, 2), (2, 1))
+OUTWARD_MOVES = ((1, 0), (2, 3))
 
 
 def send(values, pairs):
@@ -320,65 +616,16 @@
 
 def partner(values):
     return lax.ppermute(values, "narrow", [(0, 1), (1, 0)])
-
-
-def add_low(left, right):
-    return (left.astype(jnp.float32) + right.astype(jnp.float32)).astype(jnp.bfloat16)
-
-
-def ordered(own, other, own_first):
-    first = jnp.where(own_first, own, other)
-    second = jnp.where(own_first, other, own)
-    return jnp.concatenate([first, second], axis=0)
-
-
-def summed_over_wide(product, rows, outer):
-    position = lax.axis_index("wide")
-    inner = "y" if outer == "x" else "x"
-    outer_bit = position % 2 if outer == "x" else position // 2 % 2
-    plane = position // 4
-    half = rows // 2
-    away = product((1 - outer_bit) * half, half).astype(jnp.bfloat16)
-    received = send(away, flip_pairs(outer))
-    pair_sum = (product(outer_bit * half, half) + received.astype(jnp.float32)).astype(jnp.bfloat16)
-    column_sum = add_low(pair_sum, send(pair_sum, plane_pairs(INWARD)))
-    quarter = half // 2
-    upper = plane >= 2
-    first, second = column_sum[:quarter], column_sum[quarter:]
-    kept = jnp.where(upper, second, first)
-    given = jnp.where(upper, first, second)
-    line_sum = add_low(kept, send(given, plane_pairs(ACROSS)))
-    total = add_low(line_sum, send(line_sum, middle_flip_pairs(inner)))
-    full = ordered(total, send(total, plane_pairs(ACROSS)), jnp.logical_not(upper))
-    outward = send(full, plane_pairs(OUTWARD))
-    is_middle = (plane == 1) | (plane == 2)
-    full = jnp.where(is_middle, full, outward)
-    return ordered(full, send(full, flip_pairs(outer)), outer_bit == 0)
-
-
-def gradient_sum(left, right):
-    rows = left.shape[1]
-
-    def half_sum(base, outer):
-        def product(start, size):
-            columns = lax.dynamic_slice_in_dim(left, base + start, size, 1)
-            return transpose_times(columns, right)
-
-        return summed_over_wide(product, rows // 2, outer)
-
-    return jnp.concatenate([half_sum(0, "x"), half_sum(rows // 2, "y")], axis=0).astype(
-        jnp.float32
-    )
 
 
 def vector_sum(values):
     values = values + partner(values)
     values = values + send(values, flip_pairs("x"))
     values = values + send(values, flip_pairs("y"))
-    values = values + send(values, plane_pairs(INWARD))
-    values = values + send(values, plane_pairs(ACROSS))
+    values = values + send(values, plane_pairs(INWARD_MOVES))
+    values = values + send(values, plane_pairs(ACROSS_MOVES))
     plane = lax.axis_index("wide") // 4
-    outward = send(values, plane_pairs(OUTWARD))
+    outward = send(values, plane_pairs(OUTWARD_MOVES))
     return jnp.where((plane == 1) | (plane == 2), values, outward)
 
 
@@ -485,7 +732,7 @@
     up_values = jnp.dot(gathered_two, w_up, preferred_element_type=jnp.float32)
     sigmoid_gate = jax.nn.sigmoid(gate_values)
     hidden_rows = (gate_values * sigmoid_gate * up_values).astype(jnp.bfloat16)
-    down_summed = gradient_sum(hidden_rows, cot_rows)
+    down_summed = transpose_times(hidden_rows, cot_rows).astype(jnp.bfloat16)
 
     out_other = jnp.dot(
         hidden_rows[block_rows:], w_down, preferred_element_type=jnp.float32
@@ -499,8 +746,8 @@
     silu_grad = sigmoid_gate * (1.0 + gate_values * (1.0 - sigmoid_gate))
     grad_gate = (grad_hidden * up_values * silu_grad).astype(jnp.bfloat16)
     grad_up = (grad_hidden * gate_values * sigmoid_gate).astype(jnp.bfloat16)
-    gate_summed = gradient_sum(gathered_two, grad_gate)
-    up_summed = gradient_sum(gathered_two, grad_up)
+    gate_summed = transpose_times(gathered_two, grad_gate).astype(jnp.bfloat16)
+    up_summed = transpose_times(gathered_two, grad_up).astype(jnp.bfloat16)
 
     def grad_two_share(rows):
         return times_transpose(grad_gate[rows], w_gate) + times_transpose(grad_up[rows], w_up)
@@ -514,7 +761,7 @@
     grad_attention = grad_resid.astype(jnp.bfloat16)
     grad_rows = rows_of(grad_attention, partner(grad_attention))
     grad_mixed = times_transpose(grad_rows, w_out).astype(jnp.bfloat16)
-    out_summed = gradient_sum(mixed_rows, grad_rows)
+    out_summed = transpose_times(mixed_rows, grad_rows).astype(jnp.bfloat16)
     grad_mixed_heads = grad_mixed.reshape(2, block_rows, local_heads, HD)
 
     def attend_backward(index, log_total):
@@ -548,7 +795,7 @@
     grad_qkv = jnp.concatenate(
         [grad_query_raw, grad_key_raw, value_own + value_other], axis=1
     ).astype(jnp.bfloat16)
-    qkv_summed = gradient_sum(gathered_one, grad_qkv)
+    qkv_summed = transpose_times(gathered_one, grad_qkv).astype(jnp.bfloat16)
     grad_one_other = times_transpose(grad_qkv[block_rows:], joined_qkv).astype(jnp.bfloat16)
     grad_normed_one = times_transpose(grad_qkv[:block_rows], joined_qkv) + partner(
         grad_one_other
@@ -560,14 +807,31 @@
     norm_summed = vector_sum(
         jnp.stack([gain_one_grad, shift_one_grad, gain_two_grad, shift_two_grad])
     )
+    width = local_width
+    down_summed, gate_summed, up_summed, out_summed, query_summed, key_summed, value_summed = [
+        total.astype(jnp.float32)
+        for total in summed_over_wide(
+            [
+                down_summed,
+                gate_summed,
+                up_summed,
+                out_summed,
+                qkv_summed[:, :width],
+                qkv_summed[:, width : 2 * width],
+                qkv_summed[:, 2 * width :],
+            ],
+            [128, 64, 64, 128, 128, 128, 128],
+            1,
+        )
+    ]
     return (
         out_values,
         token_grad,
         norm_summed[0],
         norm_summed[1],
-        qkv_summed[:, :local_width],
-        qkv_summed[:, local_width : 2 * local_width],
-        qkv_summed[:, 2 * local_width :],
+        query_summed,
+        key_summed,
+        value_summed,
         out_summed,
         norm_summed[2],
         norm_summed[3],

time: 885 us -> 629 us (0.71)
  waiting for transfers between devices: 331 us -> 8.28 us
  Pallas kernels: 0 us -> 268 us
  starting transfers between devices: 205 us -> 11.1 us
    ppermute x75 -> x5, waiting for transfers between devices: 330 us -> 8.26 us  [send(): return lax.ppermute(values, 'wide', pairs)]
    pallas_call x0 -> x1, Pallas kernels: none -> 268 us  [summed_over_wide(): pl.pallas_call(functools.partial(sum_kernel, jobs), out_shape=[jax.ShapeD...]
    ppermute x75 -> x5, starting transfers between devices: 203 us -> 7.98 us  [send(): return lax.ppermute(values, 'wide', pairs)]
    convert_element_type x35 -> x7, other arithmetic: 31.4 us -> 21.1 us  [on_device(): total.astype(jnp.float32)]
    dot_general x20 -> x5, matrix products: 26 us -> 27.2 us  [transpose_times(): lax.dot_general(left, right, (((0,), (0,)), ((), ())), preferred_element_...]
  transfers between devices with their start and end apart: 84 -> 14, of which waited for: 28 -> 2; matrix products, arithmetic and copies ran while one was open for 33% -> 45% of each run, Pallas kernels for 0% -> 43%
where the time goes in v2:
time: 629 us; the launch traced here: 625 us
  Pallas kernels  268 us (43%)
  matrix products  168 us (27%)
  other arithmetic  101 us (16%)
  local copies, waits for them, and re-layouts  65.7 us (10%)
  starting transfers between devices  11.1 us (2%)
  waiting for transfers between devices  8.28 us (1%)
    pallas_call x1, Pallas kernels, summed_over_wide(): pl.pallas_call(functools.partial(sum_kernel, jobs), out_shape=[jax.ShapeD...  268 us
    dot_general x8, matrix products, times_transpose(): lax.dot_general(left, right, (((1,), (1,)), ((), ())), preferred_element_...  29.1 us
    convert_element_type x2, other arithmetic, attend_backward(): grad_scores = (attention_probs * (grad_probs - centre)).astype(jnp.bfloat16)  27.8 us
    dot_general x5, matrix products, transpose_times(): lax.dot_general(left, right, (((0,), (0,)), ((), ())), preferred_element_...  27.2 us
    convert_element_type x7, other arithmetic, on_device(): total.astype(jnp.float32)  21.1 us
    dot_general x2, matrix products, attend_backward(): jnp.einsum('qhd,khd->hqk', grad_block, value_heads, preferred_element_typ...  19.3 us
    dot_general x1, matrix products, on_device(): jnp.dot(gathered_two, w_gate, preferred_element_type=jnp.float32)  16.4 us
    unnamed x182, local copies, waits for them, and re-layouts  15.4 us
  transfers between devices with their start and end apart: 14, of which 2 were waited for; matrix products, arithmetic and copies ran while one was open for 45% of the time, Pallas kernels for 43%

profile of v2, /device:TPU:0, one launch (start us, length us, event | category | flops | bytes accessed | tf_op | source)
XLA Modules:
  0.0 624.6 jit_solution(1928005296269112292)
XLA Ops:
  4.0 2.8 fusion.27
  11.0 6.0 fusion.82
  22.9 3.3 copy.51
  26.2 3.2 rev.14
  29.4 2.9 copy.52
  32.2 2.9 copy.48
  35.1 3.2 rev.13
  38.3 2.9 copy.49
  41.2 11.3 %fusion.38 = (bf16[1024,512]{1,0:T(8,128)(2,1)}, bf16[1024,512]{1,0:T(8,128)(2,1)}) fusion(f32[1024,512]{1,0:T(8,128)} %copy.52, f32[512]{0:T(512)S(1)} %get-tuple-element.74, f32[512]{0:T(512)S(1)} %get-tuple-element.73, f32[1024]{0:T(1024)S(1)} %bitcast.137, f32[1024,1536]{1,0:T(8,128)} %copy-done.11, f32[1024,512]{1,0:T(8,128)} %copy.49), kind=kLoop, calls=%fused_computation.63 | loop fusion | flops 5767168 | bytes 10493952 | tf_op jit(solution)/shard_map/convert_element_type | solution.py:688
  53.9 2.6 fusion.131
  60.7 3.5 select_reduce_fusion
  64.2 3.5 fusion.1
  70.0 4.3 fusion.83
  78.1 3.5 fusion
  83.9 5.3 fusion.84
  95.4 6.8 %fusion.135 = f32[1024,2048]{1,0:T(8,128)} fusion(bf16[1024,1024]{1,0:T(8,128)(2,1)S(1)} %constant_dynamic-update-slice_fusion.3, bf16[2048,1024]{1,0:T(8,128)(2,1)S(1)} %copy-done.66), kind=kOutput, calls=%fused_computation.204 | convolution fusion | flops 4294967296 | bytes 14680064 | tf_op jit(solution)/shard_map/dot_general | solution.py:21
  102.2 7.6 %fusion.124 = f32[1024,2048]{1,0:T(8,128)} fusion(bf16[1024,2048]{1,0:T(8,128)(2,1)S(1)} %copy-done.62, bf16[512,1024]{1,0:T(8,128)(2,1)S(1)} %collective-permute-done.2, bf16[512,1024]{1,0:T(8,128)(2,1)S(1)} %add_convert_fusion.1), kind=kOutput, calls=%fused_computation.194 | convolution fusion | flops 4299161600 | bytes 14680064 | tf_op jit(solution)/shard_map/dot_general | solution.py:732
  109.9 16.4 %multiply_convert_fusion.3 = (bf16[1024,2048]{1,0:T(8,128)(2,1)}, bf16[1024,2048]{1,0:T(8,128)(2,1)}, bf16[1024,2048]{1,0:T(8,128)(2,1)}) fusion(f32[1024,2048]{1,0:T(8,128)} %fusion.135, f32[1024,2048]{1,0:T(8,128)} %fusion.124, bf16[1024,2048]{1,0:T(8,128)(2,1)} %param.26, bf16[512,1024]{1,0:T(8,128)(2,1)S(1)} %collective-permute-done.2, ...), kind=kOutput, calls=%fused_computation.22 | convolution fusion | flops 4332716032 | bytes 35651584 | tf_op jit(solution)/shard_map/dot_general | solution.py:731
  126.3 4.1 fusion.47
  130.5 3.7 fusion.73
  135.9 6.3 %fusion.79 = bf16[512,1024]{1,0:T(8,128)(2,1)} fusion(bf16[2048,1024]{1,0:T(8,128)(2,1)} %param.28, bf16[1024,2048]{1,0:T(8,128)(2,1)} %get-tuple-element.40), kind=kOutput, calls=%fused_computation.114 | convolution fusion | flops 2148007936 | bytes 7340032 | tf_op jit(solution)/shard_map/dot_general | solution.py:737
  145.6 5.3 multiply_reduce_fusion.2
  150.9 3.5 fusion.126
  154.5 6.5 %convolution_convert_fusion.1.refs_2_ = bf16[1024,2048]{1,0:T(8,128)(2,1)} fusion(bf16[1024,2048]{1,0:T(8,128)(2,1)S(1)} %copy-done.79, bf16[512,1024]{1,0:T(8,128)(2,1)S(1)} %copy-done.69, bf16[512,1024]{1,0:T(8,128)(2,1)S(1)} %copy-done.36), kind=kOutput, calls=%fused_computation.32 | convolution fusion | flops 4301258752 | bytes 10485760 | tf_op jit(solution)/shard_map/dot_general | solution.py:27
  161.1 6.2 convolution_convert_fusion.3.refs_0_
  170.4 9.5 %multiply_reduce_fusion.1 = (f32[8,512]{1,0:T(8,128)}, f32[8,512,1024]{2,1,0:T(8,128)}) fusion(f32[8,512,1024]{2,1,0:T(8,128)S(1)} %bitcast.103, f32[8,512]{1,0:T(8,128)} %log_add_fusion.1, pred[1024]{0:T(1024)(128)(4,1)S(1)} %get-tuple-element.37, bf16[512,8,64]{0,2,1:T(8,128)(2,1)S(1)} %bitcast.128, bf16[1024,8,64]{0,2,1:T(8,128)(2,1)S(1)} %bitcast.112), kind=kOutput, calls=%fused_computation.5 | convolution fusion | flops 553644032 | bytes 35161088 | tf_op jit(solution)/shard_map/qhd,khd->hqk/dot_general | solution.py:771
  179.9 15.9 %multiply_convert_fusion.1 = bf16[8,512,1024]{2,1,0:T(8,128)(2,1)} fusion(f32[8,512,1024]{2,1,0:T(8,128)} %get-tuple-element.71, f32[8,512,1024]{2,1,0:T(8,128)} %copy-done.4, f32[8,512]{1,0:T(8,128)} %get-tuple-element.70, f32[8,512]{1,0:T(8,128)} %log_add_fusion.1, pred[1024]{0:T(1024)(128)(4,1)S(1)} %get-tuple-element.37), kind=kLoop, calls=%fused_computation.4 | loop fusion | flops 20971520 | bytes 41976832 | tf_op jit(solution)/shard_map/convert_element_type | solution.py:775
  195.8 7.9 %fusion.136 = f32[8,64,512]{2,1,0:T(8,128)} fusion(bf16[1024,8,64]{0,2,1:T(8,128)(2,1)S(1)} %bitcast.106, bf16[8,512,1024]{2,1,0:T(8,128)(2,1)} %multiply_convert_fusion.1), kind=kOutput, calls=%fused_computation.205 | convolution fusion | flops 536870912 | bytes 10485760 | tf_op jit(solution)/shard_map/hqk,khd->qhd/dot_general | solution.py:776
  203.7 6.3 %fusion.138 = f32[8,64,1024]{2,1,0:T(8,128)} fusion(bf16[512,8,64]{0,2,1:T(8,128)(2,1)S(1)} %bitcast.127, bf16[8,512,1024]{2,1,0:T(8,128)(2,1)} %multiply_convert_fusion.1), kind=kOutput, calls=%fused_computation.207 | convolution fusion | flops 536870912 | bytes 11010048 | tf_op jit(solution)/shard_map/hqk,qhd->khd/dot_general | solution.py:779
  210.0 4.6 fusion.4
  214.7 9.8 %multiply_reduce_fusion = (f32[8,512]{1,0:T(8,128)}, f32[8,512,1024]{2,1,0:T(8,128)}) fusion(f32[8,512,1024]{2,1,0:T(8,128)S(1)} %bitcast.101, f32[8,512]{1,0:T(8,128)S(1)} %log_add_fusion, pred[1024]{0:T(1024)(128)(4,1)S(1)} %fusion.103, bf16[512,8,64]{0,2,1:T(8,128)(2,1)} %bitcast.130, bf16[1024,8,64]{0,2,1:T(8,128)(2,1)S(1)} %bitcast.113), kind=kOutput, calls=%fused_computation.2 | convolution fusion | flops 553644032 | bytes 35161088 | tf_op jit(solution)/shard_map/qhd,khd->hqk/dot_general | solution.py:771
  224.5 9.3 %add_convert_fusion = bf16[8,64,1024]{2,1,0:T(8,128)(2,1)} fusion(f32[8,64,1024]{2,1,0:T(8,128)} %fusion.4, bf16[512,8,64]{0,2,1:T(8,128)(2,1)S(1)} %bitcast.129, f32[8,512,1024]{2,1,0:T(8,128)} %copy-done.4, f32[8,512]{1,0:T(8,128)} %log_add_fusion.1, pred[1024]{0:T(1024)(128)(4,1)S(1)} %get-tuple-element.37), kind=kOutput, calls=%fused_computation.93 | convolution fusion | flops 550502400 | bytes 20464640 | tf_op jit(solution)/shard_map/hqk,qhd->khd/dot_general | solution.py:782
  237.4 11.9 %multiply_convert_fusion = bf16[8,512,1024]{2,1,0:T(8,128)(2,1)S(1)} fusion(f32[8,512,1024]{2,1,0:T(8,128)} %get-tuple-element.69, f32[8,512,1024]{2,1,0:T(8,128)} %copy-done.3, f32[8,512]{1,0:T(8,128)S(1)} %copy-done.46, f32[8,512]{1,0:T(8,128)S(1)} %log_add_fusion, pred[1024]{0:T(1024)(128)(4,1)S(1)} %fusion.103), kind=kLoop, calls=%fused_computation.1 | loop fusion | flops 20971520 | bytes 41976832 | tf_op jit(solution)/shard_map/convert_element_type | solution.py:775
  249.3 3.6 fusion.137
  254.6 2.6 copy.56
  259.0 9.5 %fusion.59 = (f32[1024,8,2,32]{0,3,2,1:T(8,128)}, f32[1024,8,2,32]{0,3,2,1:T(8,128)}) fusion(f32[512,8,2,32]{0,3,2,1:T(8,128)} %bitcast.117, f32[512,8,2,32]{0,3,2,1:T(8,128)S(1)} %bitcast.115, f32[8,2,32]{2,1,0:T(2,128)S(1)} %copy-done.51, f32[8,2,32]{2,1,0:T(2,128)S(1)} %copy-done.52, f32[1024]{0:T(1024)S(1)} %bitcast.138, f32[1024,8,2,32]{0,3,2,1:T(8,128)S(1)} %bitcast.109), kind=kLoop, calls=%fused_computation.90 | loop fusion | flops 3145728 | bytes 8396800 | tf_op jit(solution)/shard_map/mul | solution.py:77
  275.6 9.9 %fusion.40 = (bf16[1024,512]{1,0:T(8,128)(2,1)S(1)}, bf16[1024,512]{1,0:T(8,128)(2,1)S(1)}) fusion(f32[1024,512]{1,0:T(8,128)} %copy.57, f32[512,512]{1,0:T(8,128)} %copy.56, f32[512,512]{1,0:T(8,128)} %copy.55, f32[512]{0:T(512)S(1)} %copy-done.56, f32[1024]{0:T(1024)S(1)} %bitcast.139, f32[1024,512]{1,0:T(8,128)} %copy.59, f32[1024,512]{1,0:T(8,128)} %copy.58), kind=kLoop, calls=%fused_computation.65 | loop fusion | flops 4718592 | bytes 10491904 | tf_op jit(solution)/shard_map/convert
  290.2 6.4 %convolution_convert_fusion.2.refs_1_ = bf16[1024,2048]{1,0:T(8,128)(2,1)} fusion(bf16[1024,2048]{1,0:T(8,128)(2,1)S(1)} %copy-done.78, bf16[512,1024]{1,0:T(8,128)(2,1)S(1)} %copy-done.70, bf16[512,1024]{1,0:T(8,128)(2,1)S(1)} %copy-done.37), kind=kOutput, calls=%fused_computation.33 | convolution fusion | flops 4301258752 | bytes 10485760 | tf_op jit(solution)/shard_map/dot_general | solution.py:27
  296.8 5.0 convert_add_fusion.2
  301.8 3.6 fusion.32
  306.0 5.7 convolution_convert_fusion
  311.8 2.6 collective-permute-start.9
  320.6 268.0 %shard_map.246 = (bf16[2048,1024]{1,0:T(8,128)(2,1)}, bf16[1024,2048]{1,0:T(8,128)(2,1)}, bf16[1024,2048]{1,0:T(8,128)(2,1)}, bf16[512,1024]{1,0:T(8,128)(2,1)},...) custom-call(bf16[2048,1024]{1,0:T(8,128)(2,1)} %convolution_convert_fusion.3.refs_0_, ...), custom_call_target="tpu_custom_call" | custom-call | bytes 41943040 | tf_op jit(solution)/shard_map/pallas_call | solution.py:566
  588.6 3.0 convert_element_type.179
  596.5 4.4 convert_element_type.183
  601.0 4.4 convert_element_type.184
  605.4 4.4 convert_element_type.185
  616.7 6.8 %collective-permute-done.13 = f32[4,1024]{1,0:T(4,128)S(1)} collective-permute-done((f32[4,1024]{1,0:T(4,128)S(1)}, f32[4,1024]{1,0:T(4,128)S(1)}, u32[]{:S(2)}, u32[]{:S(2)}) %collective-permute-start.13) | collective-permute-done | bytes 16416 | tf_op jit(solution)/shard_map/ppermute | solution.py:614
  (271 shorter events, 79.3 us)
Async XLA Ops:
  0.6 73.7 %copy-start = (bf16[512,1024]{1,0:T(8,128)(2,1)S(1)}, bf16[512,1024]{1,0:T(8,128)(2,1)}, u32[]{:S(2)}) copy-start(bf16[512,1024]{1,0:T(8,128)(2,1)} %param.23) | copy-start | bytes 3145732
  0.7 6.6 %copy-start.73 = (s32[2]{0:T(128)S(1)}, s32[2]{0:T(128)}, u32[]{:S(2)}) copy-start(s32[2]{0:T(128)} %param.16) | copy-start | bytes 28
  0.7 6.7 %copy-start.2 = (s32[2]{0:T(128)S(1)}, s32[2]{0:T(128)}, u32[]{:S(2)}) copy-start(s32[2]{0:T(128)} %param.17) | copy-start | bytes 28
  2.2 8.5 %copy-start.32 = (bf16[1024,512]{1,0:T(8,128)(2,1)S(1)}, bf16[1024,512]{1,0:T(8,128)(2,1)}, u32[]{:S(2)}) copy-start(bf16[1024,512]{1,0:T(8,128)(2,1)} %param.20) | copy-start | bytes 3145732
  4.0 6.8 %copy-start.33 = (bf16[1024,512]{1,0:T(8,128)(2,1)S(1)}, bf16[1024,512]{1,0:T(8,128)(2,1)}, u32[]{:S(2)}) copy-start(bf16[1024,512]{1,0:T(8,128)(2,1)} %param.21) | copy-start | bytes 3145732
  6.8 4.2 collective-permute-start
  7.3 85.2 %collective-permute-start.4 = (bf16[512,1024]{1,0:T(8,128)(2,1)}, bf16[512,1024]{1,0:T(8,128)(2,1)}, u32[]{:S(2)}, u32[]{:S(2)}) collective-permute-start(bf16[512,1024]{1,0:T(8,128)(2,1)} %param.29), channel_id=1, source_target_pairs={{0,1},{1,0},{2,3},{3,2},{4,5},{5,4},{6,7},{7,6},{8,9},{9,8},{10,11... | collective-permute-start | bytes 3145736 | tf_op jit(solution)/shard_map/ppermute | solution.py:618
  8.3 32.9 %copy-start.55 = (f32[512]{0:T(512)}, f32[512]{0:T(512)S(1)}, u32[]{:S(2)}) copy-start(f32[512]{0:T(512)S(1)} %get-tuple-element.73) | copy-start | bytes 6148
  8.3 32.9 %copy-start.47 = (f32[1,4,2,128]{3,1,2,0:T(4,128)}, f32[1,4,2,128]{3,1,2,0:T(4,128)S(1)}, u32[]{:S(2)}) copy-start(f32[1,4,2,128]{3,1,2,0:T(4,128)S(1)} %copy.62) | copy-start | bytes 12292
  22.9 58.7 %copy-start.13 = (bf16[1024,512]{0,1:T(8,128)(2,1)}, bf16[1024,512]{0,1:T(8,128)(2,1)S(1)}, u32[]{:S(2)}) copy-start(bf16[1024,512]{0,1:T(8,128)(2,1)S(1)} %copy.47) | copy-start | bytes 3145732
  53.9 21.7 %copy-start.9 = (bf16[1024,512]{0,1:T(8,128)(2,1)}, bf16[1024,512]{0,1:T(8,128)(2,1)S(1)}, u32[]{:S(2)}) copy-start(bf16[1024,512]{0,1:T(8,128)(2,1)S(1)} %copy.53) | copy-start | bytes 3145732
  75.1 14.1 %collective-permute-start.1 = (f32[512,1024]{1,0:T(8,128)S(1)}, f32[512,1024]{1,0:T(8,128)S(1)}, u32[]{:S(2)}, u32[]{:S(2)}) collective-permute-start(f32[512,1024]{1,0:T(8,128)S(1)} %fusion.134), channel_id=1, source_target_pairs={{0,1},{1,0},{2,3},{3,2},{4,5},{5,4},{6,7},{7,6},{8,9},{9,8},{10,11... | collective-permute-start | bytes 6291464 | tf_op jit(solution)/shard_map/ppermute | solution.py:618
  91.1 59.8 %copy-start.5 = (f32[512,1024]{1,0:T(8,128)}, f32[512,1024]{1,0:T(8,128)S(1)}, u32[]{:S(2)}) copy-start(f32[512,1024]{1,0:T(8,128)S(1)} %get-tuple-element.66) | copy-start | bytes 6291460
  91.9 17.9 %copy-start.35 = (bf16[512,1024]{1,0:T(8,128)(2,1)}, bf16[512,1024]{1,0:T(8,128)(2,1)S(1)}, u32[]{:S(2)}) copy-start(bf16[512,1024]{1,0:T(8,128)(2,1)S(1)} %add_convert_fusion.1) | copy-start | bytes 3145732
  91.9 10.3 %collective-permute-start.2 = (bf16[512,1024]{1,0:T(8,128)(2,1)S(1)}, bf16[512,1024]{1,0:T(8,128)(2,1)S(1)}, u32[]{:S(2)}, u32[]{:S(2)}) collective-permute-start(bf16[512,1024]{1,0:T(8,128)(2,1)S(1)} %add_convert_fusion.1), channel_id=1, source_target_pairs={{0,1},{1,0},{2,3},{3,2},{4,5},{5,4},{6,7},{7,6},{8,9},{9,8},{10,11... | collective-permute-start | bytes 3145736 | tf_op jit(solution)/shard_map/ppermute | solution.py:618
  95.4 6.8 %copy-start.42 = (bf16[1024,1024]{1,0:T(8,128)(2,1)}, bf16[1024,1024]{1,0:T(8,128)(2,1)S(1)}, u32[]{:S(2)}) copy-start(bf16[1024,1024]{1,0:T(8,128)(2,1)S(1)} %constant_dynamic-update-slice_fusion.3) | copy-start | bytes 6291460
  95.4 6.8 %copy-start.62 = (bf16[1024,2048]{1,0:T(8,128)(2,1)S(1)}, bf16[1024,2048]{1,0:T(8,128)(2,1)}, u32[]{:S(2)}) copy-start(bf16[1024,2048]{1,0:T(8,128)(2,1)} %param.27) | copy-start | bytes 12582916
  102.2 7.6 %copy-start.68 = (bf16[512,1024]{1,0:T(8,128)(2,1)}, bf16[512,1024]{1,0:T(8,128)(2,1)S(1)}, u32[]{:S(2)}) copy-start(bf16[512,1024]{1,0:T(8,128)(2,1)S(1)} %collective-permute-done.2) | copy-start | bytes 3145732
  134.2 10.5 %collective-permute-start.5 = (f32[512,1024]{1,0:T(8,128)}, f32[512,1024]{1,0:T(8,128)}, u32[]{:S(2)}, u32[]{:S(2)}) collective-permute-start(f32[512,1024]{1,0:T(8,128)} %fusion.73), channel_id=1, source_target_pairs={{0,1},{1,0},{2,3},{3,2},{4,5},{5,4},{6,7},{7,6},{8,9},{9,8},{10,11... | collective-permute-start | bytes 6291464 | tf_op jit(solution)/shard_map/ppermute | solution.py:618
  142.1 154.6 %collective-permute-start.3 = (bf16[512,1024]{1,0:T(8,128)(2,1)}, bf16[512,1024]{1,0:T(8,128)(2,1)}, u32[]{:S(2)}, u32[]{:S(2)}) collective-permute-start(bf16[512,1024]{1,0:T(8,128)(2,1)} %fusion.79), channel_id=1, source_target_pairs={{0,1},{1,0},{2,3},{3,2},{4,5},{5,4},{6,7},{7,6},{8,9},{9,8},{10,11... | collective-permute-start | bytes 3145736 | tf_op jit(solution)/shard_map/ppermute | solution.py:618
  154.4 12.9 %copy-start.27 = (bf16[512,1024]{1,0:T(8,128)(2,1)}, bf16[512,1024]{1,0:T(8,128)(2,1)S(1)}, u32[]{:S(2)}) copy-start(bf16[512,1024]{1,0:T(8,128)(2,1)S(1)} %get-tuple-element.35) | copy-start | bytes 3145732
  154.4 6.6 %copy-start.43 = (bf16[1024,1024]{1,0:T(8,128)(2,1)S(1)}, bf16[1024,1024]{1,0:T(8,128)(2,1)}, u32[]{:S(2)}) copy-start(bf16[1024,1024]{1,0:T(8,128)(2,1)} %copy-done.42) | copy-start | bytes 6291460
  154.4 6.6 %copy-start.74 = (bf16[1024,2048]{1,0:T(8,128)(2,1)S(1)}, bf16[1024,2048]{1,0:T(8,128)(2,1)}, u32[]{:S(2)}) copy-start(bf16[1024,2048]{1,0:T(8,128)(2,1)} %get-tuple-element.40) | copy-start | bytes 12582916
  154.4 12.9 %collective-permute-start.6 = (bf16[512,1024]{1,0:T(8,128)(2,1)S(1)}, bf16[512,1024]{1,0:T(8,128)(2,1)S(1)}, u32[]{:S(2)}, u32[]{:S(2)}) collective-permute-start(bf16[512,1024]{1,0:T(8,128)(2,1)S(1)} %get-tuple-element.35), channel_id=1, source_target_pairs={{0,1},{1,0},{2,3},{3,2},{4,5},{5,4},{6,7},{7,6},{8,9},{9,8},{10,11... | collective-permute-start | bytes 3145736 | tf_op jit(solution)/shard_map/ppermute | solution.py:618
  161.1 8.5 %slice-start.4 = ((s8[16777216]{0:T(1024)(128)(4,1)}), s8[4194304]{0:T(1024)(128)(4,1)S(1)}, s32[]{:S(2)}) async-start(s8[16777216]{0:T(1024)(128)(4,1)} %bitcast.102), calls=%async_computation.4 | async-start | bytes 8388608
  161.1 8.5 %slice-start.5 = ((s8[16777216]{0:T(1024)(128)(4,1)}), s8[4194304]{0:T(1024)(128)(4,1)S(1)}, s32[]{:S(2)}) async-start(s8[16777216]{0:T(1024)(128)(4,1)} %bitcast.102), calls=%async_computation.5 | async-start | bytes 8388608
  161.1 8.5 %slice-start.6 = ((s8[16777216]{0:T(1024)(128)(4,1)}), s8[4194304]{0:T(1024)(128)(4,1)S(1)}, s32[]{:S(2)}) async-start(s8[16777216]{0:T(1024)(128)(4,1)} %bitcast.102), calls=%async_computation.6 | async-start | bytes 8388608
  179.9 15.9 %copy-start.10 = (bf16[1024,512]{0,1:T(8,128)(2,1)S(1)}, bf16[1024,512]{0,1:T(8,128)(2,1)}, u32[]{:S(2)}) copy-start(bf16[1024,512]{0,1:T(8,128)(2,1)} %copy-done.9) | copy-start | bytes 3145732
  179.9 30.1 %slice-start = ((s8[16777216]{0:T(1024)(128)(4,1)}), s8[4194304]{0:T(1024)(128)(4,1)S(1)}, s32[]{:S(2)}) async-start(s8[16777216]{0:T(1024)(128)(4,1)} %bitcast.100), calls=%async_computation | async-start | bytes 8388608
  179.9 30.1 %slice-start.1 = ((s8[16777216]{0:T(1024)(128)(4,1)}), s8[4194304]{0:T(1024)(128)(4,1)S(1)}, s32[]{:S(2)}) async-start(s8[16777216]{0:T(1024)(128)(4,1)} %bitcast.100), calls=%async_computation.1 | async-start | bytes 8388608
  179.9 30.1 %slice-start.2 = ((s8[16777216]{0:T(1024)(128)(4,1)}), s8[4194304]{0:T(1024)(128)(4,1)S(1)}, s32[]{:S(2)}) async-start(s8[16777216]{0:T(1024)(128)(4,1)} %bitcast.100), calls=%async_computation.2 | async-start | bytes 8388608
  195.8 7.9 %copy-start.20 = (bf16[512,512]{0,1:T(8,128)(2,1)S(1)}, bf16[512,512]{0,1:T(8,128)(2,1)}, u32[]{:S(2)}) copy-start(bf16[512,512]{0,1:T(8,128)(2,1)} %copy.50) | copy-start | bytes 1572868
  195.8 14.2 %slice-start.3 = ((s8[16777216]{0:T(1024)(128)(4,1)}), s8[4194304]{0:T(1024)(128)(4,1)S(1)}, s32[]{:S(2)}) async-start(s8[16777216]{0:T(1024)(128)(4,1)} %bitcast.100), calls=%async_computation.3 | async-start | bytes 8388608
  224.5 11.6 %copy-start.15 = (f32[8,64,512]{2,1,0:T(8,128)S(1)}, f32[8,64,512]{2,1,0:T(8,128)}, u32[]{:S(2)}) copy-start(f32[8,64,512]{2,1,0:T(8,128)} %fusion.136) | copy-start | bytes 3145732
  275.6 9.9 %copy-start.25 = (bf16[1024,512]{1,0:T(8,128)(2,1)S(1)}, bf16[1024,512]{1,0:T(8,128)(2,1)}, u32[]{:S(2)}) copy-start(bf16[1024,512]{1,0:T(8,128)(2,1)} %copy.60) | copy-start | bytes 3145732
  289.2 7.5 %copy-start.6 = (f32[512,1024]{1,0:T(8,128)S(1)}, f32[512,1024]{1,0:T(8,128)}, u32[]{:S(2)}) copy-start(f32[512,1024]{1,0:T(8,128)} %copy-done.5) | copy-start | bytes 6291460
  289.2 7.5 %copy-start.67 = (bf16[2048,1024]{1,0:T(8,128)(2,1)S(1)}, bf16[2048,1024]{1,0:T(8,128)(2,1)}, u32[]{:S(2)}) copy-start(bf16[2048,1024]{1,0:T(8,128)(2,1)} %param.28) | copy-start | bytes 12582916
  289.3 7.5 %copy-start.75 = (bf16[1024,2048]{1,0:T(8,128)(2,1)S(1)}, bf16[1024,2048]{1,0:T(8,128)(2,1)}, u32[]{:S(2)}) copy-start(bf16[1024,2048]{1,0:T(8,128)(2,1)} %get-tuple-element.40) | copy-start | bytes 12582916
  289.3 12.5 %collective-permute-start.7 = (bf16[512,1024]{1,0:T(8,128)(2,1)S(1)}, bf16[512,1024]{1,0:T(8,128)(2,1)S(1)}, u32[]{:S(2)}, u32[]{:S(2)}) collective-permute-start(bf16[512,1024]{1,0:T(8,128)(2,1)S(1)} %fusion.76), channel_id=1, source_target_pairs={{0,1},{1,0},{2,3},{3,2},{4,5},{5,4},{6,7},{7,6},{8,9},{9,8},{10,11... | collective-permute-start | bytes 3145736 | tf_op jit(solution)/shard_map/ppermute | solution.py:618
  305.5 6.2 collective-permute-start.8
  311.8 4.4 collective-permute-start.9
  316.2 293.7 %collective-permute-start.10 = (f32[4,1024]{1,0:T(4,128)S(1)}, f32[4,1024]{1,0:T(4,128)S(1)}, u32[]{:S(2)}, u32[]{:S(2)}) collective-permute-start(f32[4,1024]{1,0:T(4,128)S(1)} %fusion.181), channel_id=1, source_target_pairs={{0,4},{2,6},{4,0},{6,2},{8,12},{10,14},{12,8},{14,10},{16,20},{18,... | collective-permute-start | bytes 49160 | tf_op jit(solution)/shard_map/ppermute | solution.py:614
  605.4 9.2 %copy-start.17 = (f32[512,1024]{1,0:T(8,128)S(1)}, f32[512,1024]{1,0:T(8,128)}, u32[]{:S(2)}) copy-start(f32[512,1024]{1,0:T(8,128)} %get-tuple-element.36) | copy-start | bytes 6291460
  605.4 9.2 %copy-start.26 = (f32[512,1024]{1,0:T(8,128)S(1)}, f32[512,1024]{1,0:T(8,128)}, u32[]{:S(2)}) copy-start(f32[512,1024]{1,0:T(8,128)} %get-tuple-element.72) | copy-start | bytes 6291460
  609.9 2.7 collective-permute-start.11
  612.6 0.7 collective-permute-start.12
  613.3 10.2 %collective-permute-start.13 = (f32[4,1024]{1,0:T(4,128)S(1)}, f32[4,1024]{1,0:T(4,128)S(1)}, u32[]{:S(2)}, u32[]{:S(2)}) collective-permute-start(f32[4,1024]{1,0:T(4,128)S(1)} %add.265), channel_id=1, source_target_pairs={{8,0},{10,2},{12,4},{14,6},{16,24},{18,26},{20,28},{22,30},{9,1},{... | collective-permute-start | bytes 49160 | tf_op jit(solution)/shard_map/ppermute | solution.py:614
  614.6 9.5 %copy-start.1 = (bf16[512,1024]{1,0:T(8,128)(2,1)S(1)}, bf16[512,1024]{1,0:T(8,128)(2,1)}, u32[]{:S(2)}) copy-start(bf16[512,1024]{1,0:T(8,128)(2,1)} %param.23) | copy-start | bytes 3145732
  (54 other events, 214.0 us)

commit v3 on v2

--- a/solution.py
+++ b/solution.py
@@ -576,6 +576,174 @@
     )(*gradients)
 
 
+LANES = 128
+QUERY_TILE = 512
+BACK_TILE = 256
+
+
+def nt_dot(left, right):
+    return lax.dot_general(
+        left, right, (((1,), (1,)), ((), ())), preferred_element_type=jnp.float32
+    )
+
+
+def nn_dot(left, right):
+    return jnp.dot(left, right, preferred_element_type=jnp.float32)
+
+
+def swap_lanes(values):
+    lane = lax.broadcasted_iota(jnp.int32, values.shape, 1)
+    half_dim = HD // 2
+    ahead = pltpu.roll(values, LANES - half_dim, axis=1)
+    behind = pltpu.roll(values, half_dim, axis=1)
+    return jnp.where(lane % HD < half_dim, ahead, behind)
+
+
+def head_lanes(rows, head):
+    return lax.broadcasted_iota(jnp.int32, (rows, LANES), 1) // HD == head
+
+
+def masked_keys(keys, mask, head):
+    lane = lax.broadcasted_iota(jnp.int32, keys.shape, 1)
+    spare = (1 - head) * HD
+    keys = jnp.where(lane // HD == head, keys, jnp.zeros_like(keys))
+    for block in range(2):
+        keys = jnp.where(lane == spare + block, mask[:, block : block + 1], keys)
+    return keys
+
+
+def head_queries(queries, head, block):
+    lane = lax.broadcasted_iota(jnp.int32, queries.shape, 1)
+    spare = (1 - head) * HD
+    queries = jnp.where(lane // HD == head, queries, jnp.zeros_like(queries))
+    return jnp.where(lane == spare + block, jnp.ones_like(queries), queries)
+
+
+def attend_kernel(
+    query_raw, key_raw, value_raw, cosine, sine, mask, query_out, key_out, value_out, mixed_out, log_out, mixed_t
+):
+    rows = query_raw.shape[0]
+    block_rows = rows // 2
+    cos, sin = cosine[...], sine[...]
+    queries = query_raw[...]
+    query_out[...] = ((queries * cos + swap_lanes(queries) * sin) * HD ** (-0.5)).astype(jnp.bfloat16)
+    keys = key_raw[...]
+    key_out[...] = (keys * cos + swap_lanes(keys) * sin).astype(jnp.bfloat16)
+    value_out[...] = value_raw[...].astype(jnp.bfloat16)
+    values_t = value_out[...].T
+    mask_low = mask[...].astype(jnp.bfloat16)
+    keys_of = [masked_keys(key_out[...], mask_low, head) for head in range(2)]
+
+    def tile(index, carry):
+        span = pl.ds(pl.multiple_of(index * QUERY_TILE, QUERY_TILE), QUERY_TILE)
+        block = index * QUERY_TILE // block_rows
+        for head in range(2):
+            scores = nt_dot(keys_of[head], head_queries(query_out[span, :], head, block))
+            highest = jnp.max(scores, axis=0, keepdims=True)
+            weights = jnp.exp(scores - highest)
+            total = jnp.sum(weights, axis=0, keepdims=True)
+            mixed = nn_dot(values_t[head * HD : (head + 1) * HD], weights.astype(jnp.bfloat16)) / total
+            mixed_t[pl.ds(head * HD, HD), span] = mixed
+            log_out[0, pl.ds(head, 1), span] = highest + jnp.log(total)
+        return carry
+
+    lax.fori_loop(0, rows // QUERY_TILE, tile, 0, unroll=True)
+    mixed_out[...] = mixed_t[...].T.astype(jnp.bfloat16)
+
+
+def attend(query_raw, key_raw, value_raw, cosine, sine, mask):
+    rows, width = query_raw.shape
+    pairs = width // LANES
+    wide_block = pl.BlockSpec((rows, LANES), lambda pair: (0, pair))
+    table = pl.BlockSpec((rows, LANES), lambda pair: (0, 0))
+    low = jax.ShapeDtypeStruct((rows, width), jnp.bfloat16)
+    return pl.pallas_call(
+        attend_kernel,
+        grid=(pairs,),
+        in_specs=[wide_block] * 3 + [table, table, pl.BlockSpec((rows, 2), lambda pair: (0, 0))],
+        out_specs=[wide_block] * 4 + [pl.BlockSpec((1, 2, rows), lambda pair: (pair, 0, 0))],
+        out_shape=[low] * 4 + [jax.ShapeDtypeStruct((pairs, 2, rows), jnp.float32)],
+        scratch_shapes=[pltpu.VMEM((LANES, rows), jnp.float32)],
+        compiler_params=pltpu.CompilerParams(vmem_limit_bytes=32 * 1024 * 1024),
+        cost_estimate=pl.CostEstimate(
+            flops=4 * rows * rows * width, bytes_accessed=20 * rows * width, transcendentals=rows * rows * width // HD
+        ),
+    )(query_raw, key_raw, value_raw, cosine, sine, mask)
+
+
+def attend_back_pair(
+    query_rows, key_rows, value_rows, mixed_rows, grad_mixed, logs, cos, sin, mask, outs, grad_query_t, grad_key, grad_value, grad_t
+):
+    rows = query_rows.shape[0]
+    block_rows = rows // 2
+    mask_low = mask[...].astype(jnp.bfloat16)
+    keys_t = key_rows[...].T
+    values = value_rows[...]
+    grad_t[...] = (grad_mixed[...].astype(jnp.float32) * mixed_rows[...].astype(jnp.float32)).T
+    grad_key[...] = jnp.zeros_like(grad_key)
+    grad_value[...] = jnp.zeros_like(grad_value)
+    keys_of = [masked_keys(key_rows[...], mask_low, head) for head in range(2)]
+
+    def tile(index, carry):
+        span = pl.ds(pl.multiple_of(index * BACK_TILE, BACK_TILE), BACK_TILE)
+        block = index * BACK_TILE // block_rows
+        for head in range(2):
+            inside = head_lanes(BACK_TILE, head)
+            queries = query_rows[span, :]
+            grads = grad_mixed[span, :]
+            grads = jnp.where(inside, grads, jnp.zeros_like(grads))
+            centre = jnp.sum(grad_t[pl.ds(head * HD, HD), span], axis=0, keepdims=True)
+            scores = nt_dot(keys_of[head], head_queries(queries, head, block))
+            probs = jnp.exp(scores - logs[0, pl.ds(head, 1), span])
+            grad_probs = nt_dot(values, grads)
+            grad_scores = (probs * (grad_probs - centre)).astype(jnp.bfloat16)
+            grad_value[...] += nn_dot(probs.astype(jnp.bfloat16), grads)
+            grad_key[...] += nn_dot(grad_scores, jnp.where(inside, queries, jnp.zeros_like(queries)))
+            grad_query_t[pl.ds(head * HD, HD), span] = nn_dot(keys_t[head * HD : (head + 1) * HD], grad_scores)
+        return carry
+
+    lax.fori_loop(0, rows // BACK_TILE, tile, 0, unroll=True)
+    grad_query = grad_query_t[...].T * HD ** (-0.5)
+    outs[0][...] = (grad_query * cos[...] + swap_lanes(grad_query * sin[...])).astype(jnp.bfloat16)
+    grad_keys = grad_key[...]
+    outs[1][...] = (grad_keys * cos[...] + swap_lanes(grad_keys * sin[...])).astype(jnp.bfloat16)
+    outs[2][...] = grad_value[...].astype(jnp.bfloat16)
+
+
+def attend_back_kernel(
+    query_rows, key_rows, value_rows, mixed_rows, grad_mixed, logs, cos, sin, mask, grad_q, grad_k, grad_v, *scratch
+):
+    attend_back_pair(
+        query_rows, key_rows, value_rows, mixed_rows, grad_mixed, logs, cos, sin, mask, (grad_q, grad_k, grad_v), *scratch
+    )
+
+
+def attend_back(query_rows, key_rows, value_rows, mixed_rows, grad_mixed, logs, cosine, sine, mask):
+    rows, width = query_rows.shape
+    pairs = width // LANES
+    wide_block = pl.BlockSpec((rows, LANES), lambda pair: (0, pair))
+    table = pl.BlockSpec((rows, LANES), lambda pair: (0, 0))
+    low = jax.ShapeDtypeStruct((rows, width), jnp.bfloat16)
+    return pl.pallas_call(
+        attend_back_kernel,
+        grid=(pairs,),
+        in_specs=[wide_block] * 5
+        + [pl.BlockSpec((1, 2, rows), lambda pair: (pair, 0, 0)), table, table, pl.BlockSpec((rows, 2), lambda pair: (0, 0))],
+        out_specs=[wide_block] * 3,
+        out_shape=[low] * 3,
+        scratch_shapes=[
+            pltpu.VMEM((LANES, rows), jnp.float32),
+            pltpu.VMEM((rows, LANES), jnp.float32),
+            pltpu.VMEM((rows, LANES), jnp.float32),
+            pltpu.VMEM((LANES, rows), jnp.float32),
+        ],
+        compiler_params=pltpu.CompilerParams(vmem_limit_bytes=32 * 1024 * 1024),
+        cost_estimate=pl.CostEstimate(
+            flops=10 * rows * rows * width, bytes_accessed=16 * rows * width, transcendentals=rows * rows * width // HD
+        ),
+    )(query_rows, key_rows, value_rows, mixed_rows, grad_mixed, logs, cosine, sine, mask)
+
+
 def wide_index(x, y, z):
     return z * 4 + y * 2 + x
 
@@ -588,12 +756,6 @@
     if axis == "x":
         return [(wide_index(x, y, z), wide_index(1 - x, y, z)) for x, y, z in chip_positions()]
     return [(wide_index(x, y, z), wide_index(x, 1 - y, z)) for x, y, z in chip_positions()]
-
-
-def middle_flip_pairs(axis):
-    return [
-        pair for pair, (_, _, z) in zip(flip_pairs(axis), chip_positions()) if z in (1, 2)
-    ]
 
 
 def plane_pairs(moves):
@@ -605,41 +767,35 @@
     ]
 
 
-INWARD_MOVES = ((0, 1), (3, 2))
-ACROSS_MOVES = ((1, 2), (2, 1))
-OUTWARD_MOVES = ((1, 0), (2, 3))
-
-
 def send(values, pairs):
     return lax.ppermute(values, "wide", pairs)
-
-
-def partner(values):
-    return lax.ppermute(values, "narrow", [(0, 1), (1, 0)])
 
 
 def vector_sum(values):
     values = values + partner(values)
     values = values + send(values, flip_pairs("x"))
     values = values + send(values, flip_pairs("y"))
-    values = values + send(values, plane_pairs(INWARD_MOVES))
-    values = values + send(values, plane_pairs(ACROSS_MOVES))
+    values = values + send(values, plane_pairs(((0, 1), (3, 2))))
+    values = values + send(values, plane_pairs(((1, 2), (2, 1))))
     plane = lax.axis_index("wide") // 4
-    outward = send(values, plane_pairs(OUTWARD_MOVES))
+    outward = send(values, plane_pairs(((1, 0), (2, 3))))
     return jnp.where((plane == 1) | (plane == 2), values, outward)
+
+
+def partner(values):
+    return lax.ppermute(values, "narrow", [(0, 1), (1, 0)])
 
 
 def rows_of(own, other):
     return jnp.concatenate([own, other], axis=0)
 
 
-def rotary_own_first(position, width):
-    columns = jnp.arange(width) % HD
+def rotary_pair_tables(position):
+    lane = jnp.arange(LANES) % HD
     half_dim = HD // 2
-    freq_index = (columns % half_dim).astype(jnp.float32)
-    frequency = ROPE_BASE ** (-2.0 * freq_index / HD)
+    frequency = ROPE_BASE ** (-2.0 * (lane % half_dim).astype(jnp.float32) / HD)
     angles = position[:, None] * frequency[None, :]
-    signs = jnp.where(columns < half_dim, -1.0, 1.0).astype(jnp.float32)
+    signs = jnp.where(lane < half_dim, -1.0, 1.0).astype(jnp.float32)
     return (jnp.cos(angles), jnp.sin(angles) * signs)
 
 
@@ -661,68 +817,32 @@
     cotangent,
 ):
     block_rows = tokens.shape[0]
-    local_width = w_query.shape[1]
-    local_heads = local_width // HD
-    local_hidden = w_gate.shape[1]
-    softmax_scale = HD ** (-0.5)
     own_block = lax.axis_index("narrow")
     joined = window_span[0] == 2
     block_ids = jnp.stack([own_block, 1 - own_block])
     lengths = valid_len[block_ids]
-    position = (
-        jnp.arange(block_rows)[None, :]
-        + block_rows * (block_ids[:, None] * joined.astype(jnp.int32))
-    ).reshape(-1).astype(jnp.float32)
+    offsets = jnp.arange(2 * block_rows)
+    row_block = offsets // block_rows
+    position = offsets % block_rows + block_rows * jnp.repeat(block_ids, block_rows) * joined.astype(jnp.int32)
+    cosine, sine = rotary_pair_tables(position.astype(jnp.float32))
+    within = offsets % block_rows < jnp.repeat(lengths, block_rows)
+    seen = within[:, None] & (joined | (row_block[:, None] == jnp.arange(2)[None, :]))
+    mask = jnp.where(seen, 0.0, MASKED).astype(jnp.float32)
 
     token_values = tokens.astype(jnp.float32)
     normed_one, scaled_one, inverse_one = norm_forward(token_values, norm1_gain, norm1_shift)
     normed_one = normed_one.astype(jnp.bfloat16)
     gathered_one = rows_of(normed_one, partner(normed_one))
     cot_rows = rows_of(cotangent, partner(cotangent))
-    joined_qkv = jnp.concatenate([w_query, w_key, w_value], axis=1)
-    projected = jnp.dot(gathered_one, joined_qkv, preferred_element_type=jnp.float32)
-    cosine, sine_signed = rotary_own_first(position, local_width)
-    query_rows = (rotate(projected[:, :local_width], cosine, sine_signed) * softmax_scale).astype(
-        jnp.bfloat16
-    )
-    key_rows = rotate(projected[:, local_width : 2 * local_width], cosine, sine_signed).astype(
-        jnp.bfloat16
-    )
-    value_rows = projected[:, 2 * local_width :].astype(jnp.bfloat16)
-    query_heads = query_rows.reshape(2, block_rows, local_heads, HD)
-    key_heads = key_rows.reshape(2 * block_rows, local_heads, HD)
-    value_heads = value_rows.reshape(2 * block_rows, local_heads, HD)
-    offsets = jnp.arange(2 * block_rows)
-    within = offsets % block_rows < jnp.repeat(lengths, block_rows)
-
-    def masked_scores(index):
-        scores = jnp.einsum(
-            "qhd,khd->hqk", query_heads[index], key_heads, preferred_element_type=jnp.float32
-        )
-        key_mask = within & (joined | (offsets // block_rows == index))
-        return jnp.where(key_mask[None, None, :], scores, MASKED)
-
-    def attend_forward(index):
-        scores = masked_scores(index)
-        highest = jnp.max(scores, axis=-1, keepdims=True)
-        weights = jnp.exp(scores - highest)
-        weight_total = jnp.sum(weights, axis=-1, keepdims=True)
-        attention_probs = (weights / weight_total).astype(jnp.bfloat16)
-        mixed_block = jnp.einsum(
-            "hqk,khd->qhd", attention_probs, value_heads, preferred_element_type=jnp.float32
-        )
-        return (
-            mixed_block.reshape(block_rows, local_width).astype(jnp.bfloat16),
-            (highest + jnp.log(weight_total))[:, :, 0],
-        )
-
-    mixed_own, log_own = attend_forward(0)
-    mixed_other, log_other = attend_forward(1)
-    mixed_rows = rows_of(mixed_own, mixed_other)
-    other_share = jnp.dot(mixed_other, w_out, preferred_element_type=jnp.float32)
+    projected = [
+        jnp.dot(gathered_one, weight, preferred_element_type=jnp.float32)
+        for weight in (w_query, w_key, w_value)
+    ]
+    query_rows, key_rows, value_rows, mixed_rows, logs = attend(*projected, cosine, sine, mask)
+    other_share = jnp.dot(mixed_rows[block_rows:], w_out, preferred_element_type=jnp.float32)
     resid_values = (
         token_values
-        + jnp.dot(mixed_own, w_out, preferred_element_type=jnp.float32)
+        + jnp.dot(mixed_rows[:block_rows], w_out, preferred_element_type=jnp.float32)
         + partner(other_share)
     )
     normed_two, scaled_two, inverse_two = norm_forward(resid_values, norm2_gain, norm2_shift)
@@ -732,7 +852,7 @@
     up_values = jnp.dot(gathered_two, w_up, preferred_element_type=jnp.float32)
     sigmoid_gate = jax.nn.sigmoid(gate_values)
     hidden_rows = (gate_values * sigmoid_gate * up_values).astype(jnp.bfloat16)
-    down_summed = transpose_times(hidden_rows, cot_rows).astype(jnp.bfloat16)
+    down_grad = transpose_times(hidden_rows, cot_rows).astype(jnp.bfloat16)
 
     out_other = jnp.dot(
         hidden_rows[block_rows:], w_down, preferred_element_type=jnp.float32
@@ -746,8 +866,8 @@
     silu_grad = sigmoid_gate * (1.0 + gate_values * (1.0 - sigmoid_gate))
     grad_gate = (grad_hidden * up_values * silu_grad).astype(jnp.bfloat16)
     grad_up = (grad_hidden * gate_values * sigmoid_gate).astype(jnp.bfloat16)
-    gate_summed = transpose_times(gathered_two, grad_gate).astype(jnp.bfloat16)
-    up_summed = transpose_times(gathered_two, grad_up).astype(jnp.bfloat16)
+    gate_grad = transpose_times(gathered_two, grad_gate).astype(jnp.bfloat16)
+    up_grad = transpose_times(gathered_two, grad_up).astype(jnp.bfloat16)
 
     def grad_two_share(rows):
         return times_transpose(grad_gate[rows], w_gate) + times_transpose(grad_up[rows], w_up)
@@ -761,45 +881,22 @@
     grad_attention = grad_resid.astype(jnp.bfloat16)
     grad_rows = rows_of(grad_attention, partner(grad_attention))
     grad_mixed = times_transpose(grad_rows, w_out).astype(jnp.bfloat16)
-    out_summed = transpose_times(mixed_rows, grad_rows).astype(jnp.bfloat16)
-    grad_mixed_heads = grad_mixed.reshape(2, block_rows, local_heads, HD)
-
-    def attend_backward(index, log_total):
-        grad_block = grad_mixed_heads[index]
-        scores = masked_scores(index)
-        attention_probs = jnp.exp(scores - log_total[:, :, None])
-        grad_probs = jnp.einsum(
-            "qhd,khd->hqk", grad_block, value_heads, preferred_element_type=jnp.float32
+    out_grad = transpose_times(mixed_rows, grad_rows).astype(jnp.bfloat16)
+    grad_projected = attend_back(
+        query_rows, key_rows, value_rows, mixed_rows, grad_mixed, logs, cosine, sine, mask
+    )
+    qkv_grads = [transpose_times(gathered_one, g).astype(jnp.bfloat16) for g in grad_projected]
+
+    def grad_one_share(rows):
+        return sum(
+            times_transpose(g[rows], weight)
+            for g, weight in zip(grad_projected, (w_query, w_key, w_value))
         )
-        centre = jnp.sum(attention_probs * grad_probs, axis=-1, keepdims=True)
-        grad_scores = (attention_probs * (grad_probs - centre)).astype(jnp.bfloat16)
-        block_query = jnp.einsum(
-            "hqk,khd->qhd", grad_scores, key_heads, preferred_element_type=jnp.float32
-        ).reshape(block_rows, local_width)
-        pair_key = jnp.einsum(
-            "hqk,qhd->khd", grad_scores, query_heads[index], preferred_element_type=jnp.float32
-        ).reshape(2 * block_rows, local_width)
-        pair_value = jnp.einsum(
-            "hqk,qhd->khd",
-            attention_probs.astype(jnp.bfloat16),
-            grad_block,
-            preferred_element_type=jnp.float32,
-        ).reshape(2 * block_rows, local_width)
-        return block_query, pair_key, pair_value
-
-    query_own, key_own, value_own = attend_backward(0, log_own)
-    query_other, key_other, value_other = attend_backward(1, log_other)
-    grad_query = rows_of(query_own, query_other)
-    grad_query_raw = rotate_back(grad_query * softmax_scale, cosine, sine_signed)
-    grad_key_raw = rotate_back(key_own + key_other, cosine, sine_signed)
-    grad_qkv = jnp.concatenate(
-        [grad_query_raw, grad_key_raw, value_own + value_other], axis=1
-    ).astype(jnp.bfloat16)
-    qkv_summed = transpose_times(gathered_one, grad_qkv).astype(jnp.bfloat16)
-    grad_one_other = times_transpose(grad_qkv[block_rows:], joined_qkv).astype(jnp.bfloat16)
-    grad_normed_one = times_transpose(grad_qkv[:block_rows], joined_qkv) + partner(
-        grad_one_other
-    ).astype(jnp.float32)
+
+    grad_one_other = grad_one_share(slice(block_rows, None)).astype(jnp.bfloat16)
+    grad_normed_one = grad_one_share(slice(0, block_rows)) + partner(grad_one_other).astype(
+        jnp.float32
+    )
     grad_in_one, gain_one_grad, shift_one_grad = norm_backward(
         grad_normed_one, scaled_one, inverse_one, norm1_gain
     )
@@ -807,19 +904,10 @@
     norm_summed = vector_sum(
         jnp.stack([gain_one_grad, shift_one_grad, gain_two_grad, shift_two_grad])
     )
-    width = local_width
     down_summed, gate_summed, up_summed, out_summed, query_summed, key_summed, value_summed = [
         total.astype(jnp.float32)
         for total in summed_over_wide(
-            [
-                down_summed,
-                gate_summed,
-                up_summed,
-                out_summed,
-                qkv_summed[:, :width],
-                qkv_summed[:, width : 2 * width],
-                qkv_summed[:, 2 * width :],
-            ],
+            [down_grad, gate_grad, up_grad, out_grad] + qkv_grads,
             [128, 64, 64, 128, 128, 128, 128],
             1,
         )

time: 629 us -> 496 us (0.79)
  other arithmetic: 101 us -> 34.5 us
  matrix products: 168 us -> 111 us
  local copies, waits for them, and re-layouts: 65.7 us -> 10.1 us
  Pallas kernels: 268 us -> 312 us
    dot_general x15 -> x5, matrix products: 76.9 us -> 13.2 us  [the longest x3 8.76 us: on_device(): jnp.dot(gathered_one, weight, preferred_element_type=jnp.float32)]
    pallas_call x0 -> x2, Pallas kernels: none -> 44.3 us  [the longest x1 23.8 us: attend_back(): pl.pallas_call(attend_back_kernel, grid=(pairs,), in_specs=[wide_block] *...]
    convert_element_type x3 -> x1, other arithmetic: 39.1 us -> 0.01 us  [on_device(): cosine, sine = rotary_pair_tables(position.astype(jnp.float32))]
    slice x10 -> x0, local copies, waits for them, and re-layouts: 18.8 us -> none  [the longest x3 6.75 us: masked_scores(): query_heads[index]]
    reshape x6 -> x0, local copies, waits for them, and re-layouts: 13.4 us -> none  [the longest x4 9.39 us: swap_halves(): return jnp.flip(parts, axis=2).reshape(row_count, width)]
    another operation x1 -> x0, other arithmetic: 9.86 us -> none
    rev x4 -> x0, local copies, waits for them, and re-layouts: 9.77 us -> none  [swap_halves(): return jnp.flip(parts, axis=2).reshape(row_count, width)]
    unnamed x182 -> x85, local copies, waits for them, and re-layouts: 15.4 us -> 7.26 us
  transfers between devices with their start and end apart: 14 -> 14, of which waited for: 2 -> 3; matrix products, arithmetic and copies ran while one was open for 45% -> 20% of each run, Pallas kernels for 43% -> 59%
where the time goes in v3:
time: 496 us; the launch traced here: 491 us
  Pallas kernels  312 us (63%)
  matrix products  111 us (22%)
  other arithmetic  34.5 us (7%)
  waiting for transfers between devices  10.8 us (2%)
  starting transfers between devices  10.4 us (2%)
  local copies, waits for them, and re-layouts  10.1 us (2%)
    pallas_call x1, Pallas kernels, summed_over_wide(): pl.pallas_call(functools.partial(sum_kernel, jobs), out_shape=[jax.ShapeD...  268 us
    dot_general x12, matrix products, times_transpose(): lax.dot_general(left, right, (((1,), (1,)), ((), ())), preferred_element_...  34.8 us
    dot_general x7, matrix products, transpose_times(): lax.dot_general(left, right, (((0,), (0,)), ((), ())), preferred_element_...  32.4 us
    pallas_call x1, Pallas kernels, attend_back(): pl.pallas_call(attend_back_kernel, grid=(pairs,), in_specs=[wide_block] *...  23.8 us
    convert_element_type x7, other arithmetic, on_device(): total.astype(jnp.float32)  21.1 us
    pallas_call x1, Pallas kernels, attend(): pl.pallas_call(attend_kernel, grid=(pairs,), in_specs=[wide_block] * 3 +...  20.5 us
    dot_general x1, matrix products, on_device(): jnp.dot(gathered_two, w_gate, preferred_element_type=jnp.float32)  16.9 us
  transfers between devices with their start and end apart: 14, of which 3 were waited for; matrix products, arithmetic and copies ran while one was open for 20% of the time, Pallas kernels for 59%

profile of v3, /device:TPU:0, one launch (start us, length us, event | category | flops | bytes accessed | tf_op | source)
XLA Modules:
  0.0 490.7 jit_solution(11880382346099646840)
XLA Ops:
  0.7 1.6 convert_reduce_fusion
  2.3 1.6 fusion.13
  4.0 1.4 fusion.7
  7.3 1.9 fusion.37
  9.2 3.1 fusion.71.key_raw
  12.3 2.9 fusion.70.value_raw
  15.2 2.8 fusion.72.query_raw
  18.0 20.5 %shard_map.246 = (bf16[1024,512]{1,0:T(8,128)(2,1)S(1)}, bf16[1024,512]{1,0:T(8,128)(2,1)S(1)}, bf16[1024,512]{1,0:T(8,128)(2,1)S(1)}, bf16[1024,512]{1,0:T(8,128)(2,1)S(1)}, f32[4,2,1024]{2,1,0:T(2,128)S(1)}) custom-call(f32[1024,512]{1,0:T(8,128)S(1)} %fusion.72.query_raw, f32[1024,512]{1,0:T(8,128)S(1)} %fusion.71.key_raw, ...), custom_call_target="tpu_custom_call" | custom-call | flops 2147483648 | bytes 10485760 | tf_op jit(solution)/shard_map/pallas_call | solution.py:660
  41.5 2.0 fusion.48
  44.0 1.4 constant_dynamic-update-slice_fusion.1
  45.5 2.5 collective-permute-done.1
  48.0 2.5 fusion.75
  51.8 1.6 constant_dynamic-update-slice_fusion
  53.7 6.8 %fusion.76 = f32[1024,2048]{1,0:T(8,128)} fusion(bf16[1024,1024]{1,0:T(8,128)(2,1)S(1)} %constant_dynamic-update-slice_fusion, bf16[2048,1024]{1,0:T(8,128)(2,1)S(1)} %copy-done.33), kind=kOutput, calls=%fused_computation.130 | convolution fusion | flops 4294967296 | bytes 14680064 | tf_op jit(solution)/shard_map/dot_general | solution.py:21
  60.5 7.7 %fusion.68 = f32[1024,2048]{1,0:T(8,128)} fusion(bf16[1024,2048]{1,0:T(8,128)(2,1)S(1)} %copy-done.30, bf16[512,1024]{1,0:T(8,128)(2,1)S(1)} %collective-permute-done.2, bf16[512,1024]{1,0:T(8,128)(2,1)S(1)} %add_convert_fusion.1), kind=kOutput, calls=%fused_computation.122 | convolution fusion | flops 4299161600 | bytes 14680064 | tf_op jit(solution)/shard_map/dot_general | solution.py:852
  68.1 16.9 %multiply_convert_fusion.1 = (bf16[1024,2048]{1,0:T(8,128)(2,1)}, bf16[1024,2048]{1,0:T(8,128)(2,1)}, bf16[1024,2048]{1,0:T(8,128)(2,1)}) fusion(f32[1024,2048]{1,0:T(8,128)} %fusion.76, f32[1024,2048]{1,0:T(8,128)} %fusion.68, bf16[1024,2048]{1,0:T(8,128)(2,1)} %param.26, bf16[512,1024]{1,0:T(8,128)(2,1)S(1)} %collective-permute-done.2, ...), kind=kOutput, calls=%fused_computation.2 | convolution fusion | flops 4332716032 | bytes 35651584 | tf_op jit(solution)/shard_map/dot_general | solution.py:851
  85.0 5.3 %fusion.15 = f32[512,1024]{1,0:T(8,128)S(1)} fusion(bf16[1024,2048]{1,0:T(8,128)(2,1)} %param.27, bf16[1024,2048]{1,0:T(8,128)(2,1)} %get-tuple-element.55), kind=kOutput, calls=%fused_computation.26 | convolution fusion | flops 2147483648 | bytes 8388608 | tf_op jit(solution)/shard_map/dot_general | solution.py:21
  90.4 4.1 fusion.31
  94.8 2.4 fusion.34
  97.5 5.5 %fusion.19 = f32[512,1024]{1,0:T(8,128)} fusion(bf16[1024,2048]{1,0:T(8,128)(2,1)S(1)} %copy-done.31, bf16[1024,2048]{1,0:T(8,128)(2,1)} %get-tuple-element.55), kind=kOutput, calls=%fused_computation.30 | convolution fusion | flops 2147483648 | bytes 8388608 | tf_op jit(solution)/shard_map/dot_general | solution.py:21
  103.0 6.4 %convolution_convert_fusion.refs_2_ = bf16[1024,2048]{1,0:T(8,128)(2,1)} fusion(bf16[1024,2048]{1,0:T(8,128)(2,1)S(1)} %copy-done.39, bf16[512,1024]{1,0:T(8,128)(2,1)S(1)} %collective-permute-done.2, bf16[512,1024]{1,0:T(8,128)(2,1)S(1)} %add_convert_fusion.1), kind=kOutput, calls=%fused_computation.5 | convolution fusion | flops 4301258752 | bytes 10485760 | tf_op jit(solution)/shard_map/dot_general | solution.py:27
  109.4 5.3 %multiply_reduce_fusion = (f32[1024]{0:T(1024)S(1)}, f32[512]{0:T(512)S(1)}, f32[512]{0:T(512)S(1)}, f32[1024]{0:T(1024)S(1)}, f32[512,1024]{1,0:T(8,128)S(1)}) fusion(f32[512,1024]{1,0:T(8,128)S(1)} %get-tuple-element.63, f32[512]{0:T(512)S(1)} %add_rsqrt_fusion, f32[512]{0:T(512)S(1)} %broadcast_multiply_fusion.4, f32[1024]{0:T(1024)S(1)} %copy-done.27, ...), kind=kOutput, calls=%fused_computation.41 | convolution fusion | flops 2153247744 | bytes 14700544 | tf_op jit(solution)/shard_map/dot_general | solution.py:21
  114.7 3.5 fusion.73
  118.4 6.2 %convolution_convert_fusion.1.refs_1_ = bf16[1024,2048]{1,0:T(8,128)(2,1)} fusion(bf16[1024,2048]{1,0:T(8,128)(2,1)S(1)} %copy-done.38, bf16[512,1024]{1,0:T(8,128)(2,1)S(1)} %collective-permute-done.2, bf16[512,1024]{1,0:T(8,128)(2,1)S(1)} %add_convert_fusion.1), kind=kOutput, calls=%fused_computation.6 | convolution fusion | flops 4301258752 | bytes 10485760 | tf_op jit(solution)/shard_map/dot_general | solution.py:27
  124.6 6.1 %convolution_convert_fusion.2.refs_0_ = bf16[2048,1024]{1,0:T(8,128)(2,1)} fusion(bf16[1024,2048]{1,0:T(8,128)(2,1)S(1)} %copy-done.37, bf16[1024,1024]{1,0:T(8,128)(2,1)S(1)} %constant_dynamic-update-slice_fusion), kind=kOutput, calls=%fused_computation.7 | convolution fusion | flops 4297064448 | bytes 10485760 | tf_op jit(solution)/shard_map/dot_general | solution.py:27
  130.7 1.3 convolution_convert_fusion.7.grad_mixed
  132.7 23.8 %shard_map.247 = (bf16[1024,512]{1,0:T(8,128)(2,1)S(1)}, bf16[1024,512]{1,0:T(8,128)(2,1)S(1)}, bf16[1024,512]{1,0:T(8,128)(2,1)S(1)}) custom-call(bf16[1024,512]{1,0:T(8,128)(2,1)S(1)} %copy-done.4, bf16[1024,512]{1,0:T(8,128)(2,1)S(1)} %copy-done.6, bf16[1024,512]{1,0:T(8,128)(2,1)S(1)} %copy-done.8, bf16[1024,512]{1,0:T(8,128)(2,1)S(1)} %get-tuple-element.28.mixed_rows, ...), custom_call_target="tpu_custom_call" | custom-call | flops 5368709120 | bytes 8388608 | tf_op jit(solution)/shard_map/pallas_call | solution.py:727
  159.8 3.7 convert_add_fusion.2
  165.0 3.8 convolution_convert_fusion.5.refs_4_
  168.8 2.8 fusion.12
  171.9 3.8 convolution_convert_fusion.4.refs_5_
  175.7 2.9 collective-permute-start.9
  178.6 3.8 convolution_convert_fusion.3.refs_6_
  182.4 1.6 collective-permute-start.10
  184.0 2.2 convolution_convert_fusion.6.refs_3_
  186.3 268.0 %shard_map.248 = (bf16[2048,1024]{1,0:T(8,128)(2,1)}, bf16[1024,2048]{1,0:T(8,128)(2,1)}, bf16[1024,2048]{1,0:T(8,128)(2,1)}, bf16[512,1024]{1,0:T(8,128)(2,1)},...) custom-call(bf16[2048,1024]{1,0:T(8,128)(2,1)} %convolution_convert_fusion.2.refs_0_, ...), custom_call_target="tpu_custom_call" | custom-call | bytes 41943040 | tf_op jit(solution)/shard_map/pallas_call | solution.py:566
  454.2 2.9 convert_element_type.118
  457.2 1.6 convert_element_type.119
  458.8 1.6 convert_element_type.120
  460.4 1.6 convert_element_type.121
  462.8 4.5 convert_element_type.122
  467.3 4.5 convert_element_type.123
  471.7 4.4 convert_element_type.124
  476.2 1.3 collective-permute-start.11
  477.5 1.4 collective-permute-done.11
  479.6 1.3 collective-permute-start.13
  480.9 2.0 fusion.11
  483.0 6.8 %collective-permute-done.13 = f32[4,1024]{1,0:T(4,128)S(1)} collective-permute-done((f32[4,1024]{1,0:T(4,128)S(1)}, f32[4,1024]{1,0:T(4,128)S(1)}, u32[]{:S(2)}, u32[]{:S(2)}) %collective-permute-start.13) | collective-permute-done | bytes 16416 | tf_op jit(solution)/shard_map/ppermute | solution.py:771
  (137 shorter events, 15.6 us)
Async XLA Ops:
  0.6 11.7 %copy-start = (bf16[1024,512]{1,0:T(8,128)(2,1)S(1)}, bf16[1024,512]{1,0:T(8,128)(2,1)}, u32[]{:S(2)}) copy-start(bf16[1024,512]{1,0:T(8,128)(2,1)} %param.22) | copy-start | bytes 3145732
  0.7 3.3 copy-start.10
  0.7 3.3 copy-start.26
  0.7 3.3 copy-start.28
  0.7 5.3 %copy-start.9 = (s32[2]{0:T(128)S(1)}, s32[2]{0:T(128)}, u32[]{:S(2)}) copy-start(s32[2]{0:T(128)} %param.17) | copy-start | bytes 28
  2.3 4.4 copy-start.35
  5.4 3.8 collective-permute-start
  7.3 10.7 %copy-start.1 = (f32[1024,2]{1,0:T(8,128)}, f32[1024,2]{1,0:T(8,128)S(1)}, u32[]{:S(2)}) copy-start(f32[1024,2]{1,0:T(8,128)S(1)} %fusion.53.mask) | copy-start | bytes 24580
  12.3 2.9 copy-start.20
  18.0 23.5 %copy-start.18 = (bf16[512,1024]{1,0:T(8,128)(2,1)S(1)}, bf16[512,1024]{1,0:T(8,128)(2,1)}, u32[]{:S(2)}) copy-start(bf16[512,1024]{1,0:T(8,128)(2,1)} %param.23) | copy-start | bytes 3145732
  43.5 4.5 collective-permute-start.1
  43.5 8.3 %collective-permute-start.4 = (bf16[512,1024]{1,0:T(8,128)(2,1)}, bf16[512,1024]{1,0:T(8,128)(2,1)}, u32[]{:S(2)}, u32[]{:S(2)}) collective-permute-start(bf16[512,1024]{1,0:T(8,128)(2,1)} %param.29), channel_id=1, source_target_pairs={{0,1},{1,0},{2,3},{3,2},{4,5},{5,4},{6,7},{7,6},{8,9},{9,8},{10,11... | collective-permute-start | bytes 3145736 | tf_op jit(solution)/shard_map/ppermute | solution.py:786
  44.0 4.0 copy-start.11
  44.0 4.0 copy-start.19
  51.2 2.5 copy-start.33
  51.6 8.9 %collective-permute-start.2 = (bf16[512,1024]{1,0:T(8,128)(2,1)S(1)}, bf16[512,1024]{1,0:T(8,128)(2,1)S(1)}, u32[]{:S(2)}, u32[]{:S(2)}) collective-permute-start(bf16[512,1024]{1,0:T(8,128)(2,1)S(1)} %add_convert_fusion.1), channel_id=1, source_target_pairs={{0,1},{1,0},{2,3},{3,2},{4,5},{5,4},{6,7},{7,6},{8,9},{9,8},{10,11... | collective-permute-start | bytes 3145736 | tf_op jit(solution)/shard_map/ppermute | solution.py:786
  53.7 6.8 %copy-start.30 = (bf16[1024,2048]{1,0:T(8,128)(2,1)S(1)}, bf16[1024,2048]{1,0:T(8,128)(2,1)}, u32[]{:S(2)}) copy-start(bf16[1024,2048]{1,0:T(8,128)(2,1)} %param.27) | copy-start | bytes 12582916
  85.0 5.3 %copy-start.32 = (bf16[1024,2048]{1,0:T(8,128)(2,1)S(1)}, bf16[1024,2048]{1,0:T(8,128)(2,1)}, u32[]{:S(2)}) copy-start(bf16[1024,2048]{1,0:T(8,128)(2,1)} %param.26) | copy-start | bytes 12582916
  90.4 4.4 copy-start.34
  90.4 4.4 copy-start.36
  94.5 14.9 %collective-permute-start.5 = (f32[512,1024]{1,0:T(8,128)S(1)}, f32[512,1024]{1,0:T(8,128)S(1)}, u32[]{:S(2)}, u32[]{:S(2)}) collective-permute-start(f32[512,1024]{1,0:T(8,128)S(1)} %fusion.31), channel_id=1, source_target_pairs={{0,1},{1,0},{2,3},{3,2},{4,5},{5,4},{6,7},{7,6},{8,9},{9,8},{10,11... | collective-permute-start | bytes 6291464 | tf_op jit(solution)/shard_map/ppermute | solution.py:786
  94.8 2.7 copy-start.31
  97.1 5.8 %copy-start.39 = (bf16[1024,2048]{1,0:T(8,128)(2,1)S(1)}, bf16[1024,2048]{1,0:T(8,128)(2,1)}, u32[]{:S(2)}) copy-start(bf16[1024,2048]{1,0:T(8,128)(2,1)} %get-tuple-element.55) | copy-start | bytes 12582916
  97.2 62.6 %collective-permute-start.3 = (bf16[512,1024]{1,0:T(8,128)(2,1)S(1)}, bf16[512,1024]{1,0:T(8,128)(2,1)S(1)}, u32[]{:S(2)}, u32[]{:S(2)}) collective-permute-start(bf16[512,1024]{1,0:T(8,128)(2,1)S(1)} %fusion.34), channel_id=1, source_target_pairs={{0,1},{1,0},{2,3},{3,2},{4,5},{5,4},{6,7},{7,6},{8,9},{9,8},{10,11... | collective-permute-start | bytes 3145736 | tf_op jit(solution)/shard_map/ppermute | solution.py:786
  114.7 3.7 copy-start.38
  118.2 6.4 %copy-start.37 = (bf16[1024,2048]{1,0:T(8,128)(2,1)S(1)}, bf16[1024,2048]{1,0:T(8,128)(2,1)}, u32[]{:S(2)}) copy-start(bf16[1024,2048]{1,0:T(8,128)(2,1)} %get-tuple-element.54) | copy-start | bytes 12582916
  118.2 12.5 %collective-permute-start.6 = (bf16[512,1024]{1,0:T(8,128)(2,1)S(1)}, bf16[512,1024]{1,0:T(8,128)(2,1)S(1)}, u32[]{:S(2)}, u32[]{:S(2)}) collective-permute-start(bf16[512,1024]{1,0:T(8,128)(2,1)S(1)} %get-tuple-element.51), channel_id=1, source_target_pairs={{0,1},{1,0},{2,3},{3,2},{4,5},{5,4},{6,7},{7,6},{8,9},{9,8},{10,11... | collective-permute-start | bytes 3145736 | tf_op jit(solution)/shard_map/ppermute | solution.py:786
  130.7 1.3 copy-start.2
  130.7 1.4 copy-start.4
  130.7 1.7 copy-start.6
  130.7 2.0 copy-start.8
  132.7 23.8 %copy-start.21 = (bf16[1024,512]{1,0:T(8,128)(2,1)S(1)}, bf16[1024,512]{1,0:T(8,128)(2,1)}, u32[]{:S(2)}) copy-start(bf16[1024,512]{1,0:T(8,128)(2,1)} %param.20) | copy-start | bytes 3145732
  159.4 9.4 %collective-permute-start.7 = (bf16[512,1024]{1,0:T(8,128)(2,1)S(1)}, bf16[512,1024]{1,0:T(8,128)(2,1)S(1)}, u32[]{:S(2)}, u32[]{:S(2)}) collective-permute-start(bf16[512,1024]{1,0:T(8,128)(2,1)S(1)} %add_convert_fusion), channel_id=1, source_target_pairs={{0,1},{1,0},{2,3},{3,2},{4,5},{5,4},{6,7},{7,6},{8,9},{9,8},{10,11... | collective-permute-start | bytes 3145736 | tf_op jit(solution)/shard_map/ppermute | solution.py:786
  171.6 4.1 collective-permute-start.8
  175.7 6.7 %collective-permute-start.9 = (f32[4,1024]{1,0:T(4,128)S(1)}, f32[4,1024]{1,0:T(4,128)S(1)}, u32[]{:S(2)}, u32[]{:S(2)}) collective-permute-start(f32[4,1024]{1,0:T(4,128)S(1)} %fusion.67), channel_id=1, source_target_pairs={{0,2},{2,0},{4,6},{6,4},{8,10},{10,8},{12,14},{14,12},{16,18},{18,... | collective-permute-start | bytes 49160 | tf_op jit(solution)/shard_map/ppermute | solution.py:771
  182.4 293.7 %collective-permute-start.10 = (f32[4,1024]{1,0:T(4,128)S(1)}, f32[4,1024]{1,0:T(4,128)S(1)}, u32[]{:S(2)}, u32[]{:S(2)}) collective-permute-start(f32[4,1024]{1,0:T(4,128)S(1)} %fusion.107), channel_id=1, source_target_pairs={{0,4},{2,6},{4,0},{6,2},{8,12},{10,14},{12,8},{14,10},{16,20},{18,... | collective-permute-start | bytes 49160 | tf_op jit(solution)/shard_map/ppermute | solution.py:771
  454.2 2.9 copy-start.25
  457.2 1.6 copy-start.24
  458.8 1.6 copy-start.23
  458.8 4.0 copy-start.17
  462.8 4.5 copy-start.16
  467.3 4.5 copy-start.15
  471.7 9.2 %copy-start.12 = (bf16[512,1024]{1,0:T(8,128)(2,1)S(1)}, bf16[512,1024]{1,0:T(8,128)(2,1)}, u32[]{:S(2)}) copy-start(bf16[512,1024]{1,0:T(8,128)(2,1)} %param.15) | copy-start | bytes 3145732
  471.7 9.2 %copy-start.13 = (f32[512,1024]{1,0:T(8,128)S(1)}, f32[512,1024]{1,0:T(8,128)}, u32[]{:S(2)}) copy-start(f32[512,1024]{1,0:T(8,128)} %get-tuple-element.52) | copy-start | bytes 6291460
  471.7 9.2 %copy-start.14 = (f32[512,1024]{1,0:T(8,128)S(1)}, f32[512,1024]{1,0:T(8,128)}, u32[]{:S(2)}) copy-start(f32[512,1024]{1,0:T(8,128)} %get-tuple-element.65) | copy-start | bytes 6291460
  476.2 2.7 collective-permute-start.11
  478.9 0.7 collective-permute-start.12
  479.6 10.2 %collective-permute-start.13 = (f32[4,1024]{1,0:T(4,128)S(1)}, f32[4,1024]{1,0:T(4,128)S(1)}, u32[]{:S(2)}, u32[]{:S(2)}) collective-permute-start(f32[4,1024]{1,0:T(4,128)S(1)} %add.189), channel_id=1, source_target_pairs={{8,0},{10,2},{12,4},{14,6},{16,24},{18,26},{20,28},{22,30},{9,1},{... | collective-permute-start | bytes 49160 | tf_op jit(solution)/shard_map/ppermute | solution.py:771
  (6 other events, 5.5 us)

commit v4 on v3

--- a/solution.py
+++ b/solution.py
@@ -341,25 +341,115 @@
         def signal(target):
             pl.semaphore_signal(barrier, inc=1, device_id={"wide": target}, device_id_type=MESH)
 
+        pl.semaphore_signal(
+            barrier, inc=1, device_id={"narrow": 1 - lax.axis_index("narrow")}, device_id_type=MESH
+        )
         for target in self.flips:
             signal(target)
 
         @pl.when(self.edge)
         def _():
             signal(self.inward)
-            pl.semaphore_wait(barrier, 3)
+            pl.semaphore_wait(barrier, 4)
 
         @pl.when(self.middle)
         def _():
             signal(self.across)
             signal(self.outward)
-            pl.semaphore_wait(barrier, 4)
+            pl.semaphore_wait(barrier, 5)
+
+
+ADD_ROWS = 16
 
 
 def add_rows(held, start, other, rows):
-    held[pl.ds(start, rows), :] = (
-        held[pl.ds(start, rows), :].astype(jnp.float32) + other[...].astype(jnp.float32)
-    ).astype(jnp.bfloat16)
+    def add(index, carry):
+        own = pl.ds(pl.multiple_of(start + index * ADD_ROWS, ADD_ROWS), ADD_ROWS)
+        arrived = other[pl.ds(pl.multiple_of(index * ADD_ROWS, ADD_ROWS), ADD_ROWS), :]
+        held[own, :] = (held[own, :].astype(jnp.float32) + arrived.astype(jnp.float32)).astype(jnp.bfloat16)
+        return carry
+
+    lax.fori_loop(0, rows // ADD_ROWS, add, 0)
+
+
+class Vectors:
+    STEPS = 7
+
+    def __init__(self, links, source, output, stages, arrived, sent, got):
+        self.links, self.source, self.output = links, source, output
+        self.stages, self.arrived, self.sent, self.got = stages, arrived, sent, got
+
+    def copy(self, number, source, target):
+        return pltpu.make_async_remote_copy(
+            src_ref=source,
+            dst_ref=self.arrived.at[number],
+            send_sem=self.sent.at[number],
+            recv_sem=self.got.at[number],
+            device_id=target,
+            device_id_type=MESH,
+        )
+
+    def exchange(self, number):
+        links = self.links
+        targets = [
+            {"narrow": 1 - lax.axis_index("narrow")},
+            {"wide": links.flips[0]},
+            {"wide": links.flips[1]},
+            {"wide": links.inward},
+            {"wide": links.across},
+            {"wide": links.outward},
+        ]
+        source = self.source if number == 0 else self.stages.at[number]
+        return self.copy(number, source, targets[number])
+
+    def add(self, number):
+        source = self.source if number == 0 else self.stages.at[number]
+        self.stages[number + 1] = source[...] + self.arrived[number]
+
+    def step(self, number):
+        links = self.links
+        if number in (1, 2, 3):
+            self.exchange(number - 1).wait_recv()
+            self.add(number - 1)
+        if number < 3:
+            self.exchange(number).start()
+        if number == 3:
+
+            @pl.when(links.edge)
+            def _():
+                self.exchange(3).start()
+
+        if number in (4, 5):
+
+            @pl.when(links.middle)
+            def _():
+                self.exchange(number - 1).wait_recv()
+                self.add(number - 1)
+                self.exchange(number).start()
+
+        if number == 6:
+
+            @pl.when(links.middle)
+            def _():
+                self.output[...] = self.stages[5]
+
+            @pl.when(links.edge)
+            def _():
+                self.exchange(5).wait_recv()
+                self.output[...] = self.arrived[5]
+
+    def close(self):
+        for number in range(3):
+            self.exchange(number).wait_send()
+
+        @pl.when(self.links.edge)
+        def _():
+            self.exchange(3).wait_send()
+
+        @pl.when(self.links.middle)
+        def _():
+            self.exchange(4).wait_send()
+            self.exchange(5).wait_send()
 
 
 class Chunk:
@@ -531,9 +621,12 @@
 
 def sum_kernel(jobs, *refs):
     count = len(jobs)
-    inputs, outputs, scratch = refs[:count], refs[count : 2 * count], refs[2 * count :]
+    inputs, refs = refs[: count + 1], refs[count + 1 :]
+    outputs, scratch = refs[: count + 1], refs[count + 1 :]
+    scratch, vector_scratch = scratch[:-4], scratch[-4:]
     per_job = len(scratch) // count
     links = Links()
+    vectors = Vectors(links, inputs[count], outputs[count], *vector_scratch)
     items = []
     for number, job in enumerate(jobs):
         own = scratch[number * per_job : (number + 1) * per_job]
@@ -545,6 +638,8 @@
             items.append((pair, load))
     links.greet()
     for tick in range(len(items) + Chunk.STEPS - 1):
+        if tick < Vectors.STEPS:
+            vectors.step(tick)
         for place, (pair, load) in enumerate(items):
             step = tick - place
             if 0 <= step < Chunk.STEPS:
@@ -555,25 +650,33 @@
     for pair, _ in items:
         for chunk in pair:
             chunk.close()
-
-
-def summed_over_wide(gradients, chunk_rows, collective_id):
+    vectors.close()
+
+
+def summed_over_wide(gradients, chunk_rows, vectors, collective_id):
     jobs = [Job(g.shape[0], g.shape[1], r) for g, r in zip(gradients, chunk_rows)]
     scratch = []
     for job in jobs:
         scratch += scratch_for(job)
+    scratch += [
+        pltpu.VMEM((6, *vectors.shape), jnp.float32),
+        pltpu.VMEM((6, *vectors.shape), jnp.float32),
+        pltpu.SemaphoreType.DMA((6,)),
+        pltpu.SemaphoreType.DMA((6,)),
+    ]
     sent = sum(2 * g.size * 5 // 4 for g in gradients)
     return pl.pallas_call(
         functools.partial(sum_kernel, jobs),
-        out_shape=[jax.ShapeDtypeStruct(g.shape, jnp.bfloat16) for g in gradients],
-        in_specs=[pl.BlockSpec(memory_space=pl.ANY)] * len(jobs),
-        out_specs=[pl.BlockSpec(memory_space=pl.ANY)] * len(jobs),
+        out_shape=[jax.ShapeDtypeStruct(g.shape, jnp.bfloat16) for g in gradients]
+        + [jax.ShapeDtypeStruct(vectors.shape, jnp.float32)],
+        in_specs=[pl.BlockSpec(memory_space=pl.ANY)] * len(jobs) + [pl.BlockSpec(memory_space=pltpu.VMEM)],
+        out_specs=[pl.BlockSpec(memory_space=pl.ANY)] * len(jobs) + [pl.BlockSpec(memory_space=pltpu.VMEM)],
         scratch_shapes=scratch,
         compiler_params=pltpu.CompilerParams(
             collective_id=collective_id, has_side_effects=True, vmem_limit_bytes=60 * 1024 * 1024
         ),
         cost_estimate=pl.CostEstimate(flops=0, bytes_accessed=2 * sent, transcendentals=0),
-    )(*gradients)
+    )(*gradients, vectors)
 
 
 LANES = 128
@@ -744,42 +847,9 @@
     )(query_rows, key_rows, value_rows, mixed_rows, grad_mixed, logs, cosine, sine, mask)
 
 
-def wide_index(x, y, z):
-    return z * 4 + y * 2 + x
-
-
-def chip_positions():
-    return [(x, y, z) for z in range(PLANES) for y in range(2) for x in range(2)]
-
-
-def flip_pairs(axis):
-    if axis == "x":
-        return [(wide_index(x, y, z), wide_index(1 - x, y, z)) for x, y, z in chip_positions()]
-    return [(wide_index(x, y, z), wide_index(x, 1 - y, z)) for x, y, z in chip_positions()]
-
-
-def plane_pairs(moves):
-    return [
-        (wide_index(x, y, src), wide_index(x, y, dst))
-        for src, dst in moves
-        for y in range(2)
-        for x in range(2)
-    ]
-
-
-def send(values, pairs):
-    return lax.ppermute(values, "wide", pairs)
-
-
-def vector_sum(values):
-    values = values + partner(values)
-    values = values + send(values, flip_pairs("x"))
-    values = values + send(values, flip_pairs("y"))
-    values = values + send(values, plane_pairs(((0, 1), (3, 2))))
-    values = values + send(values, plane_pairs(((1, 2), (2, 1))))
-    plane = lax.axis_index("wide") // 4
-    outward = send(values, plane_pairs(((1, 0), (2, 3))))
-    return jnp.where((plane == 1) | (plane == 2), values, outward)
+NAMES = ("down", "gate", "up", "out", "query", "key", "value")
+CHUNK = {"down": 128, "gate": 64, "up": 64, "out": 128, "query": 128, "key": 128, "value": 128}
+SLOW = ("down", "gate")
 
 
 def partner(values):
@@ -901,16 +971,17 @@
         grad_normed_one, scaled_one, inverse_one, norm1_gain
     )
     token_grad = grad_resid + grad_in_one
-    norm_summed = vector_sum(
-        jnp.stack([gain_one_grad, shift_one_grad, gain_two_grad, shift_two_grad])
-    )
+    norm_grads = jnp.stack([gain_one_grad, shift_one_grad, gain_two_grad, shift_two_grad])
+    gradients = dict(zip(NAMES, [down_grad, gate_grad, up_grad, out_grad] + qkv_grads))
+    fast = [name for name in NAMES if name not in SLOW]
+    *fast_sums, norm_summed = summed_over_wide(
+        [gradients[n] for n in fast], [CHUNK[n] for n in fast], jnp.pad(norm_grads, ((0, 4), (0, 0))), 1
+    )
+    sums = dict(zip(fast, fast_sums))
+    for name in SLOW:
+        sums[name] = lax.psum(gradients[name], "wide")
     down_summed, gate_summed, up_summed, out_summed, query_summed, key_summed, value_summed = [
-        total.astype(jnp.float32)
-        for total in summed_over_wide(
-            [down_grad, gate_grad, up_grad, out_grad] + qkv_grads,
-            [128, 64, 64, 128, 128, 128, 128],
-            1,
-        )
+        sums[name].astype(jnp.float32) for name in NAMES
     ]
     return (
         out_values,

time: 496 us -> 452 us (0.911)
  Pallas kernels: 312 us -> 272 us
  between operations: 1.46 us -> 14.9 us
  starting transfers between devices: 10.4 us -> 1.5 us
  waiting for transfers between devices: 10.8 us -> 2.87 us
    pallas_call x1, Pallas kernels: 268 us -> 227 us  [summed_over_wide(): pl.pallas_call(functools.partial(sum_kernel, jobs), out_shape=[jax.ShapeD...]
    ppermute x5 -> x0, waiting for transfers between devices: 8.26 us -> none  [send(): return lax.ppermute(values, 'wide', pairs)]
    ppermute x5 -> x0, starting transfers between devices: 7.68 us -> none  [send(): return lax.ppermute(values, 'wide', pairs)]
  transfers between devices with their start and end apart: 14 -> 9, of which waited for: 3 -> 1; matrix products, arithmetic and copies ran while one was open for 20% -> 20% of each run, Pallas kernels for 59% -> 56%
where the time goes in v4:
time: 452 us; the launch traced here: 447 us
  Pallas kernels  272 us (60%)
  matrix products  110 us (24%)
  other arithmetic  36 us (8%)
  between operations  14.9 us (3%)
  local copies, waits for them, and re-layouts  10.3 us (2%)
    pallas_call x1, Pallas kernels, summed_over_wide(): pl.pallas_call(functools.partial(sum_kernel, jobs), out_shape=[jax.ShapeD...  227 us
    dot_general x7, matrix products, transpose_times(): lax.dot_general(left, right, (((0,), (0,)), ((), ())), preferred_element_...  33 us
    dot_general x12, matrix products, times_transpose(): lax.dot_general(left, right, (((1,), (1,)), ((), ())), preferred_element_...  30.8 us
    pallas_call x1, Pallas kernels, attend_back(): pl.pallas_call(attend_back_kernel, grid=(pairs,), in_specs=[wide_block] *...  23.8 us
    convert_element_type x7, other arithmetic, on_device(): sums[name].astype(jnp.float32)  23.4 us
    pallas_call x1, Pallas kernels, attend(): pl.pallas_call(attend_kernel, grid=(pairs,), in_specs=[wide_block] * 3 +...  20.6 us
    dot_general x1, matrix products, on_device(): jnp.dot(gathered_two, w_gate, preferred_element_type=jnp.float32)  17.1 us
  transfers between devices with their start and end apart: 9, of which 1 were waited for; matrix products, arithmetic and copies ran while one was open for 20% of the time, Pallas kernels for 56%

profile of v4, /device:TPU:0, one launch (start us, length us, event | category | flops | bytes accessed | tf_op | source)
XLA Modules:
  0.0 447.1 jit_solution(3849077106459594486)
XLA Ops:
  7.3 1.6 convert_reduce_fusion
  8.9 1.6 fusion.13
  10.5 1.4 fusion.7
  13.9 1.9 fusion.37
  15.8 3.1 fusion.70.key_raw
  18.9 2.9 fusion.69.value_raw
  21.8 2.8 fusion.71.query_raw
  24.6 20.6 %shard_map.246 = (bf16[1024,512]{1,0:T(8,128)(2,1)S(1)}, bf16[1024,512]{1,0:T(8,128)(2,1)S(1)}, bf16[1024,512]{1,0:T(8,128)(2,1)S(1)}, bf16[1024,512]{1,0:T(8,128)(2,1)S(1)}, f32[4,2,1024]{2,1,0:T(2,128)S(1)}) custom-call(f32[1024,512]{1,0:T(8,128)S(1)} %fusion.71.query_raw, f32[1024,512]{1,0:T(8,128)S(1)} %fusion.70.key_raw, ...), custom_call_target="tpu_custom_call" | custom-call | flops 2147483648 | bytes 10485760 | tf_op jit(solution)/shard_map/pallas_call | solution.py:763
  46.1 1.2 copy-done.24
  47.4 2.8 collective-permute-done.1
  50.3 0.8 fusion.74
  52.6 1.8 copy-done.39
  54.4 6.8 %fusion.75 = f32[1024,2048]{1,0:T(8,128)} fusion(bf16[1024,1024]{1,0:T(8,128)(2,1)S(1)} %constant_dynamic-update-slice_fusion, bf16[2048,1024]{1,0:T(8,128)(2,1)S(1)} %copy-done.39), kind=kOutput, calls=%fused_computation.131 | convolution fusion | flops 4294967296 | bytes 14680064 | tf_op jit(solution)/shard_map/dot_general | solution.py:21
  61.2 7.7 %fusion.67 = f32[1024,2048]{1,0:T(8,128)} fusion(bf16[1024,2048]{1,0:T(8,128)(2,1)S(1)} %copy-done.36, bf16[512,1024]{1,0:T(8,128)(2,1)S(1)} %collective-permute-done.2, bf16[512,1024]{1,0:T(8,128)(2,1)S(1)} %add_convert_fusion.1), kind=kOutput, calls=%fused_computation.123 | convolution fusion | flops 4299161600 | bytes 14680064 | tf_op jit(solution)/shard_map/dot_general | solution.py:922
  68.9 17.1 %multiply_convert_fusion.1 = (bf16[1024,2048]{1,0:T(8,128)(2,1)}, bf16[1024,2048]{1,0:T(8,128)(2,1)}, bf16[1024,2048]{1,0:T(8,128)(2,1)}) fusion(f32[1024,2048]{1,0:T(8,128)} %fusion.75, f32[1024,2048]{1,0:T(8,128)} %fusion.67, bf16[1024,2048]{1,0:T(8,128)(2,1)} %param.26, bf16[512,1024]{1,0:T(8,128)(2,1)S(1)} %collective-permute-done.2, ...), kind=kOutput, calls=%fused_computation.2 | convolution fusion | flops 4332716032 | bytes 35651584 | tf_op jit(solution)/shard_map/dot_general | solution.py:921
  86.0 6.3 %fusion.34 = bf16[512,1024]{1,0:T(8,128)(2,1)} fusion(bf16[2048,1024]{1,0:T(8,128)(2,1)} %param.28, bf16[1024,2048]{1,0:T(8,128)(2,1)} %get-tuple-element.54), kind=kOutput, calls=%fused_computation.59 | convolution fusion | flops 2148007936 | bytes 7340032 | tf_op jit(solution)/shard_map/dot_general | solution.py:927
  92.4 2.4 fusion.15
  94.8 1.1 copy-done.46
  95.9 3.7 fusion.31
  99.9 6.3 %convolution_convert_fusion.1 = bf16[1024,2048]{1,0:T(8,128)(2,1)} fusion(bf16[1024,2048]{1,0:T(8,128)(2,1)S(1)} %copy-done.46, bf16[512,1024]{1,0:T(8,128)(2,1)S(1)} %collective-permute-done.2, bf16[512,1024]{1,0:T(8,128)(2,1)S(1)} %add_convert_fusion.1), kind=kOutput, calls=%fused_computation.6 | convolution fusion | flops 4301258752 | bytes 10485760 | tf_op jit(solution)/shard_map/dot_general | solution.py:27
  106.3 6.4 %convolution_convert_fusion = bf16[2048,1024]{1,0:T(8,128)(2,1)} fusion(bf16[1024,2048]{1,0:T(8,128)(2,1)S(1)} %copy-done.44, bf16[1024,1024]{1,0:T(8,128)(2,1)S(1)} %constant_dynamic-update-slice_fusion), kind=kOutput, calls=%fused_computation.5 | convolution fusion | flops 4297064448 | bytes 10485760 | tf_op jit(solution)/shard_map/dot_general | solution.py:27
  112.7 5.3 %fusion.19 = f32[512,1024]{1,0:T(8,128)S(1)} fusion(bf16[1024,2048]{1,0:T(8,128)(2,1)} %param.27, bf16[1024,2048]{1,0:T(8,128)(2,1)} %get-tuple-element.55), kind=kOutput, calls=%fused_computation.30 | convolution fusion | flops 2147483648 | bytes 8388608 | tf_op jit(solution)/shard_map/dot_general | solution.py:21
  118.6 4.8 %multiply_reduce_fusion = (f32[1024]{0:T(1024)S(1)}, f32[512]{0:T(512)S(1)}, f32[512]{0:T(512)S(1)}, f32[1024]{0:T(1024)S(1)}, f32[512,1024]{1,0:T(8,128)S(1)}) fusion(f32[512,1024]{1,0:T(8,128)S(1)} %copy-done.14, f32[512]{0:T(512)S(1)} %add_rsqrt_fusion, f32[512]{0:T(512)S(1)} %broadcast_multiply_fusion.4, f32[1024]{0:T(1024)S(1)} %copy-done.32, ...), kind=kOutput, calls=%fused_computation.41 | convolution fusion | flops 2153247744 | bytes 14700544 | tf_op jit(solution)/shard_map/dot_general | solution.py:21
  123.4 2.1 fusion.72
  125.7 1.3 copy-done.49
  127.0 6.4 %convolution_convert_fusion.2.refs_0_ = bf16[1024,2048]{1,0:T(8,128)(2,1)} fusion(bf16[1024,2048]{1,0:T(8,128)(2,1)S(1)} %copy-done.49, bf16[512,1024]{1,0:T(8,128)(2,1)S(1)} %copy-done.42, bf16[512,1024]{1,0:T(8,128)(2,1)S(1)} %copy-done.30), kind=kOutput, calls=%fused_computation.7 | convolution fusion | flops 4301258752 | bytes 10485760 | tf_op jit(solution)/shard_map/dot_general | solution.py:27
  133.5 5.0 %convert_add_fusion.2 = f32[512,1024]{1,0:T(8,128)} fusion(bf16[512,1024]{1,0:T(8,128)(2,1)} %collective-permute-done.3, f32[512,1024]{1,0:T(8,128)S(1)} %copy-done.14, bf16[2048,1024]{1,0:T(8,128)(2,1)S(1)} %copy-done.40, bf16[1024,2048]{1,0:T(8,128)(2,1)S(1)} %copy-done.45), kind=kOutput, calls=%fused_computation.47 | convolution fusion | flops 2149056512 | bytes 11534336 | tf_op jit(solution)/shard_map/dot_general | solution.py:932
  138.5 1.3 convolution_convert_fusion.7.grad_mixed
  140.6 23.8 %shard_map.247 = (bf16[1024,512]{1,0:T(8,128)(2,1)S(1)}, bf16[1024,512]{1,0:T(8,128)(2,1)S(1)}, bf16[1024,512]{1,0:T(8,128)(2,1)S(1)}) custom-call(bf16[1024,512]{1,0:T(8,128)(2,1)S(1)} %copy-done.4, bf16[1024,512]{1,0:T(8,128)(2,1)S(1)} %copy-done.6, bf16[1024,512]{1,0:T(8,128)(2,1)S(1)} %copy-done.8, bf16[1024,512]{1,0:T(8,128)(2,1)S(1)} %get-tuple-element.27.mixed_rows, ...), custom_call_target="tpu_custom_call" | custom-call | flops 5368709120 | bytes 8388608 | tf_op jit(solution)/shard_map/pallas_call | solution.py:830
  164.5 0.7 fusion.41
  165.7 0.7 fusion.39
  166.5 0.8 add_convert_fusion
  168.1 0.7 fusion.44
  168.8 3.8 convolution_convert_fusion.5.refs_2_
  172.6 2.3 convolution_convert_fusion.6.refs_1_
  174.9 3.9 convolution_convert_fusion.4.refs_3_
  178.8 3.9 convolution_convert_fusion.3.refs_4_
  182.7 2.8 fusion.12
  186.1 227.1 %shard_map.248 = (bf16[1024,2048]{1,0:T(8,128)(2,1)}, bf16[512,1024]{1,0:T(8,128)(2,1)}, bf16[1024,512]{1,0:T(8,128)(2,1)}, bf16[1024,512]{1,0:T(8,128)(2,1)}, b...) custom-call(bf16[1024,2048]{1,0:T(8,128)(2,1)} %convolution_convert_fusion.2.refs_0_, ...), custom_call_target="tpu_custom_call" | custom-call | bytes 20971520 | tf_op jit(solution)/shard_map/pallas_call | solution.py:668
  413.2 2.9 convert_element_type.118
  416.1 1.6 convert_element_type.119
  417.7 1.6 convert_element_type.120
  419.3 1.6 convert_element_type.121
  420.9 0.9 copy-done.18
  421.7 4.5 convert_element_type.124
  426.8 2.0 fusion.11
  428.9 6.8 %convert_element_type.123 = f32[1024,2048]{1,0:T(8,128)} convert(bf16[1024,2048]{1,0:T(8,128)(2,1)} %get-tuple-element.49) | non-fusion elementwise | flops 2097152 | bytes 12582912 | tf_op jit(solution)/shard_map/convert_element_type | solution.py:984
  435.7 4.4 convert_element_type.126
  (142 shorter events, 9.0 us)
Async XLA Ops:
  7.2 11.7 %copy-start = (bf16[1024,512]{1,0:T(8,128)(2,1)S(1)}, bf16[1024,512]{1,0:T(8,128)(2,1)}, u32[]{:S(2)}) copy-start(bf16[1024,512]{1,0:T(8,128)(2,1)} %param.22) | copy-start | bytes 3145732
  7.2 3.3 copy-start.10
  7.2 3.3 copy-start.31
  7.2 3.3 copy-start.34
  7.2 5.3 %copy-start.9 = (s32[2]{0:T(128)S(1)}, s32[2]{0:T(128)}, u32[]{:S(2)}) copy-start(s32[2]{0:T(128)} %param.17) | copy-start | bytes 28
  7.2 421.6 %all-reduce.4.cloned.1.call-start = ((), (), s32[]{:S(2)}) async-start(), calls=%async_computation | async-start | bytes 16777216 | tf_op jit(solution)/shard_map/psum | solution.py:982
  8.8 4.4 copy-start.43
  12.0 3.8 collective-permute-start
  13.8 10.7 %copy-start.1 = (f32[1024,2]{1,0:T(8,128)}, f32[1024,2]{1,0:T(8,128)S(1)}, u32[]{:S(2)}) copy-start(f32[1024,2]{1,0:T(8,128)S(1)} %fusion.53.mask) | copy-start | bytes 24580
  18.9 2.9 copy-start.21
  24.6 20.7 %copy-start.19 = (bf16[512,1024]{1,0:T(8,128)(2,1)S(1)}, bf16[512,1024]{1,0:T(8,128)(2,1)}, u32[]{:S(2)}) copy-start(bf16[512,1024]{1,0:T(8,128)(2,1)} %param.23) | copy-start | bytes 3145732
  45.3 2.1 copy-start.3
  45.3 2.1 copy-start.5
  45.3 2.1 copy-start.7
  45.3 5.0 %copy-start.11 = (bf16[512,1024]{1,0:T(8,128)(2,1)S(1)}, bf16[512,1024]{1,0:T(8,128)(2,1)}, u32[]{:S(2)}) copy-start(bf16[512,1024]{1,0:T(8,128)(2,1)} %param.15) | copy-start | bytes 3145732
  46.0 4.2 collective-permute-start.1
  47.3 5.3 %collective-permute-start.4 = (bf16[512,1024]{1,0:T(8,128)(2,1)S(1)}, bf16[512,1024]{1,0:T(8,128)(2,1)S(1)}, u32[]{:S(2)}, u32[]{:S(2)}) collective-permute-start(bf16[512,1024]{1,0:T(8,128)(2,1)S(1)} %copy-done.24), channel_id=1, source_target_pairs={{0,1},{1,0},{2,3},{3,2},{4,5},{5,4},{6,7},{7,6},{8,9},{9,8},{10,11... | collective-permute-start | bytes 3145736 | tf_op jit(solution)/shard_map/ppermute | solution.py:856
  51.9 2.6 copy-start.39
  52.4 47.5 %copy-start.29 = (bf16[512,1024]{1,0:T(8,128)(2,1)}, bf16[512,1024]{1,0:T(8,128)(2,1)S(1)}, u32[]{:S(2)}) copy-start(bf16[512,1024]{1,0:T(8,128)(2,1)S(1)} %add_convert_fusion.1) | copy-start | bytes 3145732
  52.4 8.8 %collective-permute-start.2 = (bf16[512,1024]{1,0:T(8,128)(2,1)S(1)}, bf16[512,1024]{1,0:T(8,128)(2,1)S(1)}, u32[]{:S(2)}, u32[]{:S(2)}) collective-permute-start(bf16[512,1024]{1,0:T(8,128)(2,1)S(1)} %add_convert_fusion.1), channel_id=1, source_target_pairs={{0,1},{1,0},{2,3},{3,2},{4,5},{5,4},{6,7},{7,6},{8,9},{9,8},{10,11... | collective-permute-start | bytes 3145736 | tf_op jit(solution)/shard_map/ppermute | solution.py:856
  54.4 6.8 %copy-start.36 = (bf16[1024,2048]{1,0:T(8,128)(2,1)S(1)}, bf16[1024,2048]{1,0:T(8,128)(2,1)}, u32[]{:S(2)}) copy-start(bf16[1024,2048]{1,0:T(8,128)(2,1)} %param.27) | copy-start | bytes 12582916
  61.2 38.7 %copy-start.41 = (bf16[512,1024]{1,0:T(8,128)(2,1)}, bf16[512,1024]{1,0:T(8,128)(2,1)S(1)}, u32[]{:S(2)}) copy-start(bf16[512,1024]{1,0:T(8,128)(2,1)S(1)} %collective-permute-done.2) | copy-start | bytes 3145732
  86.0 6.4 %copy-start.48 = (bf16[1024,2048]{1,0:T(8,128)(2,1)S(1)}, bf16[1024,2048]{1,0:T(8,128)(2,1)}, u32[]{:S(2)}) copy-start(bf16[1024,2048]{1,0:T(8,128)(2,1)} %get-tuple-element.55) | copy-start | bytes 12582916
  92.3 41.2 %collective-permute-start.3 = (bf16[512,1024]{1,0:T(8,128)(2,1)}, bf16[512,1024]{1,0:T(8,128)(2,1)}, u32[]{:S(2)}, u32[]{:S(2)}) collective-permute-start(bf16[512,1024]{1,0:T(8,128)(2,1)} %fusion.34), channel_id=1, source_target_pairs={{0,1},{1,0},{2,3},{3,2},{4,5},{5,4},{6,7},{7,6},{8,9},{9,8},{10,11... | collective-permute-start | bytes 3145736 | tf_op jit(solution)/shard_map/ppermute | solution.py:856
  92.4 2.4 copy-start.37
  92.4 3.5 copy-start.46
  99.6 6.7 %copy-start.44 = (bf16[1024,2048]{1,0:T(8,128)(2,1)S(1)}, bf16[1024,2048]{1,0:T(8,128)(2,1)}, u32[]{:S(2)}) copy-start(bf16[1024,2048]{1,0:T(8,128)(2,1)} %get-tuple-element.54) | copy-start | bytes 12582916
  99.6 18.5 %collective-permute-start.5 = (f32[512,1024]{1,0:T(8,128)}, f32[512,1024]{1,0:T(8,128)}, u32[]{:S(2)}, u32[]{:S(2)}) collective-permute-start(f32[512,1024]{1,0:T(8,128)} %fusion.31), channel_id=1, source_target_pairs={{0,1},{1,0},{2,3},{3,2},{4,5},{5,4},{6,7},{7,6},{8,9},{9,8},{10,11... | collective-permute-start | bytes 6291464 | tf_op jit(solution)/shard_map/ppermute | solution.py:856
  112.7 5.4 %copy-start.14 = (f32[512,1024]{1,0:T(8,128)S(1)}, f32[512,1024]{1,0:T(8,128)}, u32[]{:S(2)}) copy-start(f32[512,1024]{1,0:T(8,128)} %copy-done.13) | copy-start | bytes 6291460
  112.7 5.4 %copy-start.38 = (bf16[1024,2048]{1,0:T(8,128)(2,1)S(1)}, bf16[1024,2048]{1,0:T(8,128)(2,1)}, u32[]{:S(2)}) copy-start(bf16[1024,2048]{1,0:T(8,128)(2,1)} %param.26) | copy-start | bytes 12582916
  112.7 5.9 %copy-start.47 = (bf16[1024,2048]{1,0:T(8,128)(2,1)S(1)}, bf16[1024,2048]{1,0:T(8,128)(2,1)}, u32[]{:S(2)}) copy-start(bf16[1024,2048]{1,0:T(8,128)(2,1)} %get-tuple-element.53) | copy-start | bytes 12582916
  118.0 5.3 %copy-start.25 = (bf16[512,1024]{1,0:T(8,128)(2,1)S(1)}, bf16[512,1024]{1,0:T(8,128)(2,1)}, u32[]{:S(2)}) copy-start(bf16[512,1024]{1,0:T(8,128)(2,1)} %param.29) | copy-start | bytes 3145732
  123.4 2.3 copy-start.30
  123.4 2.3 copy-start.42
  123.4 3.6 copy-start.49
  125.5 7.9 %copy-start.40 = (bf16[2048,1024]{1,0:T(8,128)(2,1)S(1)}, bf16[2048,1024]{1,0:T(8,128)(2,1)}, u32[]{:S(2)}) copy-start(bf16[2048,1024]{1,0:T(8,128)(2,1)} %param.28) | copy-start | bytes 12582916
  125.5 7.9 %copy-start.45 = (bf16[1024,2048]{1,0:T(8,128)(2,1)S(1)}, bf16[1024,2048]{1,0:T(8,128)(2,1)}, u32[]{:S(2)}) copy-start(bf16[1024,2048]{1,0:T(8,128)(2,1)} %get-tuple-element.54) | copy-start | bytes 12582916
  125.5 13.0 %collective-permute-start.6 = (bf16[512,1024]{1,0:T(8,128)(2,1)S(1)}, bf16[512,1024]{1,0:T(8,128)(2,1)S(1)}, u32[]{:S(2)}, u32[]{:S(2)}) collective-permute-start(bf16[512,1024]{1,0:T(8,128)(2,1)S(1)} %get-tuple-element.51), channel_id=1, source_target_pairs={{0,1},{1,0},{2,3},{3,2},{4,5},{5,4},{6,7},{7,6},{8,9},{9,8},{10,11... | collective-permute-start | bytes 3145736 | tf_op jit(solution)/shard_map/ppermute | solution.py:856
  133.4 5.1 %copy-start.20 = (bf16[512,1024]{1,0:T(8,128)(2,1)S(1)}, bf16[512,1024]{1,0:T(8,128)(2,1)}, u32[]{:S(2)}) copy-start(bf16[512,1024]{1,0:T(8,128)(2,1)} %param.23) | copy-start | bytes 3145732
  140.6 23.8 %copy-start.22 = (bf16[1024,512]{1,0:T(8,128)(2,1)S(1)}, bf16[1024,512]{1,0:T(8,128)(2,1)}, u32[]{:S(2)}) copy-start(bf16[1024,512]{1,0:T(8,128)(2,1)} %param.20) | copy-start | bytes 3145732
  167.2 15.4 %collective-permute-start.7 = (bf16[512,1024]{1,0:T(8,128)(2,1)S(1)}, bf16[512,1024]{1,0:T(8,128)(2,1)S(1)}, u32[]{:S(2)}, u32[]{:S(2)}) collective-permute-start(bf16[512,1024]{1,0:T(8,128)(2,1)S(1)} %add_convert_fusion), channel_id=1, source_target_pairs={{0,1},{1,0},{2,3},{3,2},{4,5},{5,4},{6,7},{7,6},{8,9},{9,8},{10,11... | collective-permute-start | bytes 3145736 | tf_op jit(solution)/shard_map/ppermute | solution.py:856
  178.8 3.9 copy-start.12
  413.2 2.9 copy-start.28
  417.7 4.0 copy-start.18
  421.7 4.5 copy-start.33
  421.7 5.1 %copy-start.15 = (f32[512,1024]{1,0:T(8,128)S(1)}, f32[512,1024]{1,0:T(8,128)}, u32[]{:S(2)}) copy-start(f32[512,1024]{1,0:T(8,128)} %get-tuple-element.52) | copy-start | bytes 6291460
  421.7 5.1 %copy-start.16 = (f32[512,1024]{1,0:T(8,128)S(1)}, f32[512,1024]{1,0:T(8,128)}, u32[]{:S(2)}) copy-start(f32[512,1024]{1,0:T(8,128)} %get-tuple-element.65) | copy-start | bytes 6291460
  428.9 6.8 %copy-start.17 = (bf16[2048,1024]{1,0:T(8,128)(2,1)S(1)}, bf16[2048,1024]{1,0:T(8,128)(2,1)}, u32[]{:S(2)}) copy-start(bf16[2048,1024]{1,0:T(8,128)(2,1)} %get-tuple-element.50) | copy-start | bytes 12582916
  (11 other events, 16.0 us)
Sparse Core Ops, SparseCore 0:
  112.8 314.5 all-reduce.3

commit v5 on v4

--- a/solution.py
+++ b/solution.py
@@ -852,6 +852,75 @@
 SLOW = ("down", "gate")
 
 
+HIDDEN_TILE = 256
+
+
+def feed_kernel(
+    rows, cots, gate_w, up_w, down_w, out_own, out_other, back_own, back_other, down_grad, gate_grad, grad_up, rows_t, out_sum, back_sum
+):
+    step = pl.program_id(0)
+
+    @pl.when(step == 0)
+    def _():
+        rows_t[...] = rows[...].T
+        out_sum[...] = jnp.zeros_like(out_sum)
+        back_sum[...] = jnp.zeros_like(back_sum)
+
+    gate = nn_dot(rows[...], gate_w[...])
+    sigmoid = 1.0 / (1.0 + jnp.exp(-gate))
+    silu = gate * sigmoid
+    up = nn_dot(rows[...], up_w[...])
+    hidden = (silu * up).astype(jnp.bfloat16)
+    grad_hidden = nt_dot(cots[...], down_w[...])
+    gate_back = (grad_hidden * up * (sigmoid * (1.0 + gate * (1.0 - sigmoid)))).astype(jnp.bfloat16)
+    up_back = (grad_hidden * silu).astype(jnp.bfloat16)
+    grad_up[...] = up_back
+    down_grad[...] = nn_dot(hidden.T, cots[...]).astype(jnp.bfloat16)
+    gate_grad[...] = nn_dot(rows_t[...], gate_back).astype(jnp.bfloat16)
+    out_sum[...] += nn_dot(hidden, down_w[...])
+    back_sum[...] += nt_dot(gate_back, gate_w[...]) + nt_dot(up_back, up_w[...])
+
+    @pl.when(step == pl.num_programs(0) - 1)
+    def _():
+        half = rows.shape[0] // 2
+        out_own[...] = out_sum[:half]
+        out_other[...] = out_sum[half:].astype(jnp.bfloat16)
+        back_own[...] = back_sum[:half]
+        back_other[...] = back_sum[half:]
+
+
+def feed_forward(rows, cots, gate_w, up_w, down_w):
+    count, width = rows.shape
+    hidden = gate_w.shape[1]
+    whole = pl.BlockSpec((count, width), lambda tile: (0, 0))
+    half = pl.BlockSpec((count // 2, width), lambda tile: (0, 0))
+    columns = pl.BlockSpec((width, HIDDEN_TILE), lambda tile: (0, tile))
+    lines = pl.BlockSpec((HIDDEN_TILE, width), lambda tile: (tile, 0))
+    half_wide = jax.ShapeDtypeStruct((count // 2, width), jnp.float32)
+    half_low = jax.ShapeDtypeStruct((count // 2, width), jnp.bfloat16)
+    return pl.pallas_call(
+        feed_kernel,
+        grid=(hidden // HIDDEN_TILE,),
+        in_specs=[whole, whole, columns, columns, lines],
+        out_specs=[half, half, half, half, lines, columns, pl.BlockSpec((count, HIDDEN_TILE), lambda tile: (0, tile))],
+        out_shape=[half_wide, half_low, half_wide, half_wide]
+        + [
+            jax.ShapeDtypeStruct((hidden, width), jnp.bfloat16),
+            jax.ShapeDtypeStruct((width, hidden), jnp.bfloat16),
+            jax.ShapeDtypeStruct((count, hidden), jnp.bfloat16),
+        ],
+        scratch_shapes=[
+            pltpu.VMEM((width, count), jnp.bfloat16),
+            pltpu.VMEM((count, width), jnp.float32),
+            pltpu.VMEM((count, width), jnp.float32),
+        ],
+        compiler_params=pltpu.CompilerParams(vmem_limit_bytes=52 * 1024 * 1024),
+        cost_estimate=pl.CostEstimate(
+            flops=16 * count * width * hidden, bytes_accessed=12 * width * hidden + 16 * count * width, transcendentals=count * hidden
+        ),
+    )(rows, cots, gate_w, up_w, down_w)
+
+
 def partner(values):
     return lax.ppermute(values, "narrow", [(0, 1), (1, 0)])
 
@@ -918,32 +987,12 @@
     normed_two, scaled_two, inverse_two = norm_forward(resid_values, norm2_gain, norm2_shift)
     normed_two = normed_two.astype(jnp.bfloat16)
     gathered_two = rows_of(normed_two, partner(normed_two))
-    gate_values = jnp.dot(gathered_two, w_gate, preferred_element_type=jnp.float32)
-    up_values = jnp.dot(gathered_two, w_up, preferred_element_type=jnp.float32)
-    sigmoid_gate = jax.nn.sigmoid(gate_values)
-    hidden_rows = (gate_values * sigmoid_gate * up_values).astype(jnp.bfloat16)
-    down_grad = transpose_times(hidden_rows, cot_rows).astype(jnp.bfloat16)
-
-    out_other = jnp.dot(
-        hidden_rows[block_rows:], w_down, preferred_element_type=jnp.float32
-    ).astype(jnp.bfloat16)
-    out_values = (
-        resid_values
-        + jnp.dot(hidden_rows[:block_rows], w_down, preferred_element_type=jnp.float32)
-        + partner(out_other).astype(jnp.float32)
-    )
-    grad_hidden = times_transpose(cot_rows, w_down)
-    silu_grad = sigmoid_gate * (1.0 + gate_values * (1.0 - sigmoid_gate))
-    grad_gate = (grad_hidden * up_values * silu_grad).astype(jnp.bfloat16)
-    grad_up = (grad_hidden * gate_values * sigmoid_gate).astype(jnp.bfloat16)
-    gate_grad = transpose_times(gathered_two, grad_gate).astype(jnp.bfloat16)
+    out_own, out_other, grad_two_own, grad_two_other, down_grad, gate_grad, grad_up = feed_forward(
+        gathered_two, cot_rows, w_gate, w_up, w_down
+    )
     up_grad = transpose_times(gathered_two, grad_up).astype(jnp.bfloat16)
-
-    def grad_two_share(rows):
-        return times_transpose(grad_gate[rows], w_gate) + times_transpose(grad_up[rows], w_up)
-
-    grad_two_other = grad_two_share(slice(block_rows, None))
-    grad_normed_two = grad_two_share(slice(0, block_rows)) + partner(grad_two_other)
+    out_values = resid_values + out_own + partner(out_other).astype(jnp.float32)
+    grad_normed_two = grad_two_own + partner(grad_two_other)
     grad_in_two, gain_two_grad, shift_two_grad = norm_backward(
         grad_normed_two, scaled_two, inverse_two, norm2_gain
     )

time: 452 us -> 438 us (0.969)
  matrix products: 110 us -> 38.2 us
  Pallas kernels: 272 us -> 310 us
  waiting for transfers between devices: 2.87 us -> 15.6 us
  other arithmetic: 36 us -> 43.5 us
    pallas_call x0 -> x1, Pallas kernels: none -> 45.8 us  [feed_forward(): pl.pallas_call(feed_kernel, grid=(hidden // HIDDEN_TILE,), in_specs=[whol...]
    dot_general x4 -> x0, matrix products: 36.1 us -> none  [the longest x1 17.1 us: on_device(): jnp.dot(gathered_two, w_gate, preferred_element_type=jnp.float32)]
    dot_general x12 -> x7, matrix products: 30.8 us -> 7.77 us  [times_transpose(): lax.dot_general(left, right, (((1,), (1,)), ((), ())), preferred_element_...]
    dot_general x7 -> x5, matrix products: 33 us -> 20.1 us  [transpose_times(): lax.dot_general(left, right, (((0,), (0,)), ((), ())), preferred_element_...]
    psum x1, waiting for transfers between devices: 0.01 us -> 7.75 us  [on_device(): sums[name] = lax.psum(gradients[name], 'wide')]
    pallas_call x1, Pallas kernels: 227 us -> 220 us  [summed_over_wide(): pl.pallas_call(functools.partial(sum_kernel, jobs), out_shape=[jax.ShapeD...]
    ppermute x8, waiting for transfers between devices: 2.85 us -> 7.84 us  [partner(): return lax.ppermute(values, 'narrow', [(0, 1), (1, 0)])]
  transfers between devices with their start and end apart: 9 -> 9, of which waited for: 1 -> 4; matrix products, arithmetic and copies ran while one was open for 20% -> 13% of each run, Pallas kernels for 56% -> 56%
where the time goes in v5:
time: 438 us; the launch traced here: 434 us
  Pallas kernels  310 us (71%)
  other arithmetic  43.5 us (10%)
  matrix products  38.2 us (9%)
  waiting for transfers between devices  15.6 us (4%)
  between operations  14.8 us (3%)
  local copies, waits for them, and re-layouts  9.82 us (2%)
    pallas_call x1, Pallas kernels, summed_over_wide(): pl.pallas_call(functools.partial(sum_kernel, jobs), out_shape=[jax.ShapeD...  220 us
    pallas_call x1, Pallas kernels, feed_forward(): pl.pallas_call(feed_kernel, grid=(hidden // HIDDEN_TILE,), in_specs=[whol...  45.8 us
    convert_element_type x7, other arithmetic, on_device(): sums[name].astype(jnp.float32)  23.4 us
    pallas_call x1, Pallas kernels, attend_back(): pl.pallas_call(attend_back_kernel, grid=(pairs,), in_specs=[wide_block] *...  23.4 us
    pallas_call x1, Pallas kernels, attend(): pl.pallas_call(attend_kernel, grid=(pairs,), in_specs=[wide_block] * 3 +...  20.4 us
    dot_general x5, matrix products, transpose_times(): lax.dot_general(left, right, (((0,), (0,)), ((), ())), preferred_element_...  20.1 us
  transfers between devices with their start and end apart: 9, of which 4 were waited for; matrix products, arithmetic and copies ran while one was open for 13% of the time, Pallas kernels for 56%

profile of v5, /device:TPU:0, one launch (start us, length us, event | category | flops | bytes accessed | tf_op | source)
XLA Modules:
  0.0 433.6 jit_solution(10216914004521118803)
XLA Ops:
  7.3 1.6 convert_reduce_fusion
  8.9 1.6 fusion.13
  10.5 1.4 fusion.7
  12.6 0.6 gather_fusion
  13.9 1.9 fusion.15
  15.8 3.1 fusion.46.key_raw
  18.9 2.9 fusion.45.value_raw
  21.8 2.8 fusion.47.query_raw
  24.6 20.4 %shard_map.246 = (bf16[1024,512]{1,0:T(8,128)(2,1)S(1)}, bf16[1024,512]{1,0:T(8,128)(2,1)S(1)}, bf16[1024,512]{1,0:T(8,128)(2,1)S(1)}, bf16[1024,512]{1,0:T(8,128)(2,1)S(1)}, f32[4,2,1024]{2,1,0:T(2,128)S(1)}) custom-call(f32[1024,512]{1,0:T(8,128)S(1)} %fusion.47.query_raw, f32[1024,512]{1,0:T(8,128)S(1)} %fusion.46.key_raw, ...), custom_call_target="tpu_custom_call" | custom-call | flops 2147483648 | bytes 10485760 | tf_op jit(solution)/shard_map/pallas_call | solution.py:763
  45.1 0.7 fusion.26
  45.9 1.2 copy-done.27
  47.1 2.9 collective-permute-done.1
  50.0 0.9 fusion.50
  52.4 1.5 pad_maximum_fusion.2.cots
  53.9 1.0 collective-permute-done.2
  54.9 1.0 copy-done.33
  55.9 1.5 pad_maximum_fusion.1.rows
  57.4 45.8 %shard_map.247 = (f32[512,1024]{1,0:T(8,128)}, bf16[512,1024]{1,0:T(8,128)(2,1)S(1)}, f32[512,1024]{1,0:T(8,128)}, f32[512,1024]{1,0:T(8,128)}, bf16[2048,1024]{...) custom-call(bf16[1024,1024]{1,0:T(8,128)(2,1)} %pad_maximum_fusion.1.rows, ...), custom_call_target="tpu_custom_call" | custom-call | flops 34359738368 | bytes 41943040 | tf_op jit(solution)/shard_map/pallas_call | solution.py:901
  103.1 1.0 copy-done.3
  104.7 3.9 collective-permute-done.5
  108.6 4.0 multiply_reduce_fusion
  112.6 0.9 copy-done.29
  113.5 2.6 fusion.48
  116.2 1.7 copy-done.41
  117.9 6.2 %convolution_convert_fusion.refs_0_ = bf16[1024,2048]{1,0:T(8,128)(2,1)} fusion(bf16[1024,2048]{1,0:T(8,128)(2,1)S(1)} %copy-done.41, bf16[512,1024]{1,0:T(8,128)(2,1)S(1)} %copy-done.34, bf16[512,1024]{1,0:T(8,128)(2,1)S(1)} %copy-done.26), kind=kOutput, calls=%fused_computation.1 | convolution fusion | flops 4301258752 | bytes 10485760 | tf_op jit(solution)/shard_map/dot_general | solution.py:27
  124.2 1.3 convolution_convert_fusion.5.grad_mixed
  126.2 23.4 %shard_map.248 = (bf16[1024,512]{1,0:T(8,128)(2,1)S(1)}, bf16[1024,512]{1,0:T(8,128)(2,1)S(1)}, bf16[1024,512]{1,0:T(8,128)(2,1)S(1)}) custom-call(bf16[1024,512]{1,0:T(8,128)(2,1)S(1)} %copy-done.5, bf16[1024,512]{1,0:T(8,128)(2,1)S(1)} %copy-done.7, bf16[1024,512]{1,0:T(8,128)(2,1)S(1)} %copy-done.9, bf16[1024,512]{1,0:T(8,128)(2,1)S(1)} %get-tuple-element.34.mixed_rows, ...), custom_call_target="tpu_custom_call" | custom-call | flops 5368709120 | bytes 8388608 | tf_op jit(solution)/shard_map/pallas_call | solution.py:830
  149.6 0.7 fusion.19
  150.8 0.7 fusion.17
  151.5 0.7 add_convert_fusion
  152.6 0.7 fusion.24
  153.3 0.7 fusion.22
  154.1 3.8 convolution_convert_fusion.3.refs_2_
  157.9 2.2 convolution_convert_fusion.4.refs_1_
  160.1 3.8 convolution_convert_fusion.2.refs_3_
  163.9 4.0 convolution_convert_fusion.1.refs_4_
  167.9 2.8 fusion.12
  171.3 220.5 %shard_map.249 = (bf16[1024,2048]{1,0:T(8,128)(2,1)}, bf16[512,1024]{1,0:T(8,128)(2,1)}, bf16[1024,512]{1,0:T(8,128)(2,1)}, bf16[1024,512]{1,0:T(8,128)(2,1)}, b...) custom-call(bf16[1024,2048]{1,0:T(8,128)(2,1)} %convolution_convert_fusion.refs_0_, ...), custom_call_target="tpu_custom_call" | custom-call | bytes 20971520 | tf_op jit(solution)/shard_map/pallas_call | solution.py:668
  391.8 2.9 convert_element_type.96
  394.7 1.6 convert_element_type.97
  396.4 1.6 convert_element_type.98
  398.0 1.6 convert_element_type.99
  399.6 0.8 copy-done.19
  400.4 4.4 %convert_element_type.101 = f32[1024,2048]{1,0:T(8,128)} convert(bf16[1024,2048]{1,0:T(8,128)(2,1)S(1)} %copy-done.19) | non-fusion elementwise | flops 2097152 | bytes 12582912 | tf_op jit(solution)/shard_map/convert_element_type | solution.py:1033
  405.5 2.0 fusion.11
  407.5 7.8 %all-reduce.4.cloned.1.call-done = (bf16[1024,2048]{1,0:T(8,128)(2,1)}, bf16[2048,1024]{1,0:T(8,128)(2,1)}) async-done(((bf16[1024,2048]{1,0:T(8,128)(2,1)}, bf16[2048,1024]{1,0:T(8,128)(2,1)}), (bf16[1024,2048]{1,0:T(8,128)(2,1)}, bf16[2048,1024]{1,0:T(8,128)(2,1)})) %all-reduce.4.cloned.1.call-update) | async-done | bytes 8388624 | tf_op jit(solution)/shard_map/psum | solution.py:1031
  415.3 6.8 %convert_element_type.100 = f32[1024,2048]{1,0:T(8,128)} convert(bf16[1024,2048]{1,0:T(8,128)(2,1)} %get-tuple-element.63) | non-fusion elementwise | flops 2097152 | bytes 12582912 | tf_op jit(solution)/shard_map/convert_element_type | solution.py:1033
  422.1 4.4 %convert_element_type.102 = f32[2048,1024]{1,0:T(8,128)} convert(bf16[2048,1024]{1,0:T(8,128)(2,1)S(1)} %copy-done.18) | non-fusion elementwise | flops 2097152 | bytes 12582912 | tf_op jit(solution)/shard_map/convert_element_type | solution.py:1033
  (117 shorter events, 6.2 us)
Async XLA Ops:
  7.2 11.7 %copy-start = (bf16[1024,512]{1,0:T(8,128)(2,1)S(1)}, bf16[1024,512]{1,0:T(8,128)(2,1)}, u32[]{:S(2)}) copy-start(bf16[1024,512]{1,0:T(8,128)(2,1)} %param.22) | copy-start | bytes 3145732
  7.2 3.3 copy-start.13
  7.2 3.3 copy-start.36
  7.2 3.3 copy-start.38
  7.2 5.3 %copy-start.10 = (s32[2]{0:T(128)S(1)}, s32[2]{0:T(128)}, u32[]{:S(2)}) copy-start(s32[2]{0:T(128)} %param.17) | copy-start | bytes 28
  7.2 408.0 %all-reduce.4.cloned.1.call-start = ((), (), s32[]{:S(2)}) async-start(), calls=%async_computation | async-start | bytes 16777216 | tf_op jit(solution)/shard_map/psum | solution.py:1031
  8.9 4.4 %copy-start.40 = (s32[2]{0:T(128)S(1)}, s32[2]{0:T(128)}, u32[]{:S(2)}) copy-start(s32[2]{0:T(128)} %param.16) | copy-start | bytes 28
  12.0 3.8 collective-permute-start
  13.9 10.7 %copy-start.1 = (f32[1024,2]{1,0:T(8,128)}, f32[1024,2]{1,0:T(8,128)S(1)}, u32[]{:S(2)}) copy-start(f32[1024,2]{1,0:T(8,128)S(1)} %fusion.31.mask) | copy-start | bytes 24580
  18.9 2.9 copy-start.22
  24.6 20.5 %copy-start.20 = (bf16[512,1024]{1,0:T(8,128)(2,1)S(1)}, bf16[512,1024]{1,0:T(8,128)(2,1)}, u32[]{:S(2)}) copy-start(bf16[512,1024]{1,0:T(8,128)(2,1)} %param.23) | copy-start | bytes 3145732
  45.0 5.9 %copy-start.4 = (bf16[1024,512]{1,0:T(8,128)(2,1)}, bf16[1024,512]{1,0:T(8,128)(2,1)S(1)}, u32[]{:S(2)}) copy-start(bf16[1024,512]{1,0:T(8,128)(2,1)S(1)} %get-tuple-element.39.query_rows) | copy-start | bytes 3145732
  45.0 5.9 %copy-start.6 = (bf16[1024,512]{1,0:T(8,128)(2,1)}, bf16[1024,512]{1,0:T(8,128)(2,1)S(1)}, u32[]{:S(2)}) copy-start(bf16[1024,512]{1,0:T(8,128)(2,1)S(1)} %get-tuple-element.40.key_rows) | copy-start | bytes 3145732
  45.0 5.9 %copy-start.8 = (bf16[1024,512]{1,0:T(8,128)(2,1)}, bf16[1024,512]{1,0:T(8,128)(2,1)S(1)}, u32[]{:S(2)}) copy-start(bf16[1024,512]{1,0:T(8,128)(2,1)S(1)} %get-tuple-element.41.value_rows) | copy-start | bytes 3145732
  45.0 2.0 copy-start.27
  45.1 5.0 %copy-start.14 = (bf16[512,1024]{1,0:T(8,128)(2,1)S(1)}, bf16[512,1024]{1,0:T(8,128)(2,1)}, u32[]{:S(2)}) copy-start(bf16[512,1024]{1,0:T(8,128)(2,1)} %param.15) | copy-start | bytes 3145732
  45.8 4.2 collective-permute-start.1
  47.1 5.3 %collective-permute-start.3 = (bf16[512,1024]{1,0:T(8,128)(2,1)S(1)}, bf16[512,1024]{1,0:T(8,128)(2,1)S(1)}, u32[]{:S(2)}, u32[]{:S(2)}) collective-permute-start(bf16[512,1024]{1,0:T(8,128)(2,1)S(1)} %copy-done.27), channel_id=1, source_target_pairs={{0,1},{1,0},{2,3},{3,2},{4,5},{5,4},{6,7},{7,6},{8,9},{9,8},{10,11... | collective-permute-start | bytes 3145736 | tf_op jit(solution)/shard_map/ppermute | solution.py:925
  50.9 1.3 copy-start.11
  52.2 2.7 copy-start.25
  52.2 2.7 collective-permute-start.2
  54.9 1.0 copy-start.33
  104.1 4.5 %collective-permute-start.5 = (f32[512,1024]{1,0:T(8,128)}, f32[512,1024]{1,0:T(8,128)}, u32[]{:S(2)}, u32[]{:S(2)}) collective-permute-start(f32[512,1024]{1,0:T(8,128)} %get-tuple-element.38), channel_id=1, source_target_pairs={{0,1},{1,0},{2,3},{3,2},{4,5},{5,4},{6,7},{7,6},{8,9},{9,8},{10,11... | collective-permute-start | bytes 6291464 | tf_op jit(solution)/shard_map/ppermute | solution.py:925
  104.3 8.4 %collective-permute-start.4 = (bf16[512,1024]{1,0:T(8,128)(2,1)}, bf16[512,1024]{1,0:T(8,128)(2,1)S(1)}, u32[]{:S(2)}, u32[]{:S(2)}) collective-permute-start(bf16[512,1024]{1,0:T(8,128)(2,1)} %copy-done.3), channel_id=1, source_target_pairs={{0,1},{1,0},{2,3},{3,2},{4,5},{5,4},{6,7},{7,6},{8,9},{9,8},{10,11... | collective-permute-start | bytes 3145736 | tf_op jit(solution)/shard_map/ppermute | solution.py:925
  108.6 4.0 copy-start.12
  108.6 4.0 copy-start.28
  108.6 4.9 %copy-start.29 = (f32[512,1024]{1,0:T(8,128)S(1)}, f32[512,1024]{1,0:T(8,128)}, u32[]{:S(2)}) copy-start(f32[512,1024]{1,0:T(8,128)} %get-tuple-element.35) | copy-start | bytes 6291460
  113.5 2.6 copy-start.26
  113.5 2.6 copy-start.34
  113.5 4.4 %copy-start.41 = (bf16[1024,2048]{1,0:T(8,128)(2,1)S(1)}, bf16[1024,2048]{1,0:T(8,128)(2,1)}, u32[]{:S(2)}) copy-start(bf16[1024,2048]{1,0:T(8,128)(2,1)} %get-tuple-element.46) | copy-start | bytes 12582916
  116.1 8.0 %collective-permute-start.6 = (bf16[512,1024]{1,0:T(8,128)(2,1)S(1)}, bf16[512,1024]{1,0:T(8,128)(2,1)S(1)}, u32[]{:S(2)}, u32[]{:S(2)}) collective-permute-start(bf16[512,1024]{1,0:T(8,128)(2,1)S(1)} %get-tuple-element.65), channel_id=1, source_target_pairs={{0,1},{1,0},{2,3},{3,2},{4,5},{5,4},{6,7},{7,6},{8,9},{9,8},{10,11... | collective-permute-start | bytes 3145736 | tf_op jit(solution)/shard_map/ppermute | solution.py:925
  117.9 6.3 %copy-start.21 = (bf16[512,1024]{1,0:T(8,128)(2,1)S(1)}, bf16[512,1024]{1,0:T(8,128)(2,1)}, u32[]{:S(2)}) copy-start(bf16[512,1024]{1,0:T(8,128)(2,1)} %param.23) | copy-start | bytes 3145732
  124.2 1.3 copy-start.2
  124.2 1.4 copy-start.5
  124.2 1.7 copy-start.7
  124.2 2.0 copy-start.9
  126.2 23.4 %copy-start.23 = (bf16[1024,512]{1,0:T(8,128)(2,1)S(1)}, bf16[1024,512]{1,0:T(8,128)(2,1)}, u32[]{:S(2)}) copy-start(bf16[1024,512]{1,0:T(8,128)(2,1)} %param.20) | copy-start | bytes 3145732
  149.6 1.2 copy-start.24
  152.3 15.6 %collective-permute-start.7 = (bf16[512,1024]{1,0:T(8,128)(2,1)S(1)}, bf16[512,1024]{1,0:T(8,128)(2,1)S(1)}, u32[]{:S(2)}, u32[]{:S(2)}) collective-permute-start(bf16[512,1024]{1,0:T(8,128)(2,1)S(1)} %add_convert_fusion), channel_id=1, source_target_pairs={{0,1},{1,0},{2,3},{3,2},{4,5},{5,4},{6,7},{7,6},{8,9},{9,8},{10,11... | collective-permute-start | bytes 3145736 | tf_op jit(solution)/shard_map/ppermute | solution.py:925
  163.9 4.0 copy-start.15
  391.8 2.9 copy-start.32
  394.7 1.6 copy-start.31
  396.4 1.6 copy-start.30
  396.4 4.0 copy-start.19
  400.4 4.5 %copy-start.37 = (f32[8,1024]{1,0:T(8,128)S(1)}, f32[8,1024]{1,0:T(8,128)}, u32[]{:S(2)}) copy-start(f32[8,1024]{1,0:T(8,128)} %get-tuple-element.47) | copy-start | bytes 98308
  400.4 5.1 %copy-start.16 = (f32[512,1024]{1,0:T(8,128)S(1)}, f32[512,1024]{1,0:T(8,128)}, u32[]{:S(2)}) copy-start(f32[512,1024]{1,0:T(8,128)} %get-tuple-element.66) | copy-start | bytes 6291460
  400.4 5.1 %copy-start.17 = (f32[512,1024]{1,0:T(8,128)S(1)}, f32[512,1024]{1,0:T(8,128)}, u32[]{:S(2)}) copy-start(f32[512,1024]{1,0:T(8,128)} %get-tuple-element.77) | copy-start | bytes 6291460
  415.3 6.8 %copy-start.18 = (bf16[2048,1024]{1,0:T(8,128)(2,1)S(1)}, bf16[2048,1024]{1,0:T(8,128)(2,1)}, u32[]{:S(2)}) copy-start(bf16[2048,1024]{1,0:T(8,128)(2,1)} %get-tuple-element.64) | copy-start | bytes 12582916
  (3 other events, 2.4 us)
Sparse Core Ops, SparseCore 0:
  104.4 310.8 all-reduce.3

commit v6 on v5

--- a/solution.py
+++ b/solution.py
@@ -814,37 +814,68 @@
 
 
 def attend_back_kernel(
-    query_rows, key_rows, value_rows, mixed_rows, grad_mixed, logs, cos, sin, mask, grad_q, grad_k, grad_v, *scratch
+    query_rows, key_rows, value_rows, mixed_rows, grad_mixed, logs, cos, sin, mask, normed, w_query, w_key, w_value,
+    query_grad, key_grad, value_grad, share_own, share_other, normed_t, share_sum, grads, *scratch
 ):
+    pair = pl.program_id(0)
+
+    @pl.when(pair == 0)
+    def _():
+        normed_t[...] = normed[...].T
+        share_sum[...] = jnp.zeros_like(share_sum)
+
+    parts = tuple(grads.at[:, pl.ds(part * LANES, LANES)] for part in range(3))
     attend_back_pair(
-        query_rows, key_rows, value_rows, mixed_rows, grad_mixed, logs, cos, sin, mask, (grad_q, grad_k, grad_v), *scratch
-    )
-
-
-def attend_back(query_rows, key_rows, value_rows, mixed_rows, grad_mixed, logs, cosine, sine, mask):
+        query_rows, key_rows, value_rows, mixed_rows, grad_mixed, logs, cos, sin, mask, parts, *scratch
+    )
+    weight_grads = nn_dot(normed_t[...], grads[...]).astype(jnp.bfloat16)
+    for part, output in enumerate((query_grad, key_grad, value_grad)):
+        output[...] = weight_grads[:, part * LANES : (part + 1) * LANES]
+    weights = jnp.concatenate([w_query[...], w_key[...], w_value[...]], axis=1)
+    share_sum[...] += nt_dot(grads[...], weights)
+
+    @pl.when(pair == pl.num_programs(0) - 1)
+    def _():
+        half = share_own.shape[0]
+        share_own[...] = share_sum[:half]
+        share_other[...] = share_sum[half:].astype(jnp.bfloat16)
+
+
+def attend_back(query_rows, key_rows, value_rows, mixed_rows, grad_mixed, logs, cosine, sine, mask, normed, w_query, w_key, w_value):
     rows, width = query_rows.shape
+    features = normed.shape[1]
     pairs = width // LANES
     wide_block = pl.BlockSpec((rows, LANES), lambda pair: (0, pair))
     table = pl.BlockSpec((rows, LANES), lambda pair: (0, 0))
-    low = jax.ShapeDtypeStruct((rows, width), jnp.bfloat16)
+    columns = pl.BlockSpec((features, LANES), lambda pair: (0, pair))
+    half = pl.BlockSpec((rows // 2, features), lambda pair: (0, 0))
     return pl.pallas_call(
         attend_back_kernel,
         grid=(pairs,),
         in_specs=[wide_block] * 5
-        + [pl.BlockSpec((1, 2, rows), lambda pair: (pair, 0, 0)), table, table, pl.BlockSpec((rows, 2), lambda pair: (0, 0))],
-        out_specs=[wide_block] * 3,
-        out_shape=[low] * 3,
+        + [pl.BlockSpec((1, 2, rows), lambda pair: (pair, 0, 0)), table, table, pl.BlockSpec((rows, 2), lambda pair: (0, 0))]
+        + [pl.BlockSpec((rows, features), lambda pair: (0, 0))]
+        + [columns] * 3,
+        out_specs=[columns] * 3 + [half, half],
+        out_shape=[jax.ShapeDtypeStruct((features, width), jnp.bfloat16)] * 3
+        + [
+            jax.ShapeDtypeStruct((rows // 2, features), jnp.float32),
+            jax.ShapeDtypeStruct((rows // 2, features), jnp.bfloat16),
+        ],
         scratch_shapes=[
+            pltpu.VMEM((features, rows), jnp.bfloat16),
+            pltpu.VMEM((rows, features), jnp.float32),
+            pltpu.VMEM((rows, 3 * LANES), jnp.bfloat16),
             pltpu.VMEM((LANES, rows), jnp.float32),
             pltpu.VMEM((rows, LANES), jnp.float32),
             pltpu.VMEM((rows, LANES), jnp.float32),
             pltpu.VMEM((LANES, rows), jnp.float32),
         ],
-        compiler_params=pltpu.CompilerParams(vmem_limit_bytes=32 * 1024 * 1024),
+        compiler_params=pltpu.CompilerParams(vmem_limit_bytes=48 * 1024 * 1024),
         cost_estimate=pl.CostEstimate(
-            flops=10 * rows * rows * width, bytes_accessed=16 * rows * width, transcendentals=rows * rows * width // HD
+            flops=10 * rows * rows * width + 12 * rows * features * width, bytes_accessed=16 * rows * width, transcendentals=rows * rows * width // HD
         ),
-    )(query_rows, key_rows, value_rows, mixed_rows, grad_mixed, logs, cosine, sine, mask)
+    )(query_rows, key_rows, value_rows, mixed_rows, grad_mixed, logs, cosine, sine, mask, normed, w_query, w_key, w_value)
 
 
 NAMES = ("down", "gate", "up", "out", "query", "key", "value")
@@ -1001,21 +1032,10 @@
     grad_rows = rows_of(grad_attention, partner(grad_attention))
     grad_mixed = times_transpose(grad_rows, w_out).astype(jnp.bfloat16)
     out_grad = transpose_times(mixed_rows, grad_rows).astype(jnp.bfloat16)
-    grad_projected = attend_back(
-        query_rows, key_rows, value_rows, mixed_rows, grad_mixed, logs, cosine, sine, mask
-    )
-    qkv_grads = [transpose_times(gathered_one, g).astype(jnp.bfloat16) for g in grad_projected]
-
-    def grad_one_share(rows):
-        return sum(
-            times_transpose(g[rows], weight)
-            for g, weight in zip(grad_projected, (w_query, w_key, w_value))
-        )
-
-    grad_one_other = grad_one_share(slice(block_rows, None)).astype(jnp.bfloat16)
-    grad_normed_one = grad_one_share(slice(0, block_rows)) + partner(grad_one_other).astype(
-        jnp.float32
-    )
+    *qkv_grads, grad_one_own, grad_one_other = attend_back(
+        query_rows, key_rows, value_rows, mixed_rows, grad_mixed, logs, cosine, sine, mask, gathered_one, w_query, w_key, w_value
+    )
+    grad_normed_one = grad_one_own + partner(grad_one_other).astype(jnp.float32)
     grad_in_one, gain_one_grad, shift_one_grad = norm_backward(
         grad_normed_one, scaled_one, inverse_one, norm1_gain
     )

time: 438 us -> 437 us (level)
  matrix products: 38.2 us -> 24.4 us
  Pallas kernels: 310 us -> 323 us
    pallas_call x1, Pallas kernels: 23.4 us -> 36.4 us  [attend_back(): pl.pallas_call(attend_back_kernel, grid=(pairs,), in_specs=[wide_block] *...]
    dot_general x5 -> x2, matrix products: 20.1 us -> 11.7 us  [transpose_times(): lax.dot_general(left, right, (((0,), (0,)), ((), ())), preferred_element_...]
    dot_general x7 -> x1, matrix products: 7.77 us -> 2.26 us  [times_transpose(): lax.dot_general(left, right, (((1,), (1,)), ((), ())), preferred_element_...]
  transfers between devices with their start and end apart: 9 -> 9, of which waited for: 4 -> 4; matrix products, arithmetic and copies ran while one was open for 13% -> 11% of each run, Pallas kernels for 56% -> 60%
where the time goes in v6:
time: 437 us; the launch traced here: 431 us
  Pallas kernels  323 us (74%)
  other arithmetic  47.7 us (11%)
  matrix products  24.4 us (6%)
  between operations  14.7 us (3%)
  waiting for transfers between devices  13.6 us (3%)
  local copies, waits for them, and re-layouts  6.02 us (1%)
    pallas_call x1, Pallas kernels, summed_over_wide(): pl.pallas_call(functools.partial(sum_kernel, jobs), out_shape=[jax.ShapeD...  221 us
    pallas_call x1, Pallas kernels, feed_forward(): pl.pallas_call(feed_kernel, grid=(hidden // HIDDEN_TILE,), in_specs=[whol...  45.5 us
    pallas_call x1, Pallas kernels, attend_back(): pl.pallas_call(attend_back_kernel, grid=(pairs,), in_specs=[wide_block] *...  36.4 us
    convert_element_type x7, other arithmetic, on_device(): sums[name].astype(jnp.float32)  23.4 us
    pallas_call x1, Pallas kernels, attend(): pl.pallas_call(attend_kernel, grid=(pairs,), in_specs=[wide_block] * 3 +...  20.3 us
    dot_general x2, matrix products, transpose_times(): lax.dot_general(left, right, (((0,), (0,)), ((), ())), preferred_element_...  11.7 us
    dot_general x3, matrix products, on_device(): jnp.dot(gathered_one, weight, preferred_element_type=jnp.float32)  8.85 us
  transfers between devices with their start and end apart: 9, of which 4 were waited for; matrix products, arithmetic and copies ran while one was open for 11% of the time, Pallas kernels for 60%

profile of v6, /device:TPU:0, one launch (start us, length us, event | category | flops | bytes accessed | tf_op | source)
XLA Modules:
  0.0 431.3 jit_solution(17651403308570055530)
XLA Ops:
  7.3 1.6 convert_reduce_fusion
  8.9 1.6 fusion.13
  10.5 1.4 fusion.7
  12.0 0.5 collective-permute-start
  12.6 0.6 gather_fusion
  13.5 0.3 fusion.21.mask
  13.9 1.9 fusion.15
  15.8 3.2 fusion.38.query_raw
  19.0 2.9 fusion.37.key_raw
  21.9 2.8 fusion.36.value_raw
  24.7 20.3 %shard_map.246 = (bf16[1024,512]{1,0:T(8,128)(2,1)S(1)}, bf16[1024,512]{1,0:T(8,128)(2,1)S(1)}, bf16[1024,512]{1,0:T(8,128)(2,1)S(1)}, bf16[1024,512]{1,0:T(8,128)(2,1)S(1)}, f32[4,2,1024]{2,1,0:T(2,128)S(1)}) custom-call(f32[1024,512]{1,0:T(8,128)S(1)} %fusion.38.query_raw, f32[1024,512]{1,0:T(8,128)S(1)} %fusion.37.key_raw, ...), custom_call_target="tpu_custom_call" | custom-call | flops 2147483648 | bytes 10485760 | tf_op jit(solution)/shard_map/pallas_call | solution.py:763
  45.1 0.7 fusion.16
  45.9 1.2 copy-done.23
  47.1 2.9 collective-permute-done.1
  50.0 0.9 fusion.41
  51.0 0.3 multiply_reduce_fusion.2
  51.3 0.3 copy-done.31
  51.7 0.4 add_convert_fusion
  52.4 1.5 pad_maximum_fusion.2.cots
  53.9 1.0 collective-permute-done.2
  54.9 1.0 copy-done.29
  55.9 1.6 pad_maximum_fusion.1.rows
  57.5 45.5 %shard_map.247 = (f32[512,1024]{1,0:T(8,128)}, bf16[512,1024]{1,0:T(8,128)(2,1)S(1)}, f32[512,1024]{1,0:T(8,128)}, f32[512,1024]{1,0:T(8,128)}, bf16[2048,1024]{...) custom-call(bf16[1024,1024]{1,0:T(8,128)(2,1)} %pad_maximum_fusion.1.rows, ...), custom_call_target="tpu_custom_call" | custom-call | flops 34359738368 | bytes 41943040 | tf_op jit(solution)/shard_map/pallas_call | solution.py:932
  103.1 0.4 collective-permute-start.4
  103.5 3.9 collective-permute-done.5
  107.5 4.0 multiply_reduce_fusion
  111.5 0.9 copy-done.25
  112.4 2.5 fusion.39
  114.8 3.0 pad_maximum_fusion.normed
  117.9 2.3 convolution_convert_fusion.2.grad_mixed
  120.1 36.4 %shard_map.248 = (bf16[1024,512]{1,0:T(8,128)(2,1)S(1)}, bf16[1024,512]{1,0:T(8,128)(2,1)S(1)}, bf16[1024,512]{1,0:T(8,128)(2,1)S(1)}, f32[512,1024]{1,0:T(8,128)}, bf16[512,1024]{1,0:T(8,128)(2,1)S(1)}) custom-call(bf16[1024,512]{1,0:T(8,128)(2,1)} %copy-done.8, bf16[1024,512]{1,0:T(8,128)(2,1)} %copy-done.9, bf16[1024,512]{1,0:T(8,128)(2,1)} %copy-done.10, ...), custom_call_target="tpu_custom_call" | custom-call | flops 11811160064 | bytes 8388608 | tf_op jit(solution)/shard_map/pallas_call | solution.py:852
  156.5 0.5 collective-permute-start.7
  157.0 9.5 %convolution_convert_fusion.refs_0_ = bf16[1024,2048]{1,0:T(8,128)(2,1)} fusion(bf16[1024,2048]{1,0:T(8,128)(2,1)} %get-tuple-element.47, bf16[512,1024]{1,0:T(8,128)(2,1)S(1)} %copy-done.30, bf16[512,1024]{1,0:T(8,128)(2,1)S(1)} %copy-done.22), kind=kOutput, calls=%fused_computation.1 | convolution fusion | flops 4301258752 | bytes 10485760 | tf_op jit(solution)/shard_map/dot_general | solution.py:27
  166.6 2.2 convolution_convert_fusion.1.refs_1_
  168.8 1.1 fusion.12
  169.9 0.6 select_maximum_fusion.refs_5_
  170.5 220.9 %shard_map.249 = (bf16[1024,2048]{1,0:T(8,128)(2,1)}, bf16[512,1024]{1,0:T(8,128)(2,1)}, bf16[1024,512]{1,0:T(8,128)(2,1)}, bf16[1024,512]{1,0:T(8,128)(2,1)}, b...) custom-call(bf16[1024,2048]{1,0:T(8,128)(2,1)} %convolution_convert_fusion.refs_0_, ...), custom_call_target="tpu_custom_call" | custom-call | bytes 20971520 | tf_op jit(solution)/shard_map/pallas_call | solution.py:668
  391.4 2.9 convert_element_type.80
  394.4 1.6 convert_element_type.81
  396.0 1.6 convert_element_type.82
  397.6 1.6 convert_element_type.83
  399.2 0.8 copy-done.20
  400.0 4.4 %convert_element_type.85 = f32[1024,2048]{1,0:T(8,128)} convert(bf16[1024,2048]{1,0:T(8,128)(2,1)S(1)} %copy-done.20) | non-fusion elementwise | flops 2097152 | bytes 12582912 | tf_op jit(solution)/shard_map/convert_element_type | solution.py:1053
  404.5 0.6 fusion.40
  405.1 2.2 fusion.11
  407.3 5.7 %all-reduce.4.cloned.1.call-done = (bf16[1024,2048]{1,0:T(8,128)(2,1)}, bf16[2048,1024]{1,0:T(8,128)(2,1)}) async-done(((bf16[1024,2048]{1,0:T(8,128)(2,1)}, bf16[2048,1024]{1,0:T(8,128)(2,1)}), (bf16[1024,2048]{1,0:T(8,128)(2,1)}, bf16[2048,1024]{1,0:T(8,128)(2,1)})) %all-reduce.4.cloned.1.call-update) | async-done | bytes 8388624 | tf_op jit(solution)/shard_map/psum | solution.py:1051
  413.0 6.8 %convert_element_type.84 = f32[1024,2048]{1,0:T(8,128)} convert(bf16[1024,2048]{1,0:T(8,128)(2,1)} %get-tuple-element.67) | non-fusion elementwise | flops 2097152 | bytes 12582912 | tf_op jit(solution)/shard_map/convert_element_type | solution.py:1053
  419.8 4.4 %convert_element_type.86 = f32[2048,1024]{1,0:T(8,128)} convert(bf16[2048,1024]{1,0:T(8,128)(2,1)S(1)} %copy-done.19) | non-fusion elementwise | flops 2097152 | bytes 12582912 | tf_op jit(solution)/shard_map/convert_element_type | solution.py:1053
  (104 shorter events, 1.2 us)
Async XLA Ops:
  7.2 37.9 %copy-start = (bf16[512,1024]{1,0:T(8,128)(2,1)S(1)}, bf16[512,1024]{1,0:T(8,128)(2,1)}, u32[]{:S(2)}) copy-start(bf16[512,1024]{1,0:T(8,128)(2,1)} %param.23) | copy-start | bytes 3145732
  7.2 3.3 copy-start.14
  7.2 3.3 copy-start.32
  7.2 3.3 copy-start.34
  7.2 5.3 %copy-start.11 = (s32[2]{0:T(128)S(1)}, s32[2]{0:T(128)}, u32[]{:S(2)}) copy-start(s32[2]{0:T(128)} %param.17) | copy-start | bytes 28
  7.2 405.8 %all-reduce.4.cloned.1.call-start = ((), (), s32[]{:S(2)}) async-start(), calls=%async_computation | async-start | bytes 16777216 | tf_op jit(solution)/shard_map/psum | solution.py:1051
  8.9 4.4 %copy-start.38 = (s32[2]{0:T(128)S(1)}, s32[2]{0:T(128)}, u32[]{:S(2)}) copy-start(s32[2]{0:T(128)} %param.16) | copy-start | bytes 28
  12.0 3.8 collective-permute-start
  13.9 10.8 %copy-start.6 = (f32[1024,2]{1,0:T(8,128)}, f32[1024,2]{1,0:T(8,128)S(1)}, u32[]{:S(2)}) copy-start(f32[1024,2]{1,0:T(8,128)S(1)} %fusion.21.mask) | copy-start | bytes 24580
  15.8 3.2 copy-start.36
  19.0 2.9 copy-start.37
  45.0 5.9 %copy-start.1 = (bf16[1024,512]{1,0:T(8,128)(2,1)}, bf16[1024,512]{1,0:T(8,128)(2,1)S(1)}, u32[]{:S(2)}) copy-start(bf16[1024,512]{1,0:T(8,128)(2,1)S(1)} %get-tuple-element.36.mixed_rows) | copy-start | bytes 3145732
  45.0 5.9 %copy-start.8 = (bf16[1024,512]{1,0:T(8,128)(2,1)}, bf16[1024,512]{1,0:T(8,128)(2,1)S(1)}, u32[]{:S(2)}) copy-start(bf16[1024,512]{1,0:T(8,128)(2,1)S(1)} %get-tuple-element.41.query_rows) | copy-start | bytes 3145732
  45.0 5.9 %copy-start.9 = (bf16[1024,512]{1,0:T(8,128)(2,1)}, bf16[1024,512]{1,0:T(8,128)(2,1)S(1)}, u32[]{:S(2)}) copy-start(bf16[1024,512]{1,0:T(8,128)(2,1)S(1)} %get-tuple-element.42.key_rows) | copy-start | bytes 3145732
  45.0 5.9 %copy-start.10 = (bf16[1024,512]{1,0:T(8,128)(2,1)}, bf16[1024,512]{1,0:T(8,128)(2,1)S(1)}, u32[]{:S(2)}) copy-start(bf16[1024,512]{1,0:T(8,128)(2,1)S(1)} %get-tuple-element.43.value_rows) | copy-start | bytes 3145732
  45.0 2.0 copy-start.23
  45.8 4.2 collective-permute-start.1
  47.1 5.3 %collective-permute-start.3 = (bf16[512,1024]{1,0:T(8,128)(2,1)S(1)}, bf16[512,1024]{1,0:T(8,128)(2,1)S(1)}, u32[]{:S(2)}, u32[]{:S(2)}) collective-permute-start(bf16[512,1024]{1,0:T(8,128)(2,1)S(1)} %copy-done.23), channel_id=1, source_target_pairs={{0,1},{1,0},{2,3},{3,2},{4,5},{5,4},{6,7},{7,6},{8,9},{9,8},{10,11... | collective-permute-start | bytes 3145736 | tf_op jit(solution)/shard_map/ppermute | solution.py:956
  50.9 1.3 copy-start.12
  50.9 0.7 copy-start.31
  50.9 0.8 copy-start.35
  52.2 2.7 copy-start.21
  52.2 2.7 collective-permute-start.2
  54.9 1.0 copy-start.29
  102.9 4.5 %collective-permute-start.5 = (f32[512,1024]{1,0:T(8,128)}, f32[512,1024]{1,0:T(8,128)}, u32[]{:S(2)}, u32[]{:S(2)}) collective-permute-start(f32[512,1024]{1,0:T(8,128)} %get-tuple-element.40), channel_id=1, source_target_pairs={{0,1},{1,0},{2,3},{3,2},{4,5},{5,4},{6,7},{7,6},{8,9},{9,8},{10,11... | collective-permute-start | bytes 6291464 | tf_op jit(solution)/shard_map/ppermute | solution.py:956
  103.1 8.4 %collective-permute-start.4 = (bf16[512,1024]{1,0:T(8,128)(2,1)S(1)}, bf16[512,1024]{1,0:T(8,128)(2,1)S(1)}, u32[]{:S(2)}, u32[]{:S(2)}) collective-permute-start(bf16[512,1024]{1,0:T(8,128)(2,1)S(1)} %get-tuple-element.38), channel_id=1, source_target_pairs={{0,1},{1,0},{2,3},{3,2},{4,5},{5,4},{6,7},{7,6},{8,9},{9,8},{10,11... | collective-permute-start | bytes 3145736 | tf_op jit(solution)/shard_map/ppermute | solution.py:956
  107.4 4.0 copy-start.13
  107.4 4.0 copy-start.24
  107.5 4.9 %copy-start.25 = (f32[512,1024]{1,0:T(8,128)S(1)}, f32[512,1024]{1,0:T(8,128)}, u32[]{:S(2)}) copy-start(f32[512,1024]{1,0:T(8,128)} %get-tuple-element.37) | copy-start | bytes 6291460
  114.8 3.0 collective-permute-start.6
  117.9 2.3 copy-start.7
  120.1 36.9 %copy-start.22 = (bf16[512,1024]{1,0:T(8,128)(2,1)S(1)}, bf16[512,1024]{1,0:T(8,128)(2,1)}, u32[]{:S(2)}) copy-start(bf16[512,1024]{1,0:T(8,128)(2,1)} %copy-done.21) | copy-start | bytes 3145732
  120.1 36.9 %copy-start.30 = (bf16[512,1024]{1,0:T(8,128)(2,1)S(1)}, bf16[512,1024]{1,0:T(8,128)(2,1)}, u32[]{:S(2)}) copy-start(bf16[512,1024]{1,0:T(8,128)(2,1)} %copy-done.29) | copy-start | bytes 3145732
  156.5 10.0 %copy-start.3 = (bf16[1024,512]{1,0:T(8,128)(2,1)}, bf16[1024,512]{1,0:T(8,128)(2,1)S(1)}, u32[]{:S(2)}) copy-start(bf16[1024,512]{1,0:T(8,128)(2,1)S(1)} %get-tuple-element.48.refs_2_) | copy-start | bytes 3145732
  156.5 10.0 %copy-start.4 = (bf16[1024,512]{1,0:T(8,128)(2,1)}, bf16[1024,512]{1,0:T(8,128)(2,1)S(1)}, u32[]{:S(2)}) copy-start(bf16[1024,512]{1,0:T(8,128)(2,1)S(1)} %get-tuple-element.49.refs_3_) | copy-start | bytes 3145732
  156.5 10.0 %copy-start.5 = (bf16[1024,512]{1,0:T(8,128)(2,1)}, bf16[1024,512]{1,0:T(8,128)(2,1)S(1)}, u32[]{:S(2)}) copy-start(bf16[1024,512]{1,0:T(8,128)(2,1)S(1)} %get-tuple-element.50.refs_4_) | copy-start | bytes 3145732
  156.5 12.3 %collective-permute-start.7 = (bf16[512,1024]{1,0:T(8,128)(2,1)S(1)}, bf16[512,1024]{1,0:T(8,128)(2,1)S(1)}, u32[]{:S(2)}, u32[]{:S(2)}) collective-permute-start(bf16[512,1024]{1,0:T(8,128)(2,1)S(1)} %get-tuple-element.46), channel_id=1, source_target_pairs={{0,1},{1,0},{2,3},{3,2},{4,5},{5,4},{6,7},{7,6},{8,9},{9,8},{10,11... | collective-permute-start | bytes 3145736 | tf_op jit(solution)/shard_map/ppermute | solution.py:956
  157.0 9.5 %copy-start.2 = (bf16[1024,512]{1,0:T(8,128)(2,1)S(1)}, bf16[1024,512]{1,0:T(8,128)(2,1)}, u32[]{:S(2)}) copy-start(bf16[1024,512]{1,0:T(8,128)(2,1)} %copy-done.1) | copy-start | bytes 3145732
  166.5 2.3 copy-start.15
  166.5 2.3 copy-start.16
  391.4 3.0 copy-start.28
  394.4 1.6 copy-start.27
  396.0 1.6 copy-start.26
  396.0 4.0 copy-start.20
  400.0 4.5 %copy-start.33 = (f32[8,1024]{1,0:T(8,128)S(1)}, f32[8,1024]{1,0:T(8,128)}, u32[]{:S(2)}) copy-start(f32[8,1024]{1,0:T(8,128)} %get-tuple-element.51) | copy-start | bytes 98308
  400.0 5.1 %copy-start.17 = (f32[512,1024]{1,0:T(8,128)S(1)}, f32[512,1024]{1,0:T(8,128)}, u32[]{:S(2)}) copy-start(f32[512,1024]{1,0:T(8,128)} %get-tuple-element.45) | copy-start | bytes 6291460
  400.0 5.1 %copy-start.18 = (f32[512,1024]{1,0:T(8,128)S(1)}, f32[512,1024]{1,0:T(8,128)}, u32[]{:S(2)}) copy-start(f32[512,1024]{1,0:T(8,128)} %get-tuple-element.70) | copy-start | bytes 6291460
  413.0 6.8 %copy-start.19 = (bf16[2048,1024]{1,0:T(8,128)(2,1)S(1)}, bf16[2048,1024]{1,0:T(8,128)(2,1)}, u32[]{:S(2)}) copy-start(bf16[2048,1024]{1,0:T(8,128)(2,1)} %get-tuple-element.68) | copy-start | bytes 12582916
Sparse Core Ops, SparseCore 0:
  103.2 309.7 all-reduce.3

commit v7 on v6

--- a/solution.py
+++ b/solution.py
@@ -887,9 +887,10 @@
 
 
 def feed_kernel(
-    rows, cots, gate_w, up_w, down_w, out_own, out_other, back_own, back_other, down_grad, gate_grad, grad_up, rows_t, out_sum, back_sum
+    rows, cots, gate_w, up_w, down_w, out_other, back_other, down_grad, gate_grad, hidden_out, grad_gate, grad_up, rows_t, out_sum, back_sum
 ):
     step = pl.program_id(0)
+    half = out_sum.shape[0]
 
     @pl.when(step == 0)
     def _():
@@ -904,20 +905,19 @@
     hidden = (silu * up).astype(jnp.bfloat16)
     grad_hidden = nt_dot(cots[...], down_w[...])
     gate_back = (grad_hidden * up * (sigmoid * (1.0 + gate * (1.0 - sigmoid)))).astype(jnp.bfloat16)
+    hidden_out[...] = hidden
+    grad_gate[...] = gate_back
     up_back = (grad_hidden * silu).astype(jnp.bfloat16)
     grad_up[...] = up_back
     down_grad[...] = nn_dot(hidden.T, cots[...]).astype(jnp.bfloat16)
     gate_grad[...] = nn_dot(rows_t[...], gate_back).astype(jnp.bfloat16)
-    out_sum[...] += nn_dot(hidden, down_w[...])
-    back_sum[...] += nt_dot(gate_back, gate_w[...]) + nt_dot(up_back, up_w[...])
+    out_sum[...] += nn_dot(hidden[half:], down_w[...])
+    back_sum[...] += nt_dot(gate_back[half:], gate_w[...]) + nt_dot(up_back[half:], up_w[...])
 
     @pl.when(step == pl.num_programs(0) - 1)
     def _():
-        half = rows.shape[0] // 2
-        out_own[...] = out_sum[:half]
-        out_other[...] = out_sum[half:].astype(jnp.bfloat16)
-        back_own[...] = back_sum[:half]
-        back_other[...] = back_sum[half:]
+        out_other[...] = out_sum[...].astype(jnp.bfloat16)
+        back_other[...] = back_sum[...]
 
 
 def feed_forward(rows, cots, gate_w, up_w, down_w):
@@ -927,27 +927,27 @@
     half = pl.BlockSpec((count // 2, width), lambda tile: (0, 0))
     columns = pl.BlockSpec((width, HIDDEN_TILE), lambda tile: (0, tile))
     lines = pl.BlockSpec((HIDDEN_TILE, width), lambda tile: (tile, 0))
-    half_wide = jax.ShapeDtypeStruct((count // 2, width), jnp.float32)
-    half_low = jax.ShapeDtypeStruct((count // 2, width), jnp.bfloat16)
+    units = pl.BlockSpec((count, HIDDEN_TILE), lambda tile: (0, tile))
     return pl.pallas_call(
         feed_kernel,
         grid=(hidden // HIDDEN_TILE,),
         in_specs=[whole, whole, columns, columns, lines],
-        out_specs=[half, half, half, half, lines, columns, pl.BlockSpec((count, HIDDEN_TILE), lambda tile: (0, tile))],
-        out_shape=[half_wide, half_low, half_wide, half_wide]
-        + [
+        out_specs=[half, half, lines, columns, units, units, units],
+        out_shape=[
+            jax.ShapeDtypeStruct((count // 2, width), jnp.bfloat16),
+            jax.ShapeDtypeStruct((count // 2, width), jnp.float32),
             jax.ShapeDtypeStruct((hidden, width), jnp.bfloat16),
             jax.ShapeDtypeStruct((width, hidden), jnp.bfloat16),
-            jax.ShapeDtypeStruct((count, hidden), jnp.bfloat16),
-        ],
+        ]
+        + [jax.ShapeDtypeStruct((count, hidden), jnp.bfloat16)] * 3,
         scratch_shapes=[
             pltpu.VMEM((width, count), jnp.bfloat16),
-            pltpu.VMEM((count, width), jnp.float32),
-            pltpu.VMEM((count, width), jnp.float32),
+            pltpu.VMEM((count // 2, width), jnp.float32),
+            pltpu.VMEM((count // 2, width), jnp.float32),
         ],
-        compiler_params=pltpu.CompilerParams(vmem_limit_bytes=52 * 1024 * 1024),
+        compiler_params=pltpu.CompilerParams(vmem_limit_bytes=44 * 1024 * 1024),
         cost_estimate=pl.CostEstimate(
-            flops=16 * count * width * hidden, bytes_accessed=12 * width * hidden + 16 * count * width, transcendentals=count * hidden
+            flops=13 * count * width * hidden, bytes_accessed=10 * width * hidden + 10 * count * width, transcendentals=count * hidden
         ),
     )(rows, cots, gate_w, up_w, down_w)
 
@@ -1018,12 +1018,21 @@
     normed_two, scaled_two, inverse_two = norm_forward(resid_values, norm2_gain, norm2_shift)
     normed_two = normed_two.astype(jnp.bfloat16)
     gathered_two = rows_of(normed_two, partner(normed_two))
-    out_own, out_other, grad_two_own, grad_two_other, down_grad, gate_grad, grad_up = feed_forward(
+    out_other, grad_two_other, down_grad, gate_grad, hidden_rows, grad_gate, grad_up = feed_forward(
         gathered_two, cot_rows, w_gate, w_up, w_down
     )
     up_grad = transpose_times(gathered_two, grad_up).astype(jnp.bfloat16)
-    out_values = resid_values + out_own + partner(out_other).astype(jnp.float32)
-    grad_normed_two = grad_two_own + partner(grad_two_other)
+    out_values = (
+        resid_values
+        + jnp.dot(hidden_rows[:block_rows], w_down, preferred_element_type=jnp.float32)
+        + partner(out_other).astype(jnp.float32)
+    )
+    grad_normed_two = (
+        times_transpose(grad_gate[:block_rows], w_gate)
+        + times_transpose(grad_up[:block_rows], w_up)
+        + partner(grad_two_other)
+    )
+    grad_normed_two, up_grad = lax.optimization_barrier((grad_normed_two, up_grad))
     grad_in_two, gain_two_grad, shift_two_grad = norm_backward(
         grad_normed_two, scaled_two, inverse_two, norm2_gain
     )

time: 437 us -> 438 us (level)
  matrix products: 24.4 us -> 33.6 us
  waiting for transfers between devices: 13.6 us -> 5.41 us
    dot_general x1 -> x3, matrix products: 2.26 us -> 12.9 us  [times_transpose(): lax.dot_general(left, right, (((1,), (1,)), ((), ())), preferred_element_...]
    pallas_call x1, Pallas kernels: 221 us -> 228 us  [summed_over_wide(): pl.pallas_call(functools.partial(sum_kernel, jobs), out_shape=[jax.ShapeD...]
    psum x1, waiting for transfers between devices: 5.74 us -> 0.03 us  [on_device(): sums[name] = lax.psum(gradients[name], 'wide')]
    pallas_call x1, Pallas kernels: 45.5 us -> 40.4 us  [feed_forward(): pl.pallas_call(feed_kernel, grid=(hidden // HIDDEN_TILE,), in_specs=[whol...]
  transfers between devices with their start and end apart: 9 -> 9, of which waited for: 4 -> 2; matrix products, arithmetic and copies ran while one was open for 11% -> 13% of each run, Pallas kernels for 60% -> 61%
where the time goes in v7:
time: 438 us; the launch traced here: 433 us
  Pallas kernels  325 us (74%)
  other arithmetic  45.4 us (10%)
  matrix products  33.6 us (8%)
  between operations  15.1 us (3%)
  local copies, waits for them, and re-layouts  6.45 us (1%)
  waiting for transfers between devices  5.41 us (1%)
    pallas_call x1, Pallas kernels, summed_over_wide(): pl.pallas_call(functools.partial(sum_kernel, jobs), out_shape=[jax.ShapeD...  228 us
    pallas_call x1, Pallas kernels, feed_forward(): pl.pallas_call(feed_kernel, grid=(hidden // HIDDEN_TILE,), in_specs=[whol...  40.4 us
    pallas_call x1, Pallas kernels, attend_back(): pl.pallas_call(attend_back_kernel, grid=(pairs,), in_specs=[wide_block] *...  36.4 us
    convert_element_type x7, other arithmetic, on_device(): sums[name].astype(jnp.float32)  23.4 us
    pallas_call x1, Pallas kernels, attend(): pl.pallas_call(attend_kernel, grid=(pairs,), in_specs=[wide_block] * 3 +...  20.8 us
    dot_general x3, matrix products, times_transpose(): lax.dot_general(left, right, (((1,), (1,)), ((), ())), preferred_element_...  12.9 us
  transfers between devices with their start and end apart: 9, of which 2 were waited for; matrix products, arithmetic and copies ran while one was open for 13% of the time, Pallas kernels for 61%

profile of v7, /device:TPU:0, one launch (start us, length us, event | category | flops | bytes accessed | tf_op | source)
XLA Modules:
  0.0 433.1 jit_solution(6044722025550274025)
XLA Ops:
  7.3 1.6 convert_reduce_fusion
  8.9 1.6 fusion.13
  10.5 1.4 fusion.7
  12.0 0.5 collective-permute-start
  12.8 0.6 gather_fusion
  13.5 0.3 fusion.27.mask
  13.9 1.9 fusion.21
  15.8 3.2 fusion.44.query_raw
  19.0 2.6 fusion.43.key_raw
  21.6 2.5 fusion.42.value_raw
  24.1 20.8 %shard_map.246 = (bf16[1024,512]{1,0:T(8,128)(2,1)S(1)}, bf16[1024,512]{1,0:T(8,128)(2,1)S(1)}, bf16[1024,512]{1,0:T(8,128)(2,1)S(1)}, bf16[1024,512]{1,0:T(8,128)(2,1)S(1)}, f32[4,2,1024]{2,1,0:T(2,128)S(1)}) custom-call(f32[1024,512]{1,0:T(8,128)S(1)} %fusion.44.query_raw, f32[1024,512]{1,0:T(8,128)S(1)} %fusion.43.key_raw, ...), custom_call_target="tpu_custom_call" | custom-call | flops 2147483648 | bytes 10485760 | tf_op jit(solution)/shard_map/pallas_call | solution.py:763
  45.0 0.7 fusion.22
  45.8 1.2 copy-done.24
  47.0 3.0 collective-permute-done.1
  50.0 0.9 fusion.47
  50.9 0.3 multiply_reduce_fusion.2
  51.7 0.4 add_convert_fusion
  52.5 2.3 collective-permute-done.2
  54.9 1.0 copy-done.32
  56.0 40.4 %shard_map.247 = (bf16[512,1024]{1,0:T(8,128)(2,1)S(1)}, f32[512,1024]{1,0:T(8,128)}, bf16[2048,1024]{1,0:T(8,128)(2,1)}, bf16[1024,2048]{1,0:T(8,128)(2,1)}, bf...) custom-call(bf16[1024,1024]{1,0:T(8,128)(2,1)S(1)} %pad_maximum_fusion.1.rows, ...), custom_call_target="tpu_custom_call" | custom-call | flops 27917287424 | bytes 31457280 | tf_op jit(solution)/shard_map/pallas_call | solution.py:931
  96.6 5.3 %fusion.17 = f32[512,1024]{1,0:T(8,128)} fusion(bf16[1024,2048]{1,0:T(8,128)(2,1)S(1)} %copy-done.39, bf16[1024,2048]{1,0:T(8,128)(2,1)} %get-tuple-element.41), kind=kOutput, calls=%fused_computation.31 | convolution fusion | flops 2147483648 | bytes 8388608 | tf_op jit(solution)/shard_map/dot_general | solution.py:21
  101.9 0.4 collective-permute-start.4
  102.3 5.3 %fusion.15 = f32[512,1024]{1,0:T(8,128)S(1)} fusion(bf16[1024,2048]{1,0:T(8,128)(2,1)} %up_w.1, bf16[1024,2048]{1,0:T(8,128)(2,1)} %get-tuple-element.42), kind=kOutput, calls=%fused_computation.29 | convolution fusion | flops 2147483648 | bytes 8388608 | tf_op jit(solution)/shard_map/dot_general | solution.py:21
  107.7 2.4 fusion.19
  110.1 0.6 copy-done.44
  110.7 6.3 %convolution_convert_fusion.refs_0_ = bf16[1024,2048]{1,0:T(8,128)(2,1)} fusion(bf16[1024,2048]{1,0:T(8,128)(2,1)S(1)} %copy-done.44, bf16[512,1024]{1,0:T(8,128)(2,1)S(1)} %copy-done.33, bf16[512,1024]{1,0:T(8,128)(2,1)S(1)} %copy-done.23), kind=kOutput, calls=%fused_computation.1 | convolution fusion | flops 4301258752 | bytes 10485760 | tf_op jit(solution)/shard_map/dot_general | solution.py:27
  117.0 2.4 add_add_fusion
  119.4 1.0 multiply_reduce_fusion
  120.7 3.6 fusion.45
  124.3 2.8 pad_maximum_fusion.normed
  127.1 2.3 convolution_convert_fusion.2.grad_mixed
  129.4 36.4 %shard_map.248 = (bf16[1024,512]{1,0:T(8,128)(2,1)S(1)}, bf16[1024,512]{1,0:T(8,128)(2,1)S(1)}, bf16[1024,512]{1,0:T(8,128)(2,1)S(1)}, f32[512,1024]{1,0:T(8,128)}, bf16[512,1024]{1,0:T(8,128)(2,1)S(1)}) custom-call(bf16[1024,512]{1,0:T(8,128)(2,1)} %copy-done.8, bf16[1024,512]{1,0:T(8,128)(2,1)} %copy-done.9, bf16[1024,512]{1,0:T(8,128)(2,1)} %copy-done.10, ...), custom_call_target="tpu_custom_call" | custom-call | flops 11811160064 | bytes 8388608 | tf_op jit(solution)/shard_map/pallas_call | solution.py:852
  165.8 0.6 collective-permute-start.7
  166.4 2.2 convolution_convert_fusion.1.refs_1_
  168.7 0.6 copy-done.17
  169.3 1.1 fusion.12
  170.4 0.6 select_maximum_fusion.refs_5_
  171.1 227.6 %shard_map.249 = (bf16[1024,2048]{1,0:T(8,128)(2,1)}, bf16[512,1024]{1,0:T(8,128)(2,1)}, bf16[1024,512]{1,0:T(8,128)(2,1)}, bf16[1024,512]{1,0:T(8,128)(2,1)}, b...) custom-call(bf16[1024,2048]{1,0:T(8,128)(2,1)} %convolution_convert_fusion.refs_0_, ...), custom_call_target="tpu_custom_call" | custom-call | bytes 20971520 | tf_op jit(solution)/shard_map/pallas_call | solution.py:668
  398.7 2.9 convert_element_type.80
  401.6 1.6 convert_element_type.81
  403.2 1.6 convert_element_type.82
  404.8 1.6 convert_element_type.83
  406.4 0.8 copy-done.21
  407.2 4.5 %convert_element_type.85 = f32[1024,2048]{1,0:T(8,128)} convert(bf16[1024,2048]{1,0:T(8,128)(2,1)S(1)} %copy-done.21) | non-fusion elementwise | flops 2097152 | bytes 12582912 | tf_op jit(solution)/shard_map/convert_element_type | solution.py:1062
  411.7 0.6 fusion.46
  412.3 2.2 fusion.11
  414.5 6.8 %convert_element_type.84 = f32[1024,2048]{1,0:T(8,128)} convert(bf16[1024,2048]{1,0:T(8,128)(2,1)} %get-tuple-element.71) | non-fusion elementwise | flops 2097152 | bytes 12582912 | tf_op jit(solution)/shard_map/convert_element_type | solution.py:1062
  421.3 4.4 %convert_element_type.86 = f32[2048,1024]{1,0:T(8,128)} convert(bf16[2048,1024]{1,0:T(8,128)(2,1)S(1)} %copy-done.20) | non-fusion elementwise | flops 2097152 | bytes 12582912 | tf_op jit(solution)/shard_map/convert_element_type | solution.py:1062
  (122 shorter events, 2.2 us)
Async XLA Ops:
  7.2 37.8 %copy-start = (bf16[512,1024]{1,0:T(8,128)(2,1)S(1)}, bf16[512,1024]{1,0:T(8,128)(2,1)}, u32[]{:S(2)}) copy-start(bf16[512,1024]{1,0:T(8,128)(2,1)} %param.23) | copy-start | bytes 3145732
  7.2 3.3 copy-start.14
  7.2 3.3 copy-start.37
  7.2 3.3 copy-start.35
  7.2 5.2 %copy-start.43 = (s32[2]{0:T(128)S(1)}, s32[2]{0:T(128)}, u32[]{:S(2)}) copy-start(s32[2]{0:T(128)} %param.16) | copy-start | bytes 28
  7.2 5.5 %copy-start.11 = (s32[2]{0:T(128)S(1)}, s32[2]{0:T(128)}, u32[]{:S(2)}) copy-start(s32[2]{0:T(128)} %param.17) | copy-start | bytes 28
  7.2 407.3 %all-reduce.4.cloned.1.call-start = ((), (), s32[]{:S(2)}) async-start(), calls=%async_computation | async-start | bytes 16777216 | tf_op jit(solution)/shard_map/psum | solution.py:1060
  12.0 3.8 collective-permute-start
  13.8 10.2 %copy-start.6 = (f32[1024,2]{1,0:T(8,128)}, f32[1024,2]{1,0:T(8,128)S(1)}, u32[]{:S(2)}) copy-start(f32[1024,2]{1,0:T(8,128)S(1)} %fusion.27.mask) | copy-start | bytes 24580
  15.8 3.2 copy-start.41
  15.8 5.8 %copy-start.30 = (bf16[512,1024]{1,0:T(8,128)(2,1)}, bf16[512,1024]{1,0:T(8,128)(2,1)S(1)}, u32[]{:S(2)}) copy-start(bf16[512,1024]{1,0:T(8,128)(2,1)S(1)} %collective-permute-done) | copy-start | bytes 3145732
  19.0 2.6 copy-start.42
  44.9 5.9 %copy-start.1 = (bf16[1024,512]{1,0:T(8,128)(2,1)}, bf16[1024,512]{1,0:T(8,128)(2,1)S(1)}, u32[]{:S(2)}) copy-start(bf16[1024,512]{1,0:T(8,128)(2,1)S(1)} %get-tuple-element.38.mixed_rows) | copy-start | bytes 3145732
  44.9 5.9 %copy-start.8 = (bf16[1024,512]{1,0:T(8,128)(2,1)}, bf16[1024,512]{1,0:T(8,128)(2,1)S(1)}, u32[]{:S(2)}) copy-start(bf16[1024,512]{1,0:T(8,128)(2,1)S(1)} %get-tuple-element.45.query_rows) | copy-start | bytes 3145732
  44.9 5.9 %copy-start.9 = (bf16[1024,512]{1,0:T(8,128)(2,1)}, bf16[1024,512]{1,0:T(8,128)(2,1)S(1)}, u32[]{:S(2)}) copy-start(bf16[1024,512]{1,0:T(8,128)(2,1)S(1)} %get-tuple-element.46.key_rows) | copy-start | bytes 3145732
  44.9 5.9 %copy-start.10 = (bf16[1024,512]{1,0:T(8,128)(2,1)}, bf16[1024,512]{1,0:T(8,128)(2,1)S(1)}, u32[]{:S(2)}) copy-start(bf16[1024,512]{1,0:T(8,128)(2,1)S(1)} %get-tuple-element.47.value_rows) | copy-start | bytes 3145732
  44.9 2.0 copy-start.24
  45.0 5.0 %copy-start.15 = (bf16[512,1024]{1,0:T(8,128)(2,1)S(1)}, bf16[512,1024]{1,0:T(8,128)(2,1)}, u32[]{:S(2)}) copy-start(bf16[512,1024]{1,0:T(8,128)(2,1)} %param.15) | copy-start | bytes 3145732
  45.7 4.2 collective-permute-start.1
  47.0 5.4 %collective-permute-start.3 = (bf16[512,1024]{1,0:T(8,128)(2,1)S(1)}, bf16[512,1024]{1,0:T(8,128)(2,1)S(1)}, u32[]{:S(2)}, u32[]{:S(2)}) collective-permute-start(bf16[512,1024]{1,0:T(8,128)(2,1)S(1)} %copy-done.24), channel_id=1, source_target_pairs={{0,1},{1,0},{2,3},{3,2},{4,5},{5,4},{6,7},{7,6},{8,9},{9,8},{10,11... | collective-permute-start | bytes 3145736 | tf_op jit(solution)/shard_map/ppermute | solution.py:956
  52.2 2.7 copy-start.22
  52.2 2.7 collective-permute-start.2
  56.0 40.6 %copy-start.39 = (bf16[1024,2048]{1,0:T(8,128)(2,1)S(1)}, bf16[1024,2048]{1,0:T(8,128)(2,1)}, u32[]{:S(2)}) copy-start(bf16[1024,2048]{1,0:T(8,128)(2,1)} %gate_w.1) | copy-start | bytes 12582916
  96.4 20.6 %collective-permute-start.5 = (f32[512,1024]{1,0:T(8,128)}, f32[512,1024]{1,0:T(8,128)}, u32[]{:S(2)}, u32[]{:S(2)}) collective-permute-start(f32[512,1024]{1,0:T(8,128)} %get-tuple-element.43), channel_id=1, source_target_pairs={{0,1},{1,0},{2,3},{3,2},{4,5},{5,4},{6,7},{7,6},{8,9},{9,8},{10,11... | collective-permute-start | bytes 6291464 | tf_op jit(solution)/shard_map/ppermute | solution.py:956
  101.9 18.5 %collective-permute-start.4 = (bf16[512,1024]{1,0:T(8,128)(2,1)S(1)}, bf16[512,1024]{1,0:T(8,128)(2,1)}, u32[]{:S(2)}, u32[]{:S(2)}) collective-permute-start(bf16[512,1024]{1,0:T(8,128)(2,1)S(1)} %get-tuple-element.40), channel_id=1, source_target_pairs={{0,1},{1,0},{2,3},{3,2},{4,5},{5,4},{6,7},{7,6},{8,9},{9,8},{10,11... | collective-permute-start | bytes 3145736 | tf_op jit(solution)/shard_map/ppermute | solution.py:956
  102.3 5.4 %copy-start.40 = (bf16[2048,1024]{1,0:T(8,128)(2,1)S(1)}, bf16[2048,1024]{1,0:T(8,128)(2,1)}, u32[]{:S(2)}) copy-start(bf16[2048,1024]{1,0:T(8,128)(2,1)} %down_w.1) | copy-start | bytes 12582916
  102.3 5.4 %copy-start.45 = (bf16[1024,2048]{1,0:T(8,128)(2,1)S(1)}, bf16[1024,2048]{1,0:T(8,128)(2,1)}, u32[]{:S(2)}) copy-start(bf16[1024,2048]{1,0:T(8,128)(2,1)} %get-tuple-element.39) | copy-start | bytes 12582916
  107.7 2.4 copy-start.23
  107.7 2.4 copy-start.33
  107.7 3.0 copy-start.44
  110.7 6.3 %copy-start.26 = (f32[512,1024]{1,0:T(8,128)S(1)}, f32[512,1024]{1,0:T(8,128)}, u32[]{:S(2)}) copy-start(f32[512,1024]{1,0:T(8,128)} %fusion.17) | copy-start | bytes 6291460
  117.0 2.4 copy-start.13
  120.4 3.9 copy-start.31
  124.3 2.8 collective-permute-start.6
  127.1 2.3 copy-start.7
  129.4 37.0 %copy-start.2 = (bf16[1024,512]{1,0:T(8,128)(2,1)S(1)}, bf16[1024,512]{1,0:T(8,128)(2,1)}, u32[]{:S(2)}) copy-start(bf16[1024,512]{1,0:T(8,128)(2,1)} %copy-done.1) | copy-start | bytes 3145732
  165.8 2.9 copy-start.3
  165.8 2.9 copy-start.4
  165.8 2.9 copy-start.5
  165.8 2.9 copy-start.16
  165.8 3.5 copy-start.17
  165.8 2.9 collective-permute-start.7
  398.7 2.9 copy-start.29
  403.2 4.0 copy-start.21
  407.2 4.5 %copy-start.36 = (f32[8,1024]{1,0:T(8,128)S(1)}, f32[8,1024]{1,0:T(8,128)}, u32[]{:S(2)}) copy-start(f32[8,1024]{1,0:T(8,128)} %get-tuple-element.55) | copy-start | bytes 98308
  407.2 5.1 %copy-start.18 = (f32[512,1024]{1,0:T(8,128)S(1)}, f32[512,1024]{1,0:T(8,128)}, u32[]{:S(2)}) copy-start(f32[512,1024]{1,0:T(8,128)} %get-tuple-element.49) | copy-start | bytes 6291460
  407.2 5.1 %copy-start.19 = (f32[512,1024]{1,0:T(8,128)S(1)}, f32[512,1024]{1,0:T(8,128)}, u32[]{:S(2)}) copy-start(f32[512,1024]{1,0:T(8,128)} %get-tuple-element.74) | copy-start | bytes 6291460
  414.5 6.8 %copy-start.20 = (bf16[2048,1024]{1,0:T(8,128)(2,1)S(1)}, bf16[2048,1024]{1,0:T(8,128)(2,1)}, u32[]{:S(2)}) copy-start(bf16[2048,1024]{1,0:T(8,128)(2,1)} %get-tuple-element.72) | copy-start | bytes 12582916
  (7 other events, 8.2 us)
Sparse Core Ops, SparseCore 0:
  102.4 312.0 all-reduce.3
